TPU v7x, 32 devices: a whole 2x2x4 slice. The times are simulated.
32 devices in a mesh: group: 8 (over y, x, core), shard: 4 (over z).
Axes of the slice: x: 2, y: 2, z: 4, core: 2. Of those that a mesh axis runs over, the one named last changes fastest.
Arguments:
- tokens: bfloat16 [2, 8, 2048, 768], P(None, 'group', 'shard'), may hold values from -6 to 6
- cond: float32 [2, 8, 128], P(None, 'group'), may hold values from -6 to 6
- seg_ids: int32 [2, 8, 2048], P(None, 'group'), may hold values from 0 to 12, as said below
- parents: int32 [2, 8, 13], P(None, 'group'), may hold values from 0 to 4, as said below
- cotangent: bfloat16 [2, 8, 2048, 768], P(None, 'group', 'shard'), may hold values from -6 to 6
- w_qkv: bfloat16 [768, 2304], P('shard'), may hold values from -0.21875 to 0.21875
- w_out: bfloat16 [768, 768], P('shard'), may hold values from -1.75 to 1.75
- w_fc1: bfloat16 [768, 3072], P('shard'), may hold values from -0.21875 to 0.21875
- b_fc1: bfloat16 [3072], P('shard'), may hold values from -3 to 3
- w_fc2: bfloat16 [3072, 768], P('shard'), may hold values from -0.109375 to 0.109375
- b_fc2: bfloat16 [768], P('shard'), may hold values from -3 to 3
- w_ada: bfloat16 [128, 4608], P(None, 'shard'), may hold values from -0.5 to 0.5
- b_ada: bfloat16 [4608], P('shard'), may hold values from -3 to 3
- gain1: bfloat16 [768], P('shard'), may hold values from 0.25 to 1.75
- gain2: bfloat16 [768], P('shard'), may hold values from 0.25 to 1.75
Outputs:
- out: bfloat16 [2, 8, 2048, 768], P(None, 'group', 'shard')
- grad_tokens: bfloat16 [2, 8, 2048, 768], P(None, 'group', 'shard')
- grad_cond: float32 [2, 8, 128], P(None, 'group')
- grad_w_qkv: float32 [768, 2304], P('shard')
- grad_w_out: float32 [768, 768], P('shard')
- grad_w_fc1: float32 [768, 3072], P('shard')
- grad_b_fc1: float32 [3072], P('shard')
- grad_w_fc2: float32 [3072, 768], P('shard')
- grad_b_fc2: float32 [768], P('shard')
- grad_w_ada: float32 [128, 4608], P(None, 'shard')
- grad_b_ada: float32 [4608], P('shard')
- grad_gain1: float32 [768], P('shard')
- grad_gain2: float32 [768], P('shard')
Inputs may be any that keep to these rules, and one draw needn't show every extreme that they name: `seg_ids`: along each tree's 2048 tokens the segment ids never fall, and every one of the 13 segments holds at least one token. In each tree segment 0 is the trunk with parents[0] = 0, segments 1 to 4 are branches with parent 0, and segments 5 to 12 are leaves, two on each branch.
All inputs are finite; a program needn't handle non-finite values.
Results may differ from a plain program's by a relative error of at most 0.02.
The roundings to bfloat16 on the way count: a program that leaves them out, or rounds other values in their place, can miss the bound.
Values may be sent and summed in bfloat16 or wider, within the bound.
No kernel may reach another device: no remote copies, remote signals or barrier semaphores. Data moves between devices by JAX's collectives and lax.ppermute only.
A program may use at most 256 MiB of HBM per device.

v0:
```python
import functools
import math

import jax
import jax.numpy as jnp
from jax import lax
from jax.experimental import pallas as pl
from jax.experimental.pallas import tpu as pltpu
from jax.sharding import PartitionSpec as P

HEADS = 12
EPS = 1e-05
GELU_C = 0.7978845608028654
GELU_K = 0.044715
HIGH = lax.Precision.HIGHEST
BF = jnp.bfloat16
F32 = jnp.float32
BLOCK = 256
SPAN = 512
LANES = 128
BIG = -float(2**30)
MASKED = -1000000000.0
PAIRS = 6


def layer_norm(values):
    centred = values - jnp.mean(values, axis=-1, keepdims=True)
    inv_std = lax.rsqrt(jnp.mean(centred * centred, axis=-1, keepdims=True) + EPS)
    return centred * inv_std, inv_std


def norm_back(grad_normed, normed, inv_std):
    first_mean = jnp.mean(grad_normed, axis=-1, keepdims=True)
    second = jnp.mean(grad_normed * normed, axis=-1, keepdims=True)
    return (grad_normed - first_mean - normed * second) * inv_std


def gelu_parts(pre_act):
    inner_arg = GELU_C * (pre_act + GELU_K * pre_act * pre_act * pre_act)
    tangent = jnp.tanh(inner_arg)
    gelu_value = 0.5 * pre_act * (1.0 + tangent)
    gelu_slope = 0.5 * (1.0 + tangent) + 0.5 * pre_act * (1.0 - tangent * tangent) * GELU_C * (
        1.0 + 3.0 * GELU_K * pre_act * pre_act
    )
    return gelu_value, gelu_slope


def mm(left, right):
    return jnp.dot(left, right, preferred_element_type=F32)


def mm_t(left, right):
    return lax.dot_general(left, right, (((1,), (1,)), ((), ())), preferred_element_type=F32)


def t_mm(left, right):
    return lax.dot_general(left, right, (((0,), (0,)), ((), ())), preferred_element_type=F32)


def split_heads(pair):
    first = lax.broadcasted_iota(jnp.int32, pair.shape, 1) < LANES // 2
    zero = jnp.zeros_like(pair)
    return jnp.concatenate([jnp.where(first, pair, zero), jnp.where(first, zero, pair)], axis=0)

def side_by_side(stack):
    n = stack.shape[0] // 2
    return jnp.concatenate([stack[:n], stack[n:]], axis=1)

def as_row(column):
    return jnp.transpose(jnp.broadcast_to(column, (column.shape[0], LANES)))[:1]

def interleave(into, near_ref, far_ref):
    for i in range(near_ref.shape[0] // BLOCK):
        rows = slice(i * BLOCK, (i + 1) * BLOCK)
        into[2 * i * BLOCK : (2 * i + 1) * BLOCK, :] = near_ref[rows, :]
        into[(2 * i + 1) * BLOCK : (2 * i + 2) * BLOCK, :] = far_ref[rows, :]

def lane_groups(x):
    return [x[:, i : i + LANES] for i in range(0, x.shape[1], LANES)]

def is_safe(peak, far_keys, scale):
    top = jnp.maximum(peak, jnp.max(jnp.abs(far_keys.astype(F32))))
    return (peak * top * (scale * (LANES // 2)) < 2.0**27).astype(jnp.int32)

def lanes_sum(x): return jnp.sum(x, axis=1, keepdims=True)

def fwd_kernel(near, pp, scale, flags, peak_ref, q_ref, kn_ref, vn_ref, kf_ref, vf_ref, feat_ref, hot_ref, o_ref, lse_ref,
               s_ref, m_ref, l_ref, acc_ref, k_all, v_all, safe_ref):
    qb = pl.program_id(1)
    nk = hot_ref.shape[0] // SPAN
    @pl.when(qb == 0)
    def _():
        interleave(k_all, kn_ref, kf_ref)
        interleave(v_all, vn_ref, vf_ref)
        safe_ref[0] = is_safe(peak_ref[0], kf_ref[...], scale)
    safe = safe_ref[0] == 1
    feat = feat_ref[...]
    feat2 = jnp.concatenate([feat, feat], axis=0)
    qs = [split_heads(q_ref[:, p*LANES:(p+1)*LANES] * scale) for p in range(pp)]
    m_ref[...] = jnp.full(m_ref.shape, -jnp.inf, F32)
    def scan_scores(exact):
        def step(j, _):
            @pl.when((flags[qb * nk + j] == 1) | jnp.logical_not(safe))
            def _():
                rows = pl.ds(pl.multiple_of(j * SPAN, SPAN), SPAN)
                hot = hot_ref[rows, :]
                for p in range(pp):
                    k = k_all[rows, p*LANES:(p+1)*LANES]
                    if exact:
                        ok = mm_t(feat2, hot) > -1.0
                        s = jnp.where(ok, mm_t(qs[p], k), MASKED)
                    else:
                        s = mm_t(jnp.concatenate([qs[p], feat2], axis=1), jnp.concatenate([k, hot], axis=1))
                    s_ref[p, j] = s
                    m_ref[p] = functools.reduce(jnp.maximum, lane_groups(s), m_ref[p])
            return 0
        lax.fori_loop(0, nk, step, 0)
    @pl.when(safe)
    def _(): scan_scores(False)
    @pl.when(jnp.logical_not(safe))
    def _(): scan_scores(True)
    tops = [jnp.max(m_ref[p], axis=1, keepdims=True) for p in range(pp)]
    l_ref[...] = jnp.zeros(l_ref.shape, F32)
    acc_ref[...] = jnp.zeros(acc_ref.shape, F32)
    def step(j, _):
        @pl.when((flags[qb * nk + j] == 1) | jnp.logical_not(safe))
        def _():
            rows = pl.ds(pl.multiple_of(j * SPAN, SPAN), SPAN)
            for p in range(pp):
                e = jnp.exp(s_ref[p, j] - tops[p])
                l_ref[p] += sum(lane_groups(e))
                v = split_heads(v_all[rows, p*LANES:(p+1)*LANES])
                acc_ref[p] += mm(side_by_side(e.astype(BF)), v)
        return 0
    lax.fori_loop(0, nk, step, 0)
    for p in range(pp):
        total = lanes_sum(l_ref[p])
        lse_ref[p, 0] = as_row(tops[p] + jnp.log(total))
        first = lax.broadcasted_iota(jnp.int32, (BLOCK, LANES), 1) < LANES // 2
        o_ref[:, p*LANES:(p+1)*LANES] = (acc_ref[p] / jnp.where(first, total[:BLOCK], total[BLOCK:])).astype(BF)

def attn_fwd(q, kv, far, feat, hot, flags, peak, scale, pp):
    near, width = q.shape
    total = hot.shape[0]
    steps = width // LANES // pp
    nq = near // BLOCK
    col = lambda c: (lambda h, i, f: (0, c * steps + h))
    return pl.pallas_call(
        functools.partial(fwd_kernel, near, pp, scale),
        grid_spec=pltpu.PrefetchScalarGridSpec(
            num_scalar_prefetch=1, grid=(steps, nq),
            in_specs=[
                pl.BlockSpec(memory_space=pltpu.SMEM),
                pl.BlockSpec((BLOCK, pp*LANES), lambda h, i, f: (i, h)),
                pl.BlockSpec((near, pp*LANES), col(0)),
                pl.BlockSpec((near, pp*LANES), col(1)),
                pl.BlockSpec((near, pp*LANES), col(0)),
                pl.BlockSpec((near, pp*LANES), col(1)),
                pl.BlockSpec((BLOCK, LANES), lambda h, i, f: (i, 0)),
                pl.BlockSpec((total, LANES), lambda h, i, f: (0, 0)),
            ],
            out_specs=[
                pl.BlockSpec((BLOCK, pp*LANES), lambda h, i, f: (i, h)),
                pl.BlockSpec((pp, 1, 1, 2*BLOCK), lambda h, i, f: (h, i, 0, 0)),
            ],
            scratch_shapes=[
                pltpu.VMEM((pp, total // SPAN, 2*BLOCK, SPAN), F32),
                pltpu.VMEM((pp, 2*BLOCK, LANES), F32),
                pltpu.VMEM((pp, 2*BLOCK, LANES), F32),
                pltpu.VMEM((pp, BLOCK, LANES), F32),
                pltpu.VMEM((total, pp*LANES), BF),
                pltpu.VMEM((total, pp*LANES), BF),
                pltpu.SMEM((1,), jnp.int32),
            ]),
        out_shape=[jax.ShapeDtypeStruct((near, width), BF), jax.ShapeDtypeStruct((width // LANES, nq, 1, 2*BLOCK), F32)],
        compiler_params=pltpu.CompilerParams(vmem_limit_bytes=56<<20),
        cost_estimate=cost(38),
        name="attn_forward",
    )(flags, peak, q, kv, kv, far, far, feat, hot)

def bwd_kernel(near, pp, scale, flags, peak_ref, q_ref, kn_ref, vn_ref, kf_ref, vf_ref, feat_ref, hot_ref, o_ref, do_ref, lse_ref,
               dq_ref, near_ref, far_ref, k_all, v_all, k_turned, dk_acc, dv_acc, dq_acc, safe_ref):
    half = LANES // 2
    qb = pl.program_id(1)
    nk = hot_ref.shape[0] // SPAN
    @pl.when(qb == 0)
    def _():
        interleave(k_all, kn_ref, kf_ref)
        interleave(v_all, vn_ref, vf_ref)
        safe_ref[0] = is_safe(peak_ref[0], kf_ref[...], scale)
        k_turned[...] = jnp.transpose(k_all[...])
        dk_acc[...] = jnp.zeros(dk_acc.shape, F32)
        dv_acc[...] = jnp.zeros(dv_acc.shape, F32)
    safe = safe_ref[0] == 1
    feat = feat_ref[...]
    feat2 = jnp.concatenate([feat, feat], axis=0)
    dq_acc[...] = jnp.zeros(dq_acc.shape, F32)
    qs, dos, deltas, lses = [], [], [], []
    for p in range(pp):
        cols = slice(p*LANES, (p+1)*LANES)
        qs.append(split_heads(q_ref[:, cols] * scale))
        do2 = split_heads(do_ref[:, cols])
        dos.append(do2)
        o = o_ref[:, cols].astype(F32)
        deltas.append(as_row(lanes_sum(do2.astype(F32) * jnp.concatenate([o, o], axis=0))))
        lses.append(lse_ref[p, 0])
    def sweep(exact):
        def step(j, _):
            @pl.when((flags[qb * nk + j] == 1) | jnp.logical_not(safe))
            def _():
                rows = pl.ds(pl.multiple_of(j * SPAN, SPAN), SPAN)
                hot = hot_ref[rows, :]
                for p in range(pp):
                    cols = slice(p*LANES, (p+1)*LANES)
                    k = k_all[rows, cols]; v = v_all[rows, cols]
                    if exact:
                        ok = mm_t(hot, feat2) > -1.0
                        s = jnp.where(ok, mm_t(k, qs[p]), MASKED)
                    else:
                        s = mm_t(jnp.concatenate([k, hot], axis=1), jnp.concatenate([qs[p], feat2], axis=1))
                    prob = jnp.exp(s - lses[p])
                    dprob = mm_t(v, dos[p])
                    ds = prob * (dprob - deltas[p])
                    if exact:
                        ds = jnp.where(ok, ds, 0.0)
                    ds = ds.astype(BF)
                    dv_acc[rows, cols] += mm(prob.astype(BF), dos[p])
                    dk_acc[rows, cols] += mm(ds, qs[p])
                    for h in range(2):
                        kt = k_turned[p*LANES + h*half : p*LANES + (h+1)*half, rows]
                        dq_acc[p, h*half:(h+1)*half] += mm(kt, ds[:, h*BLOCK:(h+1)*BLOCK])
            return 0
        lax.fori_loop(0, nk, step, 0)
    @pl.when(safe)
    def _(): sweep(False)
    @pl.when(jnp.logical_not(safe))
    def _(): sweep(True)
    for p in range(pp):
        dq_ref[:, p*LANES:(p+1)*LANES] = jnp.transpose(dq_acc[p] * scale).astype(BF)
    @pl.when(qb == pl.num_programs(1) - 1)
    def _():
        for i in range(near // BLOCK):
            rows = slice(i * BLOCK, (i + 1) * BLOCK)
            for side, acc in enumerate((dk_acc, dv_acc)):
                near_ref[side, rows] = acc[2 * i * BLOCK : (2 * i + 1) * BLOCK]
                far_ref[side, rows] = acc[(2 * i + 1) * BLOCK : (2 * i + 2) * BLOCK].astype(BF)

def attn_bwd(q, kv, far, feat, hot, flags, peak, attn, dattn, lse, scale, pp):
    near, width = q.shape
    total = hot.shape[0]
    steps = width // LANES // pp
    nq = near // BLOCK
    col = lambda c: (lambda h, i, f: (0, c * steps + h))
    rowblk = pl.BlockSpec((BLOCK, pp*LANES), lambda h, i, f: (i, h))
    whole = pl.BlockSpec((near, pp*LANES), col(0))
    both = pl.BlockSpec((2, near, pp*LANES), lambda h, i, f: (0, 0, h))
    return pl.pallas_call(
        functools.partial(bwd_kernel, near, pp, scale),
        grid_spec=pltpu.PrefetchScalarGridSpec(
            num_scalar_prefetch=1, grid=(steps, nq),
            in_specs=[
                pl.BlockSpec(memory_space=pltpu.SMEM),
                rowblk,
                pl.BlockSpec((near, pp*LANES), col(0)),
                pl.BlockSpec((near, pp*LANES), col(1)),
                whole,
                pl.BlockSpec((near, pp*LANES), col(1)),
                pl.BlockSpec((BLOCK, LANES), lambda h, i, f: (i, 0)),
                pl.BlockSpec((total, LANES), lambda h, i, f: (0, 0)),
                rowblk, rowblk,
                pl.BlockSpec((pp, 1, 1, 2*BLOCK), lambda h, i, f: (h, i, 0, 0)),
            ],
            out_specs=[rowblk, both, both],
            scratch_shapes=[
                pltpu.VMEM((total, pp*LANES), BF),
                pltpu.VMEM((total, pp*LANES), BF),
                pltpu.VMEM((pp*LANES, total), BF),
                pltpu.VMEM((total, pp*LANES), F32),
                pltpu.VMEM((total, pp*LANES), F32),
                pltpu.VMEM((pp, LANES, BLOCK), F32),
                pltpu.SMEM((1,), jnp.int32),
            ]),
        out_shape=[
            jax.ShapeDtypeStruct((near, width), BF),
            jax.ShapeDtypeStruct((2, near, width), F32),
            jax.ShapeDtypeStruct((2, near, width), BF),
        ],
        compiler_params=pltpu.CompilerParams(vmem_limit_bytes=56<<20),
        cost_estimate=cost(63),
        name="attn_backward",
    )(flags, peak, q, kv, kv, far, far, feat, hot, attn, dattn, lse)


def assemble_kernel(shards, where, own_ref, half_ref, other_ref, out_ref):
    s, c, plane = where[0], where[1], where[2]
    groups, planes = own_ref.shape[0], half_ref.shape[0]
    out_ref[pl.ds(s * groups, groups)] = own_ref[...]
    for side, source in ((c, half_ref), (1 - c, other_ref)):
        for j in range(planes):
            for k in range(1, shards):
                place = lax.rem(s + shards - k, shards)
                out_ref[place * groups + side * planes + (plane ^ j)] = source[j, k - 1]


def assemble(where, own, half, other, shards):
    rows, width = own.shape
    fine = half.shape[2]
    groups = rows // fine
    full = lambda *shape: pl.BlockSpec(shape, lambda i, w: (0,) * len(shape))
    out = pl.pallas_call(
        functools.partial(assemble_kernel, shards),
        grid_spec=pltpu.PrefetchScalarGridSpec(
            num_scalar_prefetch=1,
            grid=(1,),
            in_specs=[full(groups, fine, width), full(*half.shape), full(*half.shape)],
            out_specs=full(groups * shards, fine, width),
        ),
        out_shape=jax.ShapeDtypeStruct((groups * shards, fine, width), own.dtype),
        compiler_params=pltpu.CompilerParams(vmem_limit_bytes=60 << 20),
        name="assemble",
    )(where, own.reshape(groups, fine, width), half, other)
    return out.reshape(shards * rows, width)


def entry_kernel(tok_ref, vec_ref, w_ref, act_ref, q_ref, kv_ref, peak_ref):
    step = pl.program_id(0)
    rows, pieces = BLOCK, tok_ref.shape[0] // BLOCK

    @pl.when(step == 0)
    def _():
        gain, lift, shift = (vec_ref[i : i + 1, :] for i in range(3))
        for i in range(pieces):
            at = slice(i * rows, (i + 1) * rows)
            normed, _unused = layer_norm(tok_ref[at, :].astype(F32))
            act_ref[at, :] = (normed * gain * lift + shift).astype(BF)
        peak_ref[...] = jnp.zeros_like(peak_ref)

    top = jnp.zeros((1, w_ref.shape[1]), F32)
    for i in range(pieces):
        at = slice(i * rows, (i + 1) * rows)
        value = mm(act_ref[at, :], w_ref[...])
        low = value.astype(BF)
        top = jnp.maximum(top, jnp.max(jnp.abs(low.astype(F32)), axis=0, keepdims=True))

        @pl.when(step < 2)
        def _():
            kv_ref[at, :] = low

        @pl.when(step == 2)
        def _():
            q_ref[at, :] = low

    peak_ref[0:1, :] = jnp.maximum(peak_ref[0:1, :], top)


def entry(tok, vec, qkv_w):
    total, width = tok.shape
    fixed = lambda *shape: pl.BlockSpec(shape, lambda j: (0,) * len(shape))
    return pl.pallas_call(
        entry_kernel,
        grid=(3,),
        in_specs=[
            fixed(total, width), fixed(8, width),
            pl.BlockSpec((width, width), lambda j: (0, lax.rem(j + 1, 3))),
        ],
        out_specs=[
            fixed(total, width), fixed(total, width),
            pl.BlockSpec((total, width), lambda j: (0, jnp.minimum(j, 1))),
            fixed(8, width),
        ],
        out_shape=[
            jax.ShapeDtypeStruct((total, width), BF),
            jax.ShapeDtypeStruct((total, width), BF),
            jax.ShapeDtypeStruct((total, 2 * width), BF),
            jax.ShapeDtypeStruct((8, width), F32),
        ],
        compiler_params=pltpu.CompilerParams(vmem_limit_bytes=48 << 20),
        cost_estimate=cost(9),
        name="entry",
    )(tok, vec, qkv_w)


def leave_kernel(spots, where, dq_ref, near_ref, far_ref, act_ref, w_ref, tok_ref, dmid_ref, vec_ref,
                 grad_ref, mine_ref, yours_ref, sums_ref, d_all, da):
    step = pl.program_id(0)
    total = dq_ref.shape[0]
    sides, planes, places, fine = spots

    @pl.when(step == 0)
    def _():
        d_all[...] = dq_ref[...]
        da[...] = jnp.zeros_like(da)

    @pl.when(step > 0)
    def _():
        d_all[...] = (near_ref[0] + far_ref[0].astype(F32)).astype(BF)

    grad = t_mm(act_ref[...], d_all[...])

    def put(ref, side):
        for place in range(places):
            turned = lax.rem(place + places - where[0], places)
            for plane in range(planes):
                start = ((place * sides + side) * planes + plane) * fine
                ref[plane ^ where[2], turned] = grad[start : start + fine].astype(BF)

    for side in range(sides):
        pl.when(where[1] == side)(functools.partial(put, mine_ref, side))
        pl.when(where[1] != side)(functools.partial(put, yours_ref, side))

    def add(r, _):
        rows = pl.ds(pl.multiple_of(r * BLOCK, BLOCK), BLOCK)
        da[rows, :] += mm_t(d_all[rows, :], w_ref[...])
        return 0

    lax.fori_loop(0, total // BLOCK, add, 0)

    @pl.when(step == 2)
    def _():
        gain, lift, shift = (vec_ref[i : i + 1, :] for i in range(3))
        sums_ref[...] = jnp.zeros_like(sums_ref)

        def finish(r, _):
            rows = pl.ds(pl.multiple_of(r * BLOCK, BLOCK), BLOCK)
            normed, inv = layer_norm(tok_ref[rows, :].astype(F32))
            part = da[rows, :]
            grad_h = part * lift
            back = norm_back(grad_h * gain, normed, inv)
            grad_ref[rows, :] = (dmid_ref[rows, :] + back).astype(BF)
            for i, term in enumerate((part, part * (normed * gain), grad_h * normed)):
                sums_ref[i : i + 1, :] += jnp.sum(term, axis=0, keepdims=True)
            return 0

        lax.fori_loop(0, total // BLOCK, finish, 0)


def leave(where, q_grads, near, far, act, qkv_w, tok, dmid, vec, spots):
    total, width = q_grads.shape
    keep = pl.Buffered(1)
    whole = pl.BlockSpec((total, width), lambda j, w: (0, 0), pipeline_mode=keep)
    both = pl.BlockSpec((1, total, width), lambda j, w: (jnp.maximum(j - 1, 0), 0, 0))
    small = pl.BlockSpec((8, width), lambda j, w: (0, 0))
    part = pl.BlockSpec(tuple(spots[1:]) + (width,), lambda j, w: (0, 0, 0, j))
    return pl.pallas_call(
        functools.partial(leave_kernel, spots),
        grid_spec=pltpu.PrefetchScalarGridSpec(
            num_scalar_prefetch=1,
            grid=(3,),
            in_specs=[
                whole, both, both, whole,
                pl.BlockSpec((width, width), lambda j, w: (0, j)),
                whole, whole, small,
            ],
            out_specs=[
                whole,
                part, part,
                small,
            ],
            scratch_shapes=[pltpu.VMEM((total, width), BF), pltpu.VMEM((total, width), F32)],
        ),
        out_shape=[
            jax.ShapeDtypeStruct((total, width), BF),
            jax.ShapeDtypeStruct(tuple(spots[1:]) + (3 * width,), BF),
            jax.ShapeDtypeStruct(tuple(spots[1:]) + (3 * width,), BF),
            jax.ShapeDtypeStruct((8, width), F32),
        ],
        compiler_params=pltpu.CompilerParams(vmem_limit_bytes=56 << 20),
        cost_estimate=cost(14),
        name="leave",
    )(where, q_grads, near, far, act, qkv_w, tok, dmid, vec)


def settle_kernel(where, half_ref, other_ref, out_ref):
    c, plane = where[1], where[2]
    for side, source in ((c, half_ref), (1 - c, other_ref)):
        for j in range(half_ref.shape[0]):
            out_ref[side * half_ref.shape[0] + (plane ^ j)] = source[j].astype(F32)


def settle(where, half, other):
    planes, fine, width = half.shape
    full = lambda *shape: pl.BlockSpec(shape, lambda i, w: (0,) * len(shape))
    return pl.pallas_call(
        settle_kernel,
        grid_spec=pltpu.PrefetchScalarGridSpec(
            num_scalar_prefetch=1,
            grid=(1,),
            in_specs=[full(planes, fine, width)] * 2,
            out_specs=full(2 * planes, fine, width),
        ),
        out_shape=jax.ShapeDtypeStruct((2 * planes, fine, width), F32),
        compiler_params=pltpu.CompilerParams(vmem_limit_bytes=40 << 20),
        name="settle",
    )(where, half, other)


def unpack_kernel(count, where, half_ref, other_ref, out_ref, fc1_ref, fc2_ref):
    step = pl.program_id(0)
    c, plane = where[1], where[2]

    def fill(ref):
        for side, source in ((c, half_ref), (1 - c, other_ref)):
            for j in range(source.shape[0]):
                ref[2 * (plane ^ j) + side] = source[j].astype(F32).reshape(ref.shape[1:])

    @pl.when(step == 0)
    def _():
        fill(out_ref)

    @pl.when((step > 0) & (step <= count))
    def _():
        fill(fc1_ref)

    @pl.when(step > count)
    def _():
        fill(fc2_ref)


def unpack(where, half, other, width):
    planes, fine, total = half.shape
    groups, count = 2 * planes, total // width // 2
    block = pl.BlockSpec((planes, fine, width), lambda i, w: (0, 0, i))
    low = lambda i: jnp.clip(i, 0, count - 1)
    out, fc1, fc2 = pl.pallas_call(
        functools.partial(unpack_kernel, count),
        grid_spec=pltpu.PrefetchScalarGridSpec(
            num_scalar_prefetch=1,
            grid=(1 + 2 * count,),
            in_specs=[block, block],
            out_specs=[
                pl.BlockSpec((groups, fine, width), lambda i, w: (0, 0, 0)),
                pl.BlockSpec((groups, fine, width), lambda i, w: (0, 0, low(i - 1))),
                pl.BlockSpec((groups, 1, fine, width), lambda i, w: (0, low(i - 1 - count), 0, 0)),
            ],
        ),
        out_shape=[
            jax.ShapeDtypeStruct((groups, fine, width), F32),
            jax.ShapeDtypeStruct((groups, fine, count * width), F32),
            jax.ShapeDtypeStruct((groups, count, fine, width), F32),
        ],
        compiler_params=pltpu.CompilerParams(vmem_limit_bytes=40 << 20),
        cost_estimate=cost(4),
        name="unpack",
    )(where, half, other)
    return out.reshape(-1, width), fc1.reshape(-1, count * width), fc2.reshape(-1, width)


def cost(microseconds):
    return pl.CostEstimate(
        flops=int(microseconds * 1.15e9), bytes_accessed=1 << 20, transcendentals=0
    )


def middle_kernel(chunks, where, attn_ref, tok_ref, cot_ref, vec_ref, b1_ref, wo_ref, w1_ref, *rest):
    w2_refs, rest = rest[:chunks], rest[chunks:]
    (out_ref, dattn_ref, dmid_ref, grads_ref, sums_ref, gb1_ref) = rest[:6]
    (mid, branch, act, dy, two, da, hid, dpre, w2, wide, tall, sems) = rest[6:]
    width = attn_ref.shape[1]

    def send_wide(column):
        cols = pl.ds(pl.multiple_of(column * width, LANES), width)
        return pltpu.make_async_copy(wide, grads_ref.at[:, :, :, cols], sems.at[0])

    def turned(place):
        return lax.rem(place + chunks - where[0], chunks)

    def send_tall(place):
        cols = pl.ds((1 + chunks) * width, chunks * width)
        return pltpu.make_async_copy(tall, grads_ref.at[:, turned(place), :, cols], sems.at[1])

    step = pl.program_id(0)
    total = attn_ref.shape[0]
    blocks = total // BLOCK
    gate_one, gain, lift, shift, gate_two, fc2_b = (vec_ref[i : i + 1, :] for i in range(6))

    def rows_of(r):
        return pl.ds(pl.multiple_of(r * BLOCK, BLOCK), BLOCK)

    @pl.when(step == 0)
    def _():
        sums_ref[...] = jnp.zeros_like(sums_ref)

        def start(r, _):
            rows = rows_of(r)
            one = mm(attn_ref[rows, :], wo_ref[...])
            middle = tok_ref[rows, :].astype(F32) + gate_one * one
            normed, _unused = layer_norm(middle)
            branch[rows, :] = one
            mid[rows, :] = middle
            act[rows, :] = (normed * gain * lift + shift).astype(BF)
            dy[rows, :] = (cot_ref[rows, :].astype(F32) * gate_two).astype(BF)
            two[rows, :] = jnp.zeros((BLOCK, two.shape[1]), F32)
            da[rows, :] = jnp.zeros((BLOCK, da.shape[1]), F32)
            return 0

        lax.fori_loop(0, blocks, start, 0)

    @pl.when(step < chunks)
    def _():
        height = w2_refs[0].shape[0]
        for b in range(chunks):
            w2[b * height : (b + 1) * height, :] = w2_refs[b][...]
        gb1_ref[...] = jnp.zeros_like(gb1_ref)

        def chunk(r, _):
            rows = rows_of(r)
            value, slope = gelu_parts(mm(act[rows, :], w1_ref[...]) + b1_ref[...])
            hidden = value.astype(BF)
            hid[rows, :] = hidden
            two[rows, :] += mm(hidden, w2[...])
            grad = (mm_t(dy[rows, :], w2[...]) * slope).astype(BF)
            dpre[rows, :] = grad
            gb1_ref[...] += jnp.sum(grad.astype(F32), axis=0, keepdims=True)
            da[rows, :] += mm_t(grad, w1_ref[...])
            return 0

        lax.fori_loop(0, blocks, chunk, 0)
        grad_two = t_mm(hid[...], dy[...])
        grad_one = t_mm(act[...], dpre[...])

        @pl.when(step > 0)
        def _():
            send_wide(step).wait()
            send_tall(step - 1).wait()

        groups, fine = tall.shape[:2]
        for g in range(groups):
            for b in range(chunks):
                start = (g * chunks + b) * fine
                tall[g, :, b * width : (b + 1) * width] = grad_two[start : start + fine].astype(BF)
        put_blocks(wide, grad_one, turned)
        send_wide(step + 1).start()
        send_tall(step).start()

    @pl.when(step == chunks)
    def _():
        def finish(r, _):
            rows = rows_of(r)
            cot = cot_ref[rows, :].astype(F32)
            middle = mid[rows, :]
            second = two[rows, :] + fc2_b
            out_ref[rows, :] = (middle + gate_two * second).astype(BF)
            normed, inv = layer_norm(middle)
            lifted = normed * gain
            grad = da[rows, :]
            grad_h = grad * lift
            dmid = cot + norm_back(grad_h * gain, normed, inv)
            dmid_ref[rows, :] = dmid
            dy_one = (dmid * gate_one).astype(BF)
            dpre[rows, :] = dy_one
            dattn_ref[rows, :] = mm_t(dy_one, wo_ref[...]).astype(BF)
            parts = (
                dmid * branch[rows, :], grad, grad * lifted, cot * second,
                grad_h * normed, dy[rows, :].astype(F32),
            )
            for i, part in enumerate(parts):
                sums_ref[i : i + 1, :] += jnp.sum(part, axis=0, keepdims=True)
            return 0

        lax.fori_loop(0, blocks, finish, 0)
        grad_out = t_mm(attn_ref[...], dpre[...])
        send_wide(step).wait()
        send_tall(step - 1).wait()
        put_blocks(wide, grad_out, turned)
        send_wide(0).start()
        send_wide(0).wait()


def put_blocks(ref, grad, turned):
    groups, places, rows = ref.shape[:3]
    for s in range(places):
        for g in range(groups):
            start = (s * groups + g) * rows
            ref[g, turned(s)] = grad[start : start + rows].astype(BF)


def middle(where, attn, tok, cot, vec, fc1_b, pack, groups):
    total, width = attn.shape
    shards = pack.shape[1] // width - 5
    fine = width // shards // groups
    keep = pl.Buffered(1)
    whole = pl.BlockSpec((total, width), lambda i, w: (0, 0), pipeline_mode=keep)
    last = shards - 1
    low = lambda i: jnp.minimum(i, last)
    w2_spec = lambda b: pl.BlockSpec((width // shards, width), lambda i, w: (low(i), 5 + b))
    return pl.pallas_call(
        functools.partial(middle_kernel, shards),
        grid_spec=pltpu.PrefetchScalarGridSpec(
            num_scalar_prefetch=1,
            grid=(shards + 1,),
            in_specs=[
            whole, whole, whole,
            pl.BlockSpec((8, width), lambda i, w: (0, 0)),
            pl.BlockSpec((1, width), lambda i, w: (0, low(i))),
            pl.BlockSpec((width, width), lambda i, w: (0, 0), pipeline_mode=keep),
            pl.BlockSpec((width, width), lambda i, w: (0, 1 + low(i))),
        ] + [w2_spec(b) for b in range(shards)],
        out_specs=[
            whole, whole, whole,
            pl.BlockSpec(memory_space=pl.ANY),
            pl.BlockSpec((8, width), lambda i, w: (0, 0)),
            pl.BlockSpec((1, width), lambda i, w: (0, low(i))),
        ],
        scratch_shapes=[
            pltpu.VMEM((total, width), F32),
            pltpu.VMEM((total, width), F32),
            pltpu.VMEM((total, width), BF),
            pltpu.VMEM((total, width), BF),
            pltpu.VMEM((total, width), F32),
            pltpu.VMEM((total, width), F32),
            pltpu.VMEM((total, width), BF),
            pltpu.VMEM((total, width), BF),
            pltpu.VMEM((width, width), BF),
            pltpu.VMEM((groups, shards, fine, width), BF),
            pltpu.VMEM((groups, fine, shards * width), BF),
            pltpu.SemaphoreType.DMA((2,)),
        ],
        ),
        out_shape=[
            jax.ShapeDtypeStruct((total, width), BF),
            jax.ShapeDtypeStruct((total, width), BF),
            jax.ShapeDtypeStruct((total, width), F32),
            jax.ShapeDtypeStruct((groups, shards, fine, 9 * width), BF),
            jax.ShapeDtypeStruct((8, width), F32),
            jax.ShapeDtypeStruct((1, 4 * width), F32),
        ],
        compiler_params=pltpu.CompilerParams(vmem_limit_bytes=60 << 20),
        cost_estimate=cost(55),
        name="middle",
    )(where, attn, tok, cot, vec, fc1_b, pack, pack, *([pack] * shards))


class Links:
    def __init__(self, groups, shards):
        self.groups, self.shards, self.planes = groups, shards, groups // 2
        self.g = lax.axis_index("group")
        self.s = lax.axis_index("shard")
        self.c = self.g % 2
        self.plane = self.g // 2
        tilt = self.plane if self.planes == 4 else 0 * self.plane
        self.where = jnp.stack([self.s, self.c, tilt]).astype(jnp.int32)

    def swap(self, value):
        return lax.ppermute(value, "group", [(i, i ^ 1) for i in range(self.groups)])

    def turn(self, value, step):
        n = self.shards
        return lax.ppermute(value, "shard", [(i, (i + step) % n) for i in range(n)])

    def across(self, value, step):
        return lax.ppermute(value, "group", [(i, i ^ (2 * step)) for i in range(self.groups)])

    def give(self, value):
        batches, rows, width = value.shape
        halves = value.reshape(batches, 2, rows // 2, width)
        keep = lax.dynamic_index_in_dim(halves, self.c, 1, False)
        return keep, lax.dynamic_index_in_dim(halves, 1 - self.c, 1, False)

    def to_trees(self, keep, got):
        return self.exchange(self.by_core(keep, got).reshape(-1, *keep.shape[1:]))

    def exchange(self, by_tree):
        return lax.all_to_all(by_tree, "shard", 0, 0).reshape(-1, by_tree.shape[-1])

    def by_core(self, mine, other):
        return jnp.where(
            self.c == 0, jnp.stack([mine, other], axis=1), jnp.stack([other, mine], axis=1)
        )

    def from_trees(self, value):
        return lax.all_to_all(
            value.reshape(self.shards, -1, value.shape[1]), "shard", 0, 0
        )

    def back(self, value, batches):
        by_core = value.reshape(batches, 2, *value.shape[1:])
        keep = lax.dynamic_index_in_dim(by_core, self.c, 1, False)
        return keep, lax.dynamic_index_in_dim(by_core, 1 - self.c, 1, False)

    def lay_out(self, keep, got):
        return self.by_core(keep, got).reshape(keep.shape[0], 1, -1, keep.shape[-1])

    def plane_order(self, parts):
        stacked = jnp.stack(parts)
        if self.planes != 4:
            return stacked
        return jnp.stack(
            [lax.dynamic_index_in_dim(stacked, self.plane ^ j, 0, False) for j in range(4)]
        )

    def line_order(self, parts):
        stacked = jnp.stack(parts)
        return jnp.stack(
            [
                lax.dynamic_index_in_dim(stacked, (self.s - j) % self.shards, 0, False)
                for j in range(self.shards)
            ]
        )

    def gather_all(self, part):
        return lax.all_gather(part, ("shard", "group"), axis=0, tiled=True)

    def my_rows(self, weight):
        rows = weight.shape[-2] // self.groups
        return lax.dynamic_slice_in_dim(weight, self.g * rows, rows, weight.ndim - 2)

    def group_sum(self, blocks):
        out = lax.psum_scatter(blocks, "group", scatter_dimension=0, tiled=True)
        return out

    def plane_sum(self, value):
        if self.planes != 4:
            groups = [[2 * p + c for p in range(self.planes)] for c in range(2)]
            return lax.psum_scatter(
                value, "group", scatter_dimension=1, axis_index_groups=groups
            ).astype(F32)
        total = lax.dynamic_index_in_dim(value, self.plane, 1, False).astype(F32)
        for k in range(1, 4):
            piece = lax.dynamic_index_in_dim(value, self.plane ^ k, 1, False)
            total = total + self.across(piece, k).astype(F32)
        return total

    def plane_gather(self, value):
        if self.planes != 4:
            groups = [[2 * p + c for p in range(self.planes)] for c in range(2)]
            return lax.all_gather(value, "group", axis_index_groups=groups)
        parts = jnp.stack([value] + [self.across(value, k) for k in range(1, 4)])
        return jnp.stack(
            [lax.dynamic_index_in_dim(parts, self.plane ^ j, 0, False) for j in range(4)]
        )

    def turns(self, values):
        return [self.turn(values[k], k) for k in range(1, self.shards)]

    def spread(self, value):
        if self.planes != 4:
            every = self.plane_gather(value)
            return [every[j] for j in range(self.planes)]
        return [value] + [self.across(value, k) for k in range(1, 4)]


def total(terms):
    result = terms[0].astype(F32)
    for term in terms[1:]:
        result = result + term.astype(F32)
    return result


def on_device(
    tokens,
    cond,
    seg_ids,
    parents,
    cotangent,
    w_qkv,
    w_out,
    w_fc1,
    b_fc1,
    w_fc2,
    b_fc2,
    w_ada,
    b_ada,
    gain1,
    gain2,
    groups,
):
    batches, _, row_count, width = tokens.shape
    shards = lax.axis_size("shard")
    assert shards == 2 * batches and groups % 2 == 0
    head_dim = width // HEADS
    scale = 1.0 / math.sqrt(head_dim)
    net = Links(groups, shards)
    rows = row_count // 2
    mine = shards * rows
    tree_len = seg_ids.shape[2]
    labels = parents.shape[2]
    cond_dim = cond.shape[2]

    fc2_blocks = net.my_rows(w_fc2.reshape(shards, -1, width))
    share = jnp.concatenate(
        [net.my_rows(w_out), net.my_rows(w_fc1)] + [fc2_blocks[b] for b in range(shards)],
        axis=1,
    )

    packed = jnp.concatenate(
        [seg_ids[:, 0].astype(F32), parents[:, 0].astype(F32), cond[:, 0]], axis=1
    )
    part_rows = w_qkv.shape[0] // groups
    early_w = jnp.concatenate([w_qkv, w_ada.reshape(-1, width)], axis=1)
    own_part = lax.dynamic_index_in_dim(
        early_w.reshape(groups, part_rows, -1), net.c * (groups // 2) + net.plane, 0, False
    )
    tok_keep, tok_give = net.give(tokens[:, 0])
    other = net.swap(packed)
    line_w = net.turns([own_part] * shards)
    tok_got = net.swap(tok_give)
    other, line_w, tok_got = lax.optimization_barrier((other, line_w, tok_got))
    tok = net.to_trees(tok_keep, tok_got)
    plane_w = net.spread(jnp.stack(line_w))
    cot_keep, cot_give = net.give(cotangent[:, 0])
    trees = jnp.where(
        net.c == 0, jnp.stack([packed, other], axis=1), jnp.stack([other, packed], axis=1)
    ).reshape(shards, packed.shape[1])
    conds = trees[:, tree_len + labels :]
    my_tree = lax.dynamic_index_in_dim(trees, net.s, 0, False)
    tree_seg = my_tree[:tree_len]
    parent_row = my_tree[tree_len : tree_len + labels]
    ada_rows = jnp.dot(conds, w_ada.astype(F32), precision=HIGH) + b_ada.astype(F32)
    small = jnp.concatenate([b_fc1, b_fc2, gain1, gain2]).astype(F32)
    pieces = jnp.concatenate(
        [ada_rows, jnp.broadcast_to(small[None], (shards, small.shape[0]))], axis=1
    )
    plane_w, tok, pieces, share, cot_give = lax.optimization_barrier(
        (plane_w, tok, pieces, share, cot_give)
    )
    cot_got = net.swap(cot_give)
    got = [lax.dynamic_index_in_dim(pieces, net.s, 0, False)]
    for k in range(1, shards):
        piece = lax.dynamic_index_in_dim(pieces, (net.s + k) % shards, 0, False)
        got.append(net.turn(piece, k))
    pack = net.gather_all(share)
    half_w = jnp.stack(plane_w)
    qkv_w = assemble(net.where, early_w, half_w, net.swap(half_w), shards)
    line = net.line_order(got)
    cut = ada_rows.shape[1]
    ada = line[:, :cut].reshape(-1)
    ends = [cut]
    for vec in (b_fc1, b_fc2, gain1, gain2):
        ends.append(ends[-1] + vec.shape[0])
    fc1_b, fc2_b, gain_a, gain_b = (
        line[:, ends[i] : ends[i + 1]].reshape(-1) for i in range(4)
    )
    shift_one, scale_one, gate_one, shift_two, scale_two, gate_two = jnp.split(ada, 6)

    half_seg = tree_seg.reshape(shards, 2, rows)

    def row_segs(half):
        return lax.dynamic_index_in_dim(half_seg, half, 1, False).reshape(-1)

    query_seg = row_segs(net.c)
    key_seg = jnp.stack(
        [query_seg.reshape(shards, rows), row_segs(1 - net.c).reshape(shards, rows)], axis=1
    ).reshape(-1)
    lanes = jnp.arange(LANES, dtype=F32)
    table = jnp.zeros((LANES,), F32).at[:labels].set(parent_row)
    up_two = jnp.sum(jnp.where(table[:, None] == lanes[None, :], table[None, :], 0.0), axis=1)
    reach = (
        (lanes[:, None] == lanes[None, :])
        | (table[:, None] == lanes[None, :])
        | (up_two[:, None] == lanes[None, :])
    )
    hot = (key_seg[:, None] == lanes[None, :]).astype(BF)
    hot_mine = hot.reshape(shards, 2, rows, LANES)[:, 0].reshape(mine, LANES)
    feat = mm(hot_mine, jnp.where(reach, 0.0, BIG).astype(BF)).astype(BF)
    held = jnp.max(hot.reshape(-1, SPAN, LANES), axis=1)
    asking = jnp.max(hot_mine.reshape(-1, BLOCK, LANES), axis=1)
    wanted = mm(asking, reach.astype(BF)).astype(BF)
    flags = (mm_t(wanted, held) > 0.5).reshape(-1).astype(jnp.int32)

    vec_one = jnp.stack([gain_a, 1.0 + scale_one, shift_one] + [gain_a] * 5)
    cot_both = net.by_core(cot_keep, cot_got).reshape(shards, rows, width)
    act_one, query, kv, peak = entry(tok, vec_one, qkv_w)
    kv, cot_both = lax.optimization_barrier((kv, cot_both))
    far = net.swap(kv)
    grad_out = net.exchange(cot_both)
    bound = jnp.max(peak[:1]).reshape(1)
    attn, log_totals = attn_fwd(query, kv, far, feat, hot, flags, bound, scale, PAIRS)
    vec = jnp.stack(
        [gate_one, gain_b, 1.0 + scale_two, shift_two, gate_two, fc2_b, fc2_b, fc2_b]
    )
    result, grad_attn, grad_mid, blocks, sums, g_b1 = middle(
        net.where, attn, tok, grad_out, vec, fc1_b[None], pack, groups
    )
    out_rows = net.from_trees(result)

    parts = net.group_sum(blocks.reshape(-1, 9 * width)).reshape(shards, -1, 9 * width)
    q_grads, near_grads, far_grads = attn_bwd(
        query, kv, far, feat, hot, flags, bound, attn, grad_attn, log_totals, scale, PAIRS
    )
    near_grads, parts, out_rows = lax.optimization_barrier((near_grads, parts, out_rows))
    out_keep, out_give = net.back(out_rows, batches)
    out_got = net.swap(out_give)
    turned = net.turns(parts)
    grad_in, g_mine, g_yours, late_sums = leave(
        net.where, q_grads, near_grads, net.swap(far_grads), act_one, qkv_w, tok, grad_mid,
        vec_one, (2, groups // 2, shards, part_rows),
    )

    turned, out_got, grad_in, g_mine, g_yours, late_sums = lax.optimization_barrier(
        (turned, out_got, grad_in, g_mine, g_yours, late_sums)
    )
    span = g_mine.shape[-1]
    g_got = net.swap(g_yours)
    grads_rows = net.from_trees(grad_in)
    small = jnp.concatenate(
        [late_sums[:2], sums[:4], late_sums[2:3], sums[4:6], g_b1.reshape(-1, width)]
    ).astype(BF)
    n_ada = 6 * width
    small_got = net.swap(small)
    rest_line = total([parts[0]] + turned).astype(BF)
    my_cond = lax.dynamic_index_in_dim(conds, net.s, 0, False)
    cond_top = my_cond.astype(BF)
    tree_extra = jnp.concatenate([cond_top, (my_cond - cond_top.astype(F32)).astype(BF)])
    g_got, small_got, rest_line, tree_extra = lax.optimization_barrier(
        (g_got, small_got, rest_line, tree_extra)
    )
    pairs = [
        total([g_mine[k], g_got[k]]).astype(BF).reshape(-1, span) for k in range(groups // 2)
    ]
    pair_small = total([small, small_got]).astype(BF).reshape(-1)
    per_tree = jnp.concatenate([pair_small[:n_ada], tree_extra, pair_small[n_ada:]])
    n_tree = per_tree.shape[0]
    if groups == 8:
        plane_terms = [pairs[0]] + [net.across(pairs[k], k) for k in range(1, 4)]
    else:
        plane_terms = [net.plane_sum(jnp.stack(pairs)[None])[0]]
    plane_small = net.spread(per_tree)
    plane_terms, plane_small, grads_rows, rest_line = lax.optimization_barrier(
        (plane_terms, plane_small, grads_rows, rest_line)
    )

    line_terms = total(plane_terms).astype(BF).reshape(shards, -1, span)
    every_plane = net.plane_order(plane_small)
    mid_part = n_ada + 2 * cond_dim
    bias_sum = jnp.sum(every_plane[:, mid_part:].astype(F32), axis=0).astype(BF)
    line_small = jnp.concatenate([every_plane[:, :mid_part].reshape(-1), bias_sum])
    n_line = line_small.shape[0]
    more = -(-n_line // (8 * span)) * 8
    line_small = jnp.pad(line_small, (0, more * span - n_line)).reshape(more, span)
    line_sent = jnp.concatenate(
        [line_terms, jnp.broadcast_to(line_small[None], (shards, more, span))], axis=1
    )
    line_got = net.turns(line_sent)
    rest_plane = net.spread(rest_line)
    grads_keep, grads_give = net.back(grads_rows, batches)
    grads_got = net.swap(grads_give)
    line_got, rest_plane, grads_got = lax.optimization_barrier((line_got, rest_plane, grads_got))
    rest_half = jnp.stack(rest_plane)
    rest_other = net.swap(rest_half)

    fine = line_terms.shape[1]
    qkv_sum = total([line_terms[0]] + [got[:fine] for got in line_got]).astype(BF)
    qkv_plane = net.spread(qkv_sum)
    everyone = net.line_order([line_small] + [got[fine:] for got in line_got])
    everyone = everyone.reshape(shards, -1)[:, :n_line].astype(F32)
    by_tree = everyone[:, : (groups // 2) * mid_part].reshape(shards, groups // 2, mid_part)
    t_out, t_fc1, t_fc2 = unpack(net.where, rest_half, rest_other, width)
    out = net.lay_out(out_keep, out_got)
    grads_x = net.lay_out(grads_keep, grads_got)

    every_dada = by_tree[:, :, : 6 * width].reshape(-1, 6 * width)
    every_cond = (
        by_tree[:, :, 6 * width : 6 * width + cond_dim] + by_tree[:, :, 6 * width + cond_dim :]
    ).reshape(-1, cond_dim)
    dada = lax.dynamic_index_in_dim(by_tree[:, :, : 6 * width], net.plane, 1, False)
    g_one, g_two, g_bias2, g_bias1 = jnp.split(
        jnp.sum(everyone[:, (groups // 2) * mid_part :], axis=0), [width, 2 * width, 3 * width]
    )

    def place(vec):
        n = vec.shape[-1] // shards
        return lax.dynamic_slice_in_dim(vec, net.s * n, n, vec.ndim - 1)

    dada_here = place(every_dada)
    t_ada = lax.dot_general(
        every_cond, dada_here, (((0,), (0,)), ((), ())), precision=HIGH
    )
    t_bada = jnp.sum(dada_here, axis=0)
    own = lax.dynamic_index_in_dim(dada.reshape(batches, 2, -1), net.c, 1, False)
    ada_w = qkv_w[:, 3 * width :].reshape(shards, cond_dim, -1).astype(F32)
    cond_total = jnp.einsum(
        "bsn,scn->bc", own.reshape(batches, shards, -1), ada_w, precision=HIGH
    )
    qkv_half = jnp.stack(qkv_plane)
    t_qkv = settle(net.where, qkv_half, net.swap(qkv_half)).reshape(w_qkv.shape)
    return (
        out,
        grads_x,
        cond_total[:, None, :],
        t_qkv,
        t_out,
        t_fc1,
        place(g_bias1),
        t_fc2,
        place(g_bias2),
        t_ada,
        t_bada,
        place(g_one),
        place(g_two),
    )


def solution(mesh):
    in_specs = (
        P(None, "group", "shard", None),
        P(None, "group", None),
        P(None, "group", None),
        P(None, "group", None),
        P(None, "group", "shard", None),
        P("shard", None),
        P("shard", None),
        P("shard", None),
        P("shard"),
        P("shard", None),
        P("shard"),
        P(None, "shard"),
        P("shard"),
        P("shard"),
        P("shard"),
    )
    out_specs = (
        P(None, "group", "shard", None),
        P(None, "group", "shard", None),
        P(None, "group", None),
        P("shard", None),
        P("shard", None),
        P("shard", None),
        P("shard"),
        P("shard", None),
        P("shard"),
        P(None, "shard"),
        P("shard"),
        P("shard"),
        P("shard"),
    )
    groups = mesh.shape["group"]

    def run(*args):
        return on_device(*args, groups)

    return jax.shard_map(
        run, mesh=mesh, in_specs=in_specs, out_specs=out_specs, check_vma=False
    )
```

profile of v0, /device:TPU:1, one launch (start us, length us, event | category | flops | bytes accessed | tf_op | source)
XLA Modules:
  0.0 468.9 jit_solution(5971471533257800680)
XLA Ops:
  7.2 1.6 constant_dynamic-slice_fusion.18
  9.3 2.8 collective-permute-start.1
  12.1 2.3 collective-permute-start.2
  16.5 1.4 dynamic-slice_dynamic-update-slice_fusion.1
  18.3 6.4 %collective-permute-done.2 = bf16[24,3072]{1,0:T(8,128)(2,1)S(1)} collective-permute-done((bf16[24,3072]{1,0:T(8,128)(2,1)S(1)}, bf16[24,3072]{1,0:T(8,128)(2,1)S(1)}, u32[]{:S(2)}, u32[]{:S(2)}) %collective-permute-start.2) | collective-permute-done | bytes 147488 | tf_op jit(solution)/shard_map/ppermute | solution.py:748
  24.8 2.9 maximum_select_fusion
  27.6 5.6 %all-to-all-start = ((bf16[4,256,768]{2,1,0:T(8,128)(2,1)}), bf16[4,256,768]{2,1,0:T(8,128)(2,1)S(1)}, u32[]{:S(2)}, u32[]{:S(2)}) async-start(bf16[4,256,768]{2,1,0:T(8,128)(2,1)} %bitcast.13), calls=%async_computation | async-start | bytes 3145728 | tf_op jit(solution)/shard_map/all_to_all | solution.py:763
  33.2 1.6 dynamic-slice_dynamic-update-slice_fusion
  34.8 1.4 fusion.19
  36.2 1.4 fusion.18
  37.6 1.4 fusion.17
  39.0 1.4 fusion.16
  40.4 1.3 constant_dynamic-slice_fusion.12
  41.7 1.3 collective-permute-start.5
  44.9 7.5 %collective-permute-done.5 = bf16[3,24,3072]{2,1,0:T(8,128)(2,1)S(1)} collective-permute-done((bf16[3,24,3072]{2,1,0:T(8,128)(2,1)S(1)}, bf16[3,24,3072]{2,1,0:T(8,128)(2,1)S(1)}, u32[]{:S(2)}, u32[]{:S(2)}) %collective-permute-start.5) | collective-permute-done | bytes 442400 | tf_op jit(solution)/shard_map/ppermute | solution.py:751
  53.3 9.7 %collective-permute-done.7 = bf16[3,24,3072]{2,1,0:T(8,128)(2,1)} collective-permute-done((bf16[3,24,3072]{2,1,0:T(8,128)(2,1)S(1)}, bf16[3,24,3072]{2,1,0:T(8,128)(2,1)}, u32[]{:S(2)}, u32[]{:S(2)}) %collective-permute-start.7) | collective-permute-done | bytes 442400 | tf_op jit(solution)/shard_map/ppermute | solution.py:751
  62.9 6.7 %all-to-all-done = bf16[4,256,768]{2,1,0:T(8,128)(2,1)S(1)} async-done(((bf16[4,256,768]{2,1,0:T(8,128)(2,1)}), bf16[4,256,768]{2,1,0:T(8,128)(2,1)S(1)}, u32[]{:S(2)}, u32[]{:S(2)}) %all-to-all-start) | async-done | bytes 1572896 | tf_op jit(solution)/shard_map/all_to_all | solution.py:763
  69.7 2.2 pad_maximum_fusion.half_ref
  71.9 1.5 collective-permute-start.11
  74.8 1.5 collective-permute-start.9
  76.3 1.7 collective-permute-start.10
  80.2 1.5 collective-permute-done.12
  81.7 3.3 maximum_select_fusion.1
  85.0 5.6 %assemble.1 = bf16[32,24,3072]{2,1,0:T(8,128)(2,1)} custom-call(s32[3]{0:T(128)} %pad_add_fusion.where, bf16[8,24,3072]{2,1,0:T(8,128)(2,1)} %pad_maximum_fusion.1.own_ref, bf16[4,3,24,3072]{3,2,1,0:T(8,128)(2,1)} %copy-done.5, bf16[4,3,24,3072]{3,2,1,0:T(8,128)(2,1)} %collective-permute-done.11.other_ref), custom_call_target="tpu_custom_call" | custom-call | tf_op jit(solution)/shard_map/assemble/pallas_call | solution.py:310
  90.6 11.3 %entry.1 = (bf16[1024,768]{1,0:T(8,128)(2,1)S(1)}, bf16[1024,768]{1,0:T(8,128)(2,1)S(1)}, bf16[1024,1536]{1,0:T(8,128)(2,1)}, f32[8,768]{1,0:T(8,128)S(1)}) custom-call(bf16[1024,768]{1,0:T(8,128)(2,1)S(1)} %bitcast.140, f32[8,768]{1,0:T(8,128)S(1)} %stack.238.vec_ref, bf16[768,3072]{1,0:T(8,128)(2,1)} %bitcast.144), custom_call_target="tpu_custom_call" | custom-call | flops 10350000128 | bytes 1048576 | tf_op jit(solution)/shard_map/entry/pallas_call | solution.py:359
  110.3 3.7 all-to-all-start.1
  114.8 44.0 %attn_forward.1 = (bf16[1024,768]{1,0:T(8,128)(2,1)}, f32[6,4,1,512]{3,2,1,0:T(1,128)}) custom-call(s32[16]{0:T(128)} %reshape.333.flags, f32[1]{0:T(128)} %bitcast.30.peak_ref, bf16[1024,768]{1,0:T(8,128)(2,1)} %copy-done.4, bf16[1024,1536]{1,0:T(8,128)(2,1)} %get-tuple-element.110.kn_ref.vn_ref, bf16[1024,1536]{1,0:T(8,128)(2,1)} %get-tuple-element.110.kn_ref.vn_ref, ...), custom_call_target="tpu_custom_call" | custom-call | flops 43699998720 | bytes 1048576 | tf_op jit(solution)/shard_map/attn_forward/pallas_call | solution.py:148
  158.8 20.4 %all-to-all-done.1 = bf16[4,256,768]{2,1,0:T(8,128)(2,1)S(1)} async-done(((bf16[4,256,768]{2,1,0:T(8,128)(2,1)}), bf16[4,256,768]{2,1,0:T(8,128)(2,1)S(1)}, u32[]{:S(2)}, u32[]{:S(2)}) %all-to-all-start.1) | async-done | bytes 1572896 | tf_op jit(solution)/shard_map/all_to_all | solution.py:763
  179.3 1.4 all-gather.2.cloned.1.call-done.wo_ref.w1_ref.rest_0_.rest_1_.rest_2_.rest_3_
  180.7 57.0 %middle.1 = (bf16[1024,768]{1,0:T(8,128)(2,1)}, bf16[1024,768]{1,0:T(8,128)(2,1)}, f32[1024,768]{1,0:T(8,128)}, bf16[8,4,24,6912]{3,2,1,0:T(8,128)(2,1)}, f32[8,768]{1,0:T(8,128)}, /*index=5*/f32[1,3072]{1,0:T(1,128)}) custom-call(s32[3]{0:T(128)} %pad_add_fusion.where, bf16[1024,768]{1,0:T(8,128)(2,1)} %get-tuple-element.111.attn_ref.o_ref, ...), custom_call_target="tpu_custom_call" | custom-call | flops 63250001920 | bytes 1048576 | tf_op jit(solution)/shard_map/middle/pallas_call | solution.py:686
  237.7 4.4 all-to-all-start.2
  242.1 73.8 %attn_backward.1 = (bf16[1024,768]{1,0:T(8,128)(2,1)}, f32[2,1024,768]{2,1,0:T(8,128)}, bf16[2,1024,768]{2,1,0:T(8,128)(2,1)}) custom-call(s32[16]{0:T(128)} %reshape.333.flags, f32[1]{0:T(128)} %bitcast.30.peak_ref, bf16[1024,768]{1,0:T(8,128)(2,1)} %copy-done.4, bf16[1024,1536]{1,0:T(8,128)(2,1)} %get-tuple-element.110.kn_ref.vn_ref, ...), custom_call_target="tpu_custom_call" | custom-call | flops 72449998848 | bytes 1048576 | tf_op jit(solution)/shard_map/attn_backward/pallas_call | solution.py:257
  316.8 3.8 reduce-scatter.2.cloned.1.call-done
  322.0 1.9 collective-permute-start.14
  323.9 1.5 collective-permute-start.15
  326.6 21.8 %leave.1 = (bf16[1024,768]{1,0:T(8,128)(2,1)}, bf16[4,4,24,2304]{3,2,1,0:T(8,128)(2,1)}, bf16[4,4,24,2304]{3,2,1,0:T(8,128)(2,1)}, f32[8,768]{1,0:T(8,128)}) custom-call(s32[3]{0:T(128)} %pad_add_fusion.where, bf16[1024,768]{1,0:T(8,128)(2,1)} %get-tuple-element.121.dq_ref, f32[2,1024,768]{2,1,0:T(8,128)} %get-tuple-element.122.near_ref, ...), custom_call_target="tpu_custom_call" | custom-call | flops 16099999744 | bytes 1048576 | tf_op jit(solution)/shard_map/leave/pallas_call | solution.py:444
  349.4 1.5 collective-permute-start.19
  352.0 7.9 %all-to-all-start.3 = ((bf16[4,256,768]{2,1,0:T(8,128)(2,1)}), bf16[4,256,768]{2,1,0:T(8,128)(2,1)S(1)}, u32[]{:S(2)}, u32[]{:S(2)}) async-start(bf16[4,256,768]{2,1,0:T(8,128)(2,1)} %bitcast.157), calls=%async_computation.4 | async-start | bytes 3145728 | tf_op jit(solution)/shard_map/all_to_all | solution.py:771
  360.0 1.9 fusion.5
  361.9 3.3 add_convert_fusion.1
  370.3 16.1 %collective-permute-done.24 = bf16[10240]{0:T(1024)(128)(2,1)S(1)} collective-permute-done((bf16[10240]{0:T(1024)(128)(2,1)S(1)}, bf16[10240]{0:T(1024)(128)(2,1)S(1)}, u32[]{:S(2)}, u32[]{:S(2)}) %collective-permute-start.24) | collective-permute-done | bytes 20512 | tf_op jit(solution)/shard_map/ppermute | solution.py:751
  387.5 2.7 collective-permute-done.26
  390.2 6.3 %all-to-all-done.3 = bf16[4,256,768]{2,1,0:T(8,128)(2,1)S(1)} async-done(((bf16[4,256,768]{2,1,0:T(8,128)(2,1)}), bf16[4,256,768]{2,1,0:T(8,128)(2,1)S(1)}, u32[]{:S(2)}, u32[]{:S(2)}) %all-to-all-start.3) | async-done | bytes 1572896 | tf_op jit(solution)/shard_map/all_to_all | solution.py:771
  397.2 1.3 constant_dynamic-slice_fusion.9
  398.5 1.4 collective-permute-start.33
  400.1 1.5 add_convert_fusion
  401.8 1.5 collective-permute-start.28
  404.7 5.2 %collective-permute-done.27 = bf16[40,2304]{1,0:T(8,128)(2,1)S(1)} collective-permute-done((bf16[40,2304]{1,0:T(8,128)(2,1)S(1)}, bf16[40,2304]{1,0:T(8,128)(2,1)S(1)}, u32[]{:S(2)}, u32[]{:S(2)}) %collective-permute-start.27) | collective-permute-done | bytes 184352 | tf_op jit(solution)/shard_map/ppermute | solution.py:748
  411.0 6.0 %collective-permute-done.28 = bf16[40,2304]{1,0:T(8,128)(2,1)S(1)} collective-permute-done((bf16[40,2304]{1,0:T(8,128)(2,1)S(1)}, bf16[40,2304]{1,0:T(8,128)(2,1)S(1)}, u32[]{:S(2)}, u32[]{:S(2)}) %collective-permute-start.28) | collective-permute-done | bytes 184352 | tf_op jit(solution)/shard_map/ppermute | solution.py:748
  417.7 1.3 slice.253
  419.0 1.7 reshape.324
  420.8 2.8 maximum_select_fusion.2
  426.5 1.6 add_convert_fusion.5
  431.9 1.3 pad_maximum_fusion.2.half_ref
  433.2 2.1 collective-permute-start.38
  435.3 2.0 fusion.20
  441.1 1.4 reshape.322
  442.5 1.8 reshape.332
  444.3 1.3 dynamic_slice.164
  445.6 1.3 dynamic_slice.167
  448.2 1.5 dynamic-slice_reduce_fusion
  450.7 3.4 maximum_select_fusion.3
  455.0 1.9 settle.1
  456.9 4.9 %unpack.1 = (f32[8,24,768]{2,1,0:T(8,128)}, f32[8,24,3072]{2,1,0:T(8,128)}, f32[8,4,24,768]{3,2,1,0:T(8,128)}) custom-call(s32[3]{0:T(128)S(1)} %copy-done.2, bf16[4,24,6912]{2,1,0:T(8,128)(2,1)S(1)} %pad_maximum_fusion.2.half_ref, bf16[4,24,6912]{2,1,0:T(8,128)(2,1)S(1)} %collective-permute-done.38.other_ref), custom_call_target="tpu_custom_call" | custom-call | flops 4600000000 | bytes 1048576 | tf_op jit(solution)/shard_map/unpack/pallas_call | solution.py:524
  (278 shorter events, 47.8 us)
Async XLA Ops:
  8.8 9.0 %copy-start.40 = (bf16[1152]{0:T(1024)(128)(2,1)S(1)}, bf16[1152]{0:T(1024)(128)(2,1)}, u32[]{:S(2)}) copy-start(bf16[1152]{0:T(1024)(128)(2,1)} %param.29) | copy-start | bytes 6916
  8.9 9.0 %copy-start.41 = (bf16[768]{0:T(1024)(128)(2,1)S(1)}, bf16[768]{0:T(1024)(128)(2,1)}, u32[]{:S(2)}) copy-start(bf16[768]{0:T(1024)(128)(2,1)} %param.25) | copy-start | bytes 4612
  8.9 9.0 %copy-start.44 = (bf16[192]{0:T(256)(128)(2,1)S(1)}, bf16[192]{0:T(256)(128)(2,1)}, u32[]{:S(2)}) copy-start(bf16[192]{0:T(256)(128)(2,1)} %param.27) | copy-start | bytes 1156
  8.9 9.0 %copy-start.45 = (bf16[192]{0:T(256)(128)(2,1)S(1)}, bf16[192]{0:T(256)(128)(2,1)}, u32[]{:S(2)}) copy-start(bf16[192]{0:T(256)(128)(2,1)} %param.30) | copy-start | bytes 1156
  8.9 9.0 %copy-start.46 = (bf16[192]{0:T(256)(128)(2,1)S(1)}, bf16[192]{0:T(256)(128)(2,1)}, u32[]{:S(2)}) copy-start(bf16[192]{0:T(256)(128)(2,1)} %param.31) | copy-start | bytes 1156
  8.9 15.8 %collective-permute-start.4 = (bf16[2,256,768]{2,1,0:T(8,128)(2,1)S(1)}, bf16[2,256,768]{2,1,0:T(8,128)(2,1)}, u32[]{:S(2)}, u32[]{:S(2)}) collective-permute-start(bf16[2,256,768]{2,1,0:T(8,128)(2,1)S(1)} %get-tuple-element.231), channel_id=1, source_target_pairs={{0,4},{4,0},{8,12},{12,8},{16,20},{20,16},{24,28},{28,24},{1,5},{5... | collective-permute-start | bytes 2359304 | tf_op jit(solution)/shard_map/ppermute | solution.py:744
  9.2 18.4 %copy-start.9 = (bf16[8,24,768]{2,1,0:T(8,128)(2,1)}, bf16[8,24,768]{2,1,0:T(8,128)(2,1)S(1)}, u32[]{:S(2)}) copy-start(bf16[8,24,768]{2,1,0:T(8,128)(2,1)S(1)} %concatenate.44) | copy-start | bytes 884740
  9.3 9.0 %collective-permute-start.1 = (bf16[24,3072]{1,0:T(8,128)(2,1)S(1)}, bf16[24,3072]{1,0:T(8,128)(2,1)S(1)}, u32[]{:S(2)}, u32[]{:S(2)}) collective-permute-start(bf16[24,3072]{1,0:T(8,128)(2,1)S(1)} %fusion.11), channel_id=1, source_target_pairs={{0,1},{1,2},{2,3},{3,0},{4,5},{5,6},{6,7},{7,4},{8,9},{9,10},{10,1... | collective-permute-start | bytes 442376 | tf_op jit(solution)/shard_map/ppermute | solution.py:748
  12.1 12.7 %collective-permute-start.2 = (bf16[24,3072]{1,0:T(8,128)(2,1)S(1)}, bf16[24,3072]{1,0:T(8,128)(2,1)S(1)}, u32[]{:S(2)}, u32[]{:S(2)}) collective-permute-start(bf16[24,3072]{1,0:T(8,128)(2,1)S(1)} %fusion.11), channel_id=1, source_target_pairs={{0,2},{1,3},{2,0},{3,1},{4,6},{5,7},{6,4},{7,5},{8,10},{9,11},{10,... | collective-permute-start | bytes 442376 | tf_op jit(solution)/shard_map/ppermute | solution.py:748
  14.4 10.4 %collective-permute-start.3 = (bf16[24,3072]{1,0:T(8,128)(2,1)S(1)}, bf16[24,3072]{1,0:T(8,128)(2,1)S(1)}, u32[]{:S(2)}, u32[]{:S(2)}) collective-permute-start(bf16[24,3072]{1,0:T(8,128)(2,1)S(1)} %fusion.11), channel_id=1, source_target_pairs={{0,3},{1,0},{2,1},{3,2},{4,7},{5,4},{6,5},{7,6},{8,11},{9,8},{10,9... | collective-permute-start | bytes 442376 | tf_op jit(solution)/shard_map/ppermute | solution.py:748
  15.6 2.4 collective-permute-start
  18.3 9.3 %copy-start.30 = (bf16[24,3072]{1,0:T(8,128)(2,1)}, bf16[24,3072]{1,0:T(8,128)(2,1)S(1)}, u32[]{:S(2)}) copy-start(bf16[24,3072]{1,0:T(8,128)(2,1)S(1)} %collective-permute-done.1) | copy-start | bytes 442372
  27.6 12.7 %copy-start.12 = (bf16[2,1,512,768]{3,2,1,0:T(8,128)(2,1)S(1)}, bf16[2,1,512,768]{3,2,1,0:T(8,128)(2,1)}, u32[]{:S(2)}) copy-start(bf16[2,1,512,768]{3,2,1,0:T(8,128)(2,1)} %param.21) | copy-start | bytes 4718596
  27.6 42.0 %all-to-all-start = ((bf16[4,256,768]{2,1,0:T(8,128)(2,1)}), bf16[4,256,768]{2,1,0:T(8,128)(2,1)S(1)}, u32[]{:S(2)}, u32[]{:S(2)}) async-start(bf16[4,256,768]{2,1,0:T(8,128)(2,1)} %bitcast.13), calls=%async_computation | async-start | bytes 3145728 | tf_op jit(solution)/shard_map/all_to_all | solution.py:763
  33.2 147.5 %all-gather.2.cloned.1.call-start = ((), (), s32[]{:S(2)}) async-start(), calls=%async_computation.5 | async-start | bytes 10948608 | tf_op jit(solution)/shard_map/all_gather | solution.py:801
  41.7 28.0 %copy-start.11 = (bf16[3,24,3072]{2,1,0:T(8,128)(2,1)}, bf16[3,24,3072]{2,1,0:T(8,128)(2,1)S(1)}, u32[]{:S(2)}) copy-start(bf16[3,24,3072]{2,1,0:T(8,128)(2,1)S(1)} %pad_maximum_fusion.3) | copy-start | bytes 1327108
  41.7 10.6 %collective-permute-start.5 = (bf16[3,24,3072]{2,1,0:T(8,128)(2,1)S(1)}, bf16[3,24,3072]{2,1,0:T(8,128)(2,1)S(1)}, u32[]{:S(2)}, u32[]{:S(2)}) collective-permute-start(bf16[3,24,3072]{2,1,0:T(8,128)(2,1)S(1)} %pad_maximum_fusion.3), channel_id=1, source_target_pairs={{0,8},{4,12},{8,0},{12,4},{16,24},{20,28},{24,16},{28,20},{1,9},{5... | collective-permute-start | bytes 1327112 | tf_op jit(solution)/shard_map/ppermute | solution.py:751
  43.0 10.3 %collective-permute-start.6 = (bf16[3,24,3072]{2,1,0:T(8,128)(2,1)S(1)}, bf16[3,24,3072]{2,1,0:T(8,128)(2,1)S(1)}, u32[]{:S(2)}, u32[]{:S(2)}) collective-permute-start(bf16[3,24,3072]{2,1,0:T(8,128)(2,1)S(1)} %pad_maximum_fusion.3), channel_id=1, source_target_pairs={{0,16},{4,20},{8,24},{12,28},{16,0},{20,4},{24,8},{28,12},{1,17},{... | collective-permute-start | bytes 1327112 | tf_op jit(solution)/shard_map/ppermute | solution.py:751
  44.2 18.7 %collective-permute-start.7 = (bf16[3,24,3072]{2,1,0:T(8,128)(2,1)S(1)}, bf16[3,24,3072]{2,1,0:T(8,128)(2,1)}, u32[]{:S(2)}, u32[]{:S(2)}) collective-permute-start(bf16[3,24,3072]{2,1,0:T(8,128)(2,1)S(1)} %pad_maximum_fusion.3), channel_id=1, source_target_pairs={{0,24},{4,28},{8,16},{12,20},{16,8},{20,12},{24,0},{28,4},{1,25},{... | collective-permute-start | bytes 1327112 | tf_op jit(solution)/shard_map/ppermute | solution.py:751
  44.5 60.1 %copy-start.36 = (f32[4,2189]{1,0:T(4,128)}, f32[4,2189]{1,0:T(4,128)S(1)}, u32[]{:S(2)}) copy-start(f32[4,2189]{1,0:T(4,128)S(1)} %select_n.209) | copy-start | bytes 105076
  52.3 17.4 %copy-start.23 = (bf16[3,24,3072]{2,1,0:T(8,128)(2,1)}, bf16[3,24,3072]{2,1,0:T(8,128)(2,1)S(1)}, u32[]{:S(2)}) copy-start(bf16[3,24,3072]{2,1,0:T(8,128)(2,1)S(1)} %collective-permute-done.5) | copy-start | bytes 1327108
  53.3 16.4 %copy-start.24 = (bf16[3,24,3072]{2,1,0:T(8,128)(2,1)}, bf16[3,24,3072]{2,1,0:T(8,128)(2,1)S(1)}, u32[]{:S(2)}) copy-start(bf16[3,24,3072]{2,1,0:T(8,128)(2,1)S(1)} %collective-permute-done.6) | copy-start | bytes 1327108
  69.7 20.9 %copy-start = (bf16[4,256,768]{2,1,0:T(8,128)(2,1)}, bf16[4,256,768]{2,1,0:T(8,128)(2,1)S(1)}, u32[]{:S(2)}) copy-start(bf16[4,256,768]{2,1,0:T(8,128)(2,1)S(1)} %all-to-all-done) | copy-start | bytes 4718596
  71.9 8.1 %copy-start.5 = (bf16[4,3,24,3072]{3,2,1,0:T(8,128)(2,1)}, bf16[4,3,24,3072]{3,2,1,0:T(8,128)(2,1)S(1)}, u32[]{:S(2)}) copy-start(bf16[4,3,24,3072]{3,2,1,0:T(8,128)(2,1)S(1)} %pad_maximum_fusion.half_ref) | copy-start | bytes 5308420
  71.9 13.1 %collective-permute-start.11 = (bf16[4,3,24,3072]{3,2,1,0:T(8,128)(2,1)S(1)}, bf16[4,3,24,3072]{3,2,1,0:T(8,128)(2,1)}, u32[]{:S(2)}, u32[]{:S(2)}) collective-permute-start(bf16[4,3,24,3072]{3,2,1,0:T(8,128)(2,1)S(1)} %pad_maximum_fusion.half_ref), channel_id=1, source_target_pairs={{0,4},{4,0},{8,12},{12,8},{16,20},{20,16},{24,28},{28,24},{1,5},{5... | collective-permute-start | bytes 5308424 | tf_op jit(solution)/shard_map/ppermute | solution.py:744
  74.7 4.7 %collective-permute-start.8 = (f32[2496]{0:T(1024)S(1)}, f32[2496]{0:T(1024)S(1)}, u32[]{:S(2)}, u32[]{:S(2)}) collective-permute-start(f32[2496]{0:T(1024)S(1)} %get-tuple-element.217), channel_id=1, source_target_pairs={{0,1},{1,2},{2,3},{3,0},{4,5},{5,6},{6,7},{7,4},{8,9},{9,10},{10,1... | collective-permute-start | bytes 29960 | tf_op jit(solution)/shard_map/ppermute | solution.py:748
  74.8 4.7 %collective-permute-start.9 = (f32[2496]{0:T(1024)S(1)}, f32[2496]{0:T(1024)S(1)}, u32[]{:S(2)}, u32[]{:S(2)}) collective-permute-start(f32[2496]{0:T(1024)S(1)} %get-tuple-element.219), channel_id=1, source_target_pairs={{0,2},{1,3},{2,0},{3,1},{4,6},{5,7},{6,4},{7,5},{8,10},{9,11},{10,... | collective-permute-start | bytes 29960 | tf_op jit(solution)/shard_map/ppermute | solution.py:748
  76.3 3.4 collective-permute-start.10
  78.6 3.1 collective-permute-start.12
  80.2 10.4 %copy-start.1 = (f32[8,768]{1,0:T(8,128)}, f32[8,768]{1,0:T(8,128)S(1)}, u32[]{:S(2)}) copy-start(f32[8,768]{1,0:T(8,128)S(1)} %stack.238.vec_ref) | copy-start | bytes 73732
  104.2 10.6 %collective-permute-start.13 = (bf16[1024,1536]{1,0:T(8,128)(2,1)}, bf16[1024,1536]{1,0:T(8,128)(2,1)}, u32[]{:S(2)}, u32[]{:S(2)}) collective-permute-start(bf16[1024,1536]{1,0:T(8,128)(2,1)} %get-tuple-element.110.kn_ref.vn_ref), channel_id=1, source_target_pairs={{0,4},{4,0},{8,12},{12,8},{16,20},{20,16},{24,28},{28,24},{1,5},{5... | collective-permute-start | bytes 9437192 | tf_op jit(solution)/shard_map/ppermute | solution.py:744
  110.3 69.0 %all-to-all-start.1 = ((bf16[4,256,768]{2,1,0:T(8,128)(2,1)}), bf16[4,256,768]{2,1,0:T(8,128)(2,1)S(1)}, u32[]{:S(2)}, u32[]{:S(2)}) async-start(bf16[4,256,768]{2,1,0:T(8,128)(2,1)} %bitcast.32), calls=%async_computation.1 | async-start | bytes 3145728 | tf_op jit(solution)/shard_map/all_to_all | solution.py:763
  114.0 206.6 %reduce-scatter.2.cloned.1.call-start = ((), (), s32[]{:S(2)}) async-start(), calls=%async_computation.6 | async-start | bytes 11943936 | tf_op jit(solution)/shard_map/reduce_scatter | solution.py:808
  237.7 79.1 %all-to-all-start.2 = ((bf16[4,256,768]{2,1,0:T(8,128)(2,1)}), bf16[4,256,768]{2,1,0:T(8,128)(2,1)S(1)}, u32[]{:S(2)}, u32[]{:S(2)}) async-start(bf16[4,256,768]{2,1,0:T(8,128)(2,1)} %bitcast.37), calls=%async_computation.3 | async-start | bytes 3145728 | tf_op jit(solution)/shard_map/all_to_all | solution.py:771
  315.9 10.7 %collective-permute-start.18 = (bf16[2,1024,768]{2,1,0:T(8,128)(2,1)}, bf16[2,1024,768]{2,1,0:T(8,128)(2,1)}, u32[]{:S(2)}, u32[]{:S(2)}) collective-permute-start(bf16[2,1024,768]{2,1,0:T(8,128)(2,1)} %get-tuple-element.123), channel_id=1, source_target_pairs={{0,4},{4,0},{8,12},{12,8},{16,20},{20,16},{24,28},{28,24},{1,5},{5... | collective-permute-start | bytes 9437192 | tf_op jit(solution)/shard_map/ppermute | solution.py:744
  320.7 27.7 %collective-permute-start.17 = (bf16[2,256,768]{2,1,0:T(8,128)(2,1)S(1)}, bf16[2,256,768]{2,1,0:T(8,128)(2,1)S(1)}, u32[]{:S(2)}, u32[]{:S(2)}) collective-permute-start(bf16[2,256,768]{2,1,0:T(8,128)(2,1)S(1)} %get-tuple-element.227), channel_id=1, source_target_pairs={{0,4},{4,0},{8,12},{12,8},{16,20},{20,16},{24,28},{28,24},{1,5},{5... | collective-permute-start | bytes 2359304 | tf_op jit(solution)/shard_map/ppermute | solution.py:744
  322.0 26.4 %collective-permute-start.14 = (bf16[24,6912]{1,0:T(8,128)(2,1)S(1)}, bf16[24,6912]{1,0:T(8,128)(2,1)S(1)}, u32[]{:S(2)}, u32[]{:S(2)}) collective-permute-start(bf16[24,6912]{1,0:T(8,128)(2,1)S(1)} %get-tuple-element.234), channel_id=1, source_target_pairs={{0,1},{1,2},{2,3},{3,0},{4,5},{5,6},{6,7},{7,4},{8,9},{9,10},{10,1... | collective-permute-start | bytes 995336 | tf_op jit(solution)/shard_map/ppermute | solution.py:748
  323.9 24.5 %collective-permute-start.15 = (bf16[24,6912]{1,0:T(8,128)(2,1)S(1)}, bf16[24,6912]{1,0:T(8,128)(2,1)S(1)}, u32[]{:S(2)}, u32[]{:S(2)}) collective-permute-start(bf16[24,6912]{1,0:T(8,128)(2,1)S(1)} %get-tuple-element.233), channel_id=1, source_target_pairs={{0,2},{1,3},{2,0},{3,1},{4,6},{5,7},{6,4},{7,5},{8,10},{9,11},{10,... | collective-permute-start | bytes 995336 | tf_op jit(solution)/shard_map/ppermute | solution.py:748
  325.4 23.1 %collective-permute-start.16 = (bf16[24,6912]{1,0:T(8,128)(2,1)S(1)}, bf16[24,6912]{1,0:T(8,128)(2,1)S(1)}, u32[]{:S(2)}, u32[]{:S(2)}) collective-permute-start(bf16[24,6912]{1,0:T(8,128)(2,1)S(1)} %get-tuple-element.232), channel_id=1, source_target_pairs={{0,3},{1,0},{2,1},{3,2},{4,7},{5,4},{6,5},{7,6},{8,11},{9,8},{10,9... | collective-permute-start | bytes 995336 | tf_op jit(solution)/shard_map/ppermute | solution.py:748
  326.6 24.3 %copy-start.37 = (f32[8,768]{1,0:T(8,128)S(1)}, f32[8,768]{1,0:T(8,128)}, u32[]{:S(2)}) copy-start(f32[8,768]{1,0:T(8,128)} %get-tuple-element.134) | copy-start | bytes 73732
  326.6 24.3 %copy-start.39 = (f32[1,3072]{1,0:T(1,128)S(1)}, f32[1,3072]{1,0:T(1,128)}, u32[]{:S(2)}) copy-start(f32[1,3072]{1,0:T(1,128)} %get-tuple-element.135) | copy-start | bytes 36868
  349.4 12.5 %collective-permute-start.19 = (bf16[4,4,24,2304]{3,2,1,0:T(8,128)(2,1)}, bf16[4,4,24,2304]{3,2,1,0:T(8,128)(2,1)}, u32[]{:S(2)}, u32[]{:S(2)}) collective-permute-start(bf16[4,4,24,2304]{3,2,1,0:T(8,128)(2,1)} %get-tuple-element.132), channel_id=1, source_target_pairs={{0,4},{4,0},{8,12},{12,8},{16,20},{20,16},{24,28},{28,24},{1,5},{5... | collective-permute-start | bytes 5308424 | tf_op jit(solution)/shard_map/ppermute | solution.py:744
  351.9 9.9 %collective-permute-start.20 = (bf16[13,768]{1,0:T(8,128)(2,1)S(1)}, bf16[13,768]{1,0:T(8,128)(2,1)S(1)}, u32[]{:S(2)}, u32[]{:S(2)}) collective-permute-start(bf16[13,768]{1,0:T(8,128)(2,1)S(1)} %concatenate.49), channel_id=1, source_target_pairs={{0,4},{4,0},{8,12},{12,8},{16,20},{20,16},{24,28},{28,24},{1,5},{5... | collective-permute-start | bytes 59912 | tf_op jit(solution)/shard_map/ppermute | solution.py:744
  352.0 44.4 %all-to-all-start.3 = ((bf16[4,256,768]{2,1,0:T(8,128)(2,1)}), bf16[4,256,768]{2,1,0:T(8,128)(2,1)S(1)}, u32[]{:S(2)}, u32[]{:S(2)}) async-start(bf16[4,256,768]{2,1,0:T(8,128)(2,1)} %bitcast.157), calls=%async_computation.4 | async-start | bytes 3145728 | tf_op jit(solution)/shard_map/all_to_all | solution.py:771
  365.1 25.0 %collective-permute-start.21 = (bf16[96,2304]{1,0:T(8,128)(2,1)}, bf16[96,2304]{1,0:T(8,128)(2,1)S(1)}, u32[]{:S(2)}, u32[]{:S(2)}) collective-permute-start(bf16[96,2304]{1,0:T(8,128)(2,1)} %bitcast.48), channel_id=1, source_target_pairs={{0,8},{4,12},{8,0},{12,4},{16,24},{20,28},{24,16},{28,20},{1,9},{5... | collective-permute-start | bytes 1327112 | tf_op jit(solution)/shard_map/ppermute | solution.py:751
  366.2 24.0 %collective-permute-start.22 = (bf16[96,2304]{1,0:T(8,128)(2,1)}, bf16[96,2304]{1,0:T(8,128)(2,1)}, u32[]{:S(2)}, u32[]{:S(2)}) collective-permute-start(bf16[96,2304]{1,0:T(8,128)(2,1)} %bitcast.49), channel_id=1, source_target_pairs={{0,16},{4,20},{8,24},{12,28},{16,0},{20,4},{24,8},{28,12},{1,17},{... | collective-permute-start | bytes 1327112 | tf_op jit(solution)/shard_map/ppermute | solution.py:751
  366.6 23.6 %collective-permute-start.23 = (bf16[96,2304]{1,0:T(8,128)(2,1)}, bf16[96,2304]{1,0:T(8,128)(2,1)}, u32[]{:S(2)}, u32[]{:S(2)}) collective-permute-start(bf16[96,2304]{1,0:T(8,128)(2,1)} %bitcast.50), channel_id=1, source_target_pairs={{0,24},{4,28},{8,16},{12,20},{16,8},{20,12},{24,0},{28,4},{1,25},{... | collective-permute-start | bytes 1327112 | tf_op jit(solution)/shard_map/ppermute | solution.py:751
  368.8 17.6 %collective-permute-start.24 = (bf16[10240]{0:T(1024)(128)(2,1)S(1)}, bf16[10240]{0:T(1024)(128)(2,1)S(1)}, u32[]{:S(2)}, u32[]{:S(2)}) collective-permute-start(bf16[10240]{0:T(1024)(128)(2,1)S(1)} %dynamic-update-slice.4), channel_id=1, source_target_pairs={{0,8},{4,12},{8,0},{12,4},{16,24},{20,28},{24,16},{28,20},{1,9},{5... | collective-permute-start | bytes 61448 | tf_op jit(solution)/shard_map/ppermute | solution.py:751
  369.9 17.6 %collective-permute-start.25 = (bf16[10240]{0:T(1024)(128)(2,1)S(1)}, bf16[10240]{0:T(1024)(128)(2,1)S(1)}, u32[]{:S(2)}, u32[]{:S(2)}) collective-permute-start(bf16[10240]{0:T(1024)(128)(2,1)S(1)} %dynamic-update-slice.4), channel_id=1, source_target_pairs={{0,16},{4,20},{8,24},{12,28},{16,0},{20,4},{24,8},{28,12},{1,17},{... | collective-permute-start | bytes 61448 | tf_op jit(solution)/shard_map/ppermute | solution.py:751
  386.3 3.8 collective-permute-start.26
  398.5 25.2 %collective-permute-start.33 = (bf16[2,256,768]{2,1,0:T(8,128)(2,1)}, bf16[2,256,768]{2,1,0:T(8,128)(2,1)}, u32[]{:S(2)}, u32[]{:S(2)}) collective-permute-start(bf16[2,256,768]{2,1,0:T(8,128)(2,1)} %get-tuple-element.225), channel_id=1, source_target_pairs={{0,4},{4,0},{8,12},{12,8},{16,20},{20,16},{24,28},{28,24},{1,5},{5... | collective-permute-start | bytes 2359304 | tf_op jit(solution)/shard_map/ppermute | solution.py:744
  401.7 8.2 %collective-permute-start.27 = (bf16[40,2304]{1,0:T(8,128)(2,1)S(1)}, bf16[40,2304]{1,0:T(8,128)(2,1)S(1)}, u32[]{:S(2)}, u32[]{:S(2)}) collective-permute-start(bf16[40,2304]{1,0:T(8,128)(2,1)S(1)} %get-tuple-element.237), channel_id=1, source_target_pairs={{0,1},{1,2},{2,3},{3,0},{4,5},{5,6},{6,7},{7,4},{8,9},{9,10},{10,1... | collective-permute-start | bytes 552968 | tf_op jit(solution)/shard_map/ppermute | solution.py:748
  401.8 15.2 %collective-permute-start.28 = (bf16[40,2304]{1,0:T(8,128)(2,1)S(1)}, bf16[40,2304]{1,0:T(8,128)(2,1)S(1)}, u32[]{:S(2)}, u32[]{:S(2)}) collective-permute-start(bf16[40,2304]{1,0:T(8,128)(2,1)S(1)} %get-tuple-element.236), channel_id=1, source_target_pairs={{0,2},{1,3},{2,0},{3,1},{4,6},{5,7},{6,4},{7,5},{8,10},{9,11},{10,... | collective-permute-start | bytes 552968 | tf_op jit(solution)/shard_map/ppermute | solution.py:748
  403.2 20.4 %collective-permute-start.30 = (bf16[24,6912]{1,0:T(8,128)(2,1)S(1)}, bf16[24,6912]{1,0:T(8,128)(2,1)S(1)}, u32[]{:S(2)}, u32[]{:S(2)}) collective-permute-start(bf16[24,6912]{1,0:T(8,128)(2,1)S(1)} %copy-done.15), channel_id=1, source_target_pairs={{0,8},{4,12},{8,0},{12,4},{16,24},{20,28},{24,16},{28,20},{1,9},{5... | collective-permute-start | bytes 995336 | tf_op jit(solution)/shard_map/ppermute | solution.py:751
  404.3 19.4 %collective-permute-start.31 = (bf16[24,6912]{1,0:T(8,128)(2,1)S(1)}, bf16[24,6912]{1,0:T(8,128)(2,1)}, u32[]{:S(2)}, u32[]{:S(2)}) collective-permute-start(bf16[24,6912]{1,0:T(8,128)(2,1)S(1)} %copy-done.15), channel_id=1, source_target_pairs={{0,16},{4,20},{8,24},{12,28},{16,0},{20,4},{24,8},{28,12},{1,17},{... | collective-permute-start | bytes 995336 | tf_op jit(solution)/shard_map/ppermute | solution.py:751
  409.9 7.1 %copy-start.26 = (bf16[40,2304]{1,0:T(8,128)(2,1)}, bf16[40,2304]{1,0:T(8,128)(2,1)S(1)}, u32[]{:S(2)}) copy-start(bf16[40,2304]{1,0:T(8,128)(2,1)S(1)} %collective-permute-done.27) | copy-start | bytes 552964
  409.9 13.8 %collective-permute-start.32 = (bf16[24,6912]{1,0:T(8,128)(2,1)S(1)}, bf16[24,6912]{1,0:T(8,128)(2,1)}, u32[]{:S(2)}, u32[]{:S(2)}) collective-permute-start(bf16[24,6912]{1,0:T(8,128)(2,1)S(1)} %copy-done.15), channel_id=1, source_target_pairs={{0,24},{4,28},{8,16},{12,20},{16,8},{20,12},{24,0},{28,4},{1,25},{... | collective-permute-start | bytes 995336 | tf_op jit(solution)/shard_map/ppermute | solution.py:751
  417.7 5.9 %collective-permute-start.29 = (bf16[40,2304]{1,0:T(8,128)(2,1)S(1)}, bf16[40,2304]{1,0:T(8,128)(2,1)}, u32[]{:S(2)}, u32[]{:S(2)}) collective-permute-start(bf16[40,2304]{1,0:T(8,128)(2,1)S(1)} %get-tuple-element.235), channel_id=1, source_target_pairs={{0,3},{1,0},{2,1},{3,2},{4,7},{5,4},{6,5},{7,6},{8,11},{9,8},{10,9... | collective-permute-start | bytes 552968 | tf_op jit(solution)/shard_map/ppermute | solution.py:748
  428.1 9.3 %collective-permute-start.34 = (bf16[24,2304]{1,0:T(8,128)(2,1)}, bf16[24,2304]{1,0:T(8,128)(2,1)}, u32[]{:S(2)}, u32[]{:S(2)}) collective-permute-start(bf16[24,2304]{1,0:T(8,128)(2,1)} %add_convert_fusion.5), channel_id=1, source_target_pairs={{0,8},{4,12},{8,0},{12,4},{16,24},{20,28},{24,16},{28,20},{1,9},{5... | collective-permute-start | bytes 331784 | tf_op jit(solution)/shard_map/ppermute | solution.py:751
  429.2 8.2 %collective-permute-start.35 = (bf16[24,2304]{1,0:T(8,128)(2,1)}, bf16[24,2304]{1,0:T(8,128)(2,1)}, u32[]{:S(2)}, u32[]{:S(2)}) collective-permute-start(bf16[24,2304]{1,0:T(8,128)(2,1)} %add_convert_fusion.5), channel_id=1, source_target_pairs={{0,16},{4,20},{8,24},{12,28},{16,0},{20,4},{24,8},{28,12},{1,17},{... | collective-permute-start | bytes 331784 | tf_op jit(solution)/shard_map/ppermute | solution.py:751
  429.6 7.8 %collective-permute-start.36 = (bf16[24,2304]{1,0:T(8,128)(2,1)}, bf16[24,2304]{1,0:T(8,128)(2,1)}, u32[]{:S(2)}, u32[]{:S(2)}) collective-permute-start(bf16[24,2304]{1,0:T(8,128)(2,1)} %add_convert_fusion.5), channel_id=1, source_target_pairs={{0,24},{4,28},{8,16},{12,20},{16,8},{20,12},{24,0},{28,4},{1,25},{... | collective-permute-start | bytes 331784 | tf_op jit(solution)/shard_map/ppermute | solution.py:751
  431.9 7.6 %copy-start.18 = (f32[4,4,4864]{2,1,0:T(4,128)S(1)}, f32[4,4,4864]{2,1,0:T(4,128)}, u32[]{:S(2)}) copy-start(f32[4,4,4864]{2,1,0:T(4,128)} %copy-done.17) | copy-start | bytes 933892
  433.2 23.7 %collective-permute-start.38 = (bf16[4,24,6912]{2,1,0:T(8,128)(2,1)S(1)}, bf16[4,24,6912]{2,1,0:T(8,128)(2,1)S(1)}, u32[]{:S(2)}, u32[]{:S(2)}) collective-permute-start(bf16[4,24,6912]{2,1,0:T(8,128)(2,1)S(1)} %pad_maximum_fusion.2.half_ref), channel_id=1, source_target_pairs={{0,4},{4,0},{8,12},{12,8},{16,20},{20,16},{24,28},{28,24},{1,5},{5... | collective-permute-start | bytes 3981320 | tf_op jit(solution)/shard_map/ppermute | solution.py:744
  438.6 16.5 %collective-permute-start.37 = (bf16[4,24,2304]{2,1,0:T(8,128)(2,1)S(1)}, bf16[4,24,2304]{2,1,0:T(8,128)(2,1)S(1)}, u32[]{:S(2)}, u32[]{:S(2)}) collective-permute-start(bf16[4,24,2304]{2,1,0:T(8,128)(2,1)S(1)} %pad_maximum_fusion.4.half_ref), channel_id=1, source_target_pairs={{0,4},{4,0},{8,12},{12,8},{16,20},{20,16},{24,28},{28,24},{1,5},{5... | collective-permute-start | bytes 1327112 | tf_op jit(solution)/shard_map/ppermute | solution.py:744
  (28 other events, 81.4 us)
Sparse Core Ops, SparseCore 0:
  69.8 110.8 all-gather.1
  237.8 82.7 reduce-scatter.1
where the time goes:
time: 478 us; the launch traced here: 469 us
  Pallas kernels  220 us (46%)
  waiting for transfers between devices  95.1 us (20%)
  starting transfers between devices  60.7 us (13%)
  local copies, waits for them, and re-layouts  39.8 us (8%)
  other arithmetic  32.9 us (7%)
  between operations  15.4 us (3%)
    pallas_call x1, Pallas kernels, attn_bwd(): pl.pallas_call(functools.partial(bwd_kernel, near, pp, scale), grid_spec=...  73.8 us
    pallas_call x1, Pallas kernels, middle(): pl.pallas_call(functools.partial(middle_kernel, shards), grid_spec=pltpu....  57 us
    pallas_call x1, Pallas kernels, attn_fwd(): pl.pallas_call(functools.partial(fwd_kernel, near, pp, scale), grid_spec=...  44 us
    ppermute x15, waiting for transfers between devices, across(): lax.ppermute(value, 'group', [(i, i ^ 2 * step) for i in range(self.group...  36.8 us
    all_to_all x2, waiting for transfers between devices, exchange(): return lax.all_to_all(by_tree, 'shard', 0, 0).reshape(-1, by_tree.shape[-1])  27.2 us
    pallas_call x1, Pallas kernels, leave(): pl.pallas_call(functools.partial(leave_kernel, spots), grid_spec=pltpu.Pr...  21.8 us
    ppermute x12, waiting for transfers between devices, turn(): return lax.ppermute(value, 'shard', [(i, (i + step) % n) for i in range(n)])  18.1 us
    ppermute x12, starting transfers between devices, turn(): return lax.ppermute(value, 'shard', [(i, (i + step) % n) for i in range(n)])  15.6 us
  transfers between devices with their start and end apart: 45, of which 16 were waited for; matrix products, arithmetic and copies ran while one was open for 13% of the time, Pallas kernels for 34%

commit v1 on v0

--- a/solution.py
+++ b/solution.py
@@ -894,7 +894,8 @@
     other = net.swap(packed)
     line_w = net.turns([own_part] * shards)
     tok_got = net.swap(tok_give)
-    other, line_w, tok_got = lax.optimization_barrier((other, line_w, tok_got))
+    other, line_w, tok_got, share = lax.optimization_barrier((other, line_w, tok_got, share))
+    pack = net.gather_all(share)
     tok = net.to_trees(tok_keep, tok_got)
     plane_w = net.spread(jnp.stack(line_w))
     cot_keep, cot_give = net.give(cotangent[:, 0])
@@ -910,15 +911,14 @@
     pieces = jnp.concatenate(
         [ada_rows, jnp.broadcast_to(small[None], (shards, small.shape[0]))], axis=1
     )
-    plane_w, tok, pieces, share, cot_give = lax.optimization_barrier(
-        (plane_w, tok, pieces, share, cot_give)
+    plane_w, tok, pieces, cot_give = lax.optimization_barrier(
+        (plane_w, tok, pieces, cot_give)
     )
     cot_got = net.swap(cot_give)
     got = [lax.dynamic_index_in_dim(pieces, net.s, 0, False)]
     for k in range(1, shards):
         piece = lax.dynamic_index_in_dim(pieces, (net.s + k) % shards, 0, False)
         got.append(net.turn(piece, k))
-    pack = net.gather_all(share)
     half_w = jnp.stack(plane_w)
     qkv_w = assemble(net.where, early_w, half_w, net.swap(half_w), shards)
     line = net.line_order(got)

time: 478 us -> 467 us (0.977)
  waiting for transfers between devices: 95.1 us -> 82.2 us
    all_to_all x2, waiting for transfers between devices: 27.2 us -> 18.3 us  [exchange(): return lax.all_to_all(by_tree, 'shard', 0, 0).reshape(-1, by_tree.shape[-1])]
    unnamed x106 -> x100, local copies, waits for them, and re-layouts: 13.7 us -> 11.6 us
  transfers between devices with their start and end apart: 45 -> 45, of which waited for: 16 -> 13; matrix products, arithmetic and copies ran while one was open for 13% -> 13% of each run, Pallas kernels for 34% -> 35%
where the time goes in v1:
time: 467 us; the launch traced here: 457 us
  Pallas kernels  221 us (47%)
  waiting for transfers between devices  82.2 us (18%)
  starting transfers between devices  63.8 us (14%)
  local copies, waits for them, and re-layouts  36.7 us (8%)
  other arithmetic  33.5 us (7%)
  between operations  15.3 us (3%)
    pallas_call x1, Pallas kernels, attn_bwd(): pl.pallas_call(functools.partial(bwd_kernel, near, pp, scale), grid_spec=...  73.8 us
    pallas_call x1, Pallas kernels, middle(): pl.pallas_call(functools.partial(middle_kernel, shards), grid_spec=pltpu....  56.9 us
    pallas_call x1, Pallas kernels, attn_fwd(): pl.pallas_call(functools.partial(fwd_kernel, near, pp, scale), grid_spec=...  44.2 us
    ppermute x15, waiting for transfers between devices, across(): lax.ppermute(value, 'group', [(i, i ^ 2 * step) for i in range(self.group...  38.4 us
    pallas_call x1, Pallas kernels, leave(): pl.pallas_call(functools.partial(leave_kernel, spots), grid_spec=pltpu.Pr...  21.8 us
    all_to_all x2, waiting for transfers between devices, exchange(): return lax.all_to_all(by_tree, 'shard', 0, 0).reshape(-1, by_tree.shape[-1])  18.3 us
    ppermute x12, starting transfers between devices, turn(): return lax.ppermute(value, 'shard', [(i, (i + step) % n) for i in range(n)])  17.7 us
    ppermute x12, waiting for transfers between devices, turn(): return lax.ppermute(value, 'shard', [(i, (i + step) % n) for i in range(n)])  15.4 us
  transfers between devices with their start and end apart: 45, of which 13 were waited for; matrix products, arithmetic and copies ran while one was open for 13% of the time, Pallas kernels for 35%

profile of v1, /device:TPU:1, one launch (start us, length us, event | category | flops | bytes accessed | tf_op | source)
XLA Modules:
  0.0 457.5 jit_solution(12634137921490689158)
XLA Ops:
  7.3 1.3 concatenate.44
  9.6 2.2 collective-permute-start.1
  11.7 2.3 collective-permute-start.2
  15.3 1.6 collective-permute-start.4
  22.3 2.2 collective-permute-done.2
  24.5 1.4 maximum_select_fusion
  26.0 4.9 %all-to-all-start = ((bf16[4,256,768]{2,1,0:T(8,128)(2,1)}), bf16[4,256,768]{2,1,0:T(8,128)(2,1)S(1)}, u32[]{:S(2)}, u32[]{:S(2)}) async-start(bf16[4,256,768]{2,1,0:T(8,128)(2,1)} %bitcast.18), calls=%async_computation | async-start | bytes 3145728 | tf_op jit(solution)/shard_map/all_to_all | solution.py:763
  31.0 1.3 constant_dynamic-slice_fusion.11
  33.3 1.3 collective-permute-start.5
  34.6 1.2 collective-permute-start.6
  36.4 9.2 %collective-permute-done.5 = bf16[3,24,3072]{2,1,0:T(8,128)(2,1)S(1)} collective-permute-done((bf16[3,24,3072]{2,1,0:T(8,128)(2,1)S(1)}, bf16[3,24,3072]{2,1,0:T(8,128)(2,1)S(1)}, u32[]{:S(2)}, u32[]{:S(2)}) %collective-permute-start.5) | collective-permute-done | bytes 442400 | tf_op jit(solution)/shard_map/ppermute | solution.py:751
  45.7 3.8 collective-permute-done.6
  49.5 6.7 %collective-permute-done.7 = bf16[3,24,3072]{2,1,0:T(8,128)(2,1)} collective-permute-done((bf16[3,24,3072]{2,1,0:T(8,128)(2,1)S(1)}, bf16[3,24,3072]{2,1,0:T(8,128)(2,1)}, u32[]{:S(2)}, u32[]{:S(2)}) %collective-permute-start.7) | collective-permute-done | bytes 442400 | tf_op jit(solution)/shard_map/ppermute | solution.py:751
  56.1 18.2 %all-to-all-done = bf16[4,256,768]{2,1,0:T(8,128)(2,1)S(1)} async-done(((bf16[4,256,768]{2,1,0:T(8,128)(2,1)}), bf16[4,256,768]{2,1,0:T(8,128)(2,1)S(1)}, u32[]{:S(2)}, u32[]{:S(2)}) %all-to-all-start) | async-done | bytes 1572896 | tf_op jit(solution)/shard_map/all_to_all | solution.py:763
  74.4 2.2 pad_maximum_fusion.half_ref
  76.7 1.6 collective-permute-start.11
  79.5 2.2 collective-permute-start.8
  81.7 3.9 collective-permute-start.9
  89.6 3.3 maximum_select_fusion.1
  92.8 6.0 %assemble.1 = bf16[32,24,3072]{2,1,0:T(8,128)(2,1)} custom-call(s32[3]{0:T(128)} %pad_add_fusion.where, bf16[8,24,3072]{2,1,0:T(8,128)(2,1)} %pad_maximum_fusion.1.own_ref, bf16[4,3,24,3072]{3,2,1,0:T(8,128)(2,1)} %copy-done.5, bf16[4,3,24,3072]{3,2,1,0:T(8,128)(2,1)} %collective-permute-done.11.other_ref), custom_call_target="tpu_custom_call" | custom-call | tf_op jit(solution)/shard_map/assemble/pallas_call | solution.py:310
  98.9 11.6 %entry.1 = (bf16[1024,768]{1,0:T(8,128)(2,1)S(1)}, bf16[1024,768]{1,0:T(8,128)(2,1)S(1)}, bf16[1024,1536]{1,0:T(8,128)(2,1)}, f32[8,768]{1,0:T(8,128)S(1)}) custom-call(bf16[1024,768]{1,0:T(8,128)(2,1)S(1)} %bitcast.140, f32[8,768]{1,0:T(8,128)S(1)} %stack.238.vec_ref, bf16[768,3072]{1,0:T(8,128)(2,1)} %bitcast.144), custom_call_target="tpu_custom_call" | custom-call | flops 10350000128 | bytes 1048576 | tf_op jit(solution)/shard_map/entry/pallas_call | solution.py:359
  110.5 1.2 copy-done.3
  119.3 3.6 all-to-all-start.1
  123.7 44.2 %attn_forward.1 = (bf16[1024,768]{1,0:T(8,128)(2,1)}, f32[6,4,1,512]{3,2,1,0:T(1,128)}) custom-call(s32[16]{0:T(128)} %reshape.333.flags, f32[1]{0:T(128)} %bitcast.30.peak_ref, bf16[1024,768]{1,0:T(8,128)(2,1)} %copy-done.4, bf16[1024,1536]{1,0:T(8,128)(2,1)} %get-tuple-element.110.kn_ref.vn_ref, bf16[1024,1536]{1,0:T(8,128)(2,1)} %get-tuple-element.110.kn_ref.vn_ref, ...), custom_call_target="tpu_custom_call" | custom-call | flops 43699998720 | bytes 1048576 | tf_op jit(solution)/shard_map/attn_forward/pallas_call | solution.py:148
  169.1 56.9 %middle.1 = (bf16[1024,768]{1,0:T(8,128)(2,1)}, bf16[1024,768]{1,0:T(8,128)(2,1)}, f32[1024,768]{1,0:T(8,128)}, bf16[8,4,24,6912]{3,2,1,0:T(8,128)(2,1)}, f32[8,768]{1,0:T(8,128)}, /*index=5*/f32[1,3072]{1,0:T(1,128)}) custom-call(s32[3]{0:T(128)} %pad_add_fusion.where, bf16[1024,768]{1,0:T(8,128)(2,1)} %get-tuple-element.111.attn_ref.o_ref, ...), custom_call_target="tpu_custom_call" | custom-call | flops 63250001920 | bytes 1048576 | tf_op jit(solution)/shard_map/middle/pallas_call | solution.py:686
  226.1 4.7 %all-to-all-start.2 = ((bf16[4,256,768]{2,1,0:T(8,128)(2,1)}), bf16[4,256,768]{2,1,0:T(8,128)(2,1)S(1)}, u32[]{:S(2)}, u32[]{:S(2)}) async-start(bf16[4,256,768]{2,1,0:T(8,128)(2,1)} %bitcast.37), calls=%async_computation.3 | async-start | bytes 3145728 | tf_op jit(solution)/shard_map/all_to_all | solution.py:771
  230.7 73.8 %attn_backward.1 = (bf16[1024,768]{1,0:T(8,128)(2,1)}, f32[2,1024,768]{2,1,0:T(8,128)}, bf16[2,1024,768]{2,1,0:T(8,128)(2,1)}) custom-call(s32[16]{0:T(128)} %reshape.333.flags, f32[1]{0:T(128)} %bitcast.30.peak_ref, bf16[1024,768]{1,0:T(8,128)(2,1)} %copy-done.4, bf16[1024,1536]{1,0:T(8,128)(2,1)} %get-tuple-element.110.kn_ref.vn_ref, ...), custom_call_target="tpu_custom_call" | custom-call | flops 72449998848 | bytes 1048576 | tf_op jit(solution)/shard_map/attn_backward/pallas_call | solution.py:257
  305.5 3.8 reduce-scatter.2.cloned.1.call-done
  310.7 1.3 collective-permute-start.14
  311.9 2.1 collective-permute-start.15
  314.1 1.1 collective-permute-start.16
  315.2 21.8 %leave.1 = (bf16[1024,768]{1,0:T(8,128)(2,1)}, bf16[4,4,24,2304]{3,2,1,0:T(8,128)(2,1)}, bf16[4,4,24,2304]{3,2,1,0:T(8,128)(2,1)}, f32[8,768]{1,0:T(8,128)}) custom-call(s32[3]{0:T(128)} %pad_add_fusion.where, bf16[1024,768]{1,0:T(8,128)(2,1)} %get-tuple-element.121.dq_ref, f32[2,1024,768]{2,1,0:T(8,128)} %get-tuple-element.122.near_ref, ...), custom_call_target="tpu_custom_call" | custom-call | flops 16099999744 | bytes 1048576 | tf_op jit(solution)/shard_map/leave/pallas_call | solution.py:444
  338.0 1.5 collective-permute-start.19
  340.6 7.9 %all-to-all-start.3 = ((bf16[4,256,768]{2,1,0:T(8,128)(2,1)}), bf16[4,256,768]{2,1,0:T(8,128)(2,1)S(1)}, u32[]{:S(2)}, u32[]{:S(2)}) async-start(bf16[4,256,768]{2,1,0:T(8,128)(2,1)} %bitcast.157), calls=%async_computation.4 | async-start | bytes 3145728 | tf_op jit(solution)/shard_map/all_to_all | solution.py:771
  348.6 1.9 fusion.5
  350.5 3.3 add_convert_fusion.1
  355.2 1.2 collective-permute-start.23
  358.9 16.1 %collective-permute-done.24 = bf16[10240]{0:T(1024)(128)(2,1)S(1)} collective-permute-done((bf16[10240]{0:T(1024)(128)(2,1)S(1)}, bf16[10240]{0:T(1024)(128)(2,1)S(1)}, u32[]{:S(2)}, u32[]{:S(2)}) %collective-permute-start.24) | collective-permute-done | bytes 20512 | tf_op jit(solution)/shard_map/ppermute | solution.py:751
  375.0 1.2 collective-permute-start.26
  376.1 2.7 collective-permute-done.26
  378.8 6.3 %all-to-all-done.3 = bf16[4,256,768]{2,1,0:T(8,128)(2,1)S(1)} async-done(((bf16[4,256,768]{2,1,0:T(8,128)(2,1)}), bf16[4,256,768]{2,1,0:T(8,128)(2,1)S(1)}, u32[]{:S(2)}, u32[]{:S(2)}) %all-to-all-start.3) | async-done | bytes 1572896 | tf_op jit(solution)/shard_map/all_to_all | solution.py:771
  385.9 1.3 constant_dynamic-slice_fusion.8
  387.1 1.4 collective-permute-start.33
  388.7 1.5 add_convert_fusion
  390.4 1.5 collective-permute-start.28
  393.3 5.2 %collective-permute-done.27 = bf16[40,2304]{1,0:T(8,128)(2,1)S(1)} collective-permute-done((bf16[40,2304]{1,0:T(8,128)(2,1)S(1)}, bf16[40,2304]{1,0:T(8,128)(2,1)S(1)}, u32[]{:S(2)}, u32[]{:S(2)}) %collective-permute-start.27) | collective-permute-done | bytes 184352 | tf_op jit(solution)/shard_map/ppermute | solution.py:748
  398.5 1.2 collective-permute-start.32
  399.7 6.0 %collective-permute-done.28 = bf16[40,2304]{1,0:T(8,128)(2,1)S(1)} collective-permute-done((bf16[40,2304]{1,0:T(8,128)(2,1)S(1)}, bf16[40,2304]{1,0:T(8,128)(2,1)S(1)}, u32[]{:S(2)}, u32[]{:S(2)}) %collective-permute-start.28) | collective-permute-done | bytes 184352 | tf_op jit(solution)/shard_map/ppermute | solution.py:748
  406.3 1.3 slice.253
  407.7 1.7 reshape.324
  409.4 2.8 maximum_select_fusion.2
  415.2 1.6 add_convert_fusion.5
  418.2 1.2 collective-permute-start.36
  420.6 1.3 pad_maximum_fusion.2.half_ref
  421.9 2.1 collective-permute-start.38
  424.0 2.0 fusion.20
  429.7 1.4 reshape.322
  431.1 1.8 reshape.332
  432.9 1.3 dynamic_slice.164
  434.2 1.3 dynamic_slice.167
  436.9 1.5 dynamic-slice_reduce_fusion
  439.3 3.4 maximum_select_fusion.3
  443.6 1.9 settle.1
  445.5 4.9 %unpack.1 = (f32[8,24,768]{2,1,0:T(8,128)}, f32[8,24,3072]{2,1,0:T(8,128)}, f32[8,4,24,768]{3,2,1,0:T(8,128)}) custom-call(s32[3]{0:T(128)S(1)} %copy-done.2, bf16[4,24,6912]{2,1,0:T(8,128)(2,1)S(1)} %pad_maximum_fusion.2.half_ref, bf16[4,24,6912]{2,1,0:T(8,128)(2,1)S(1)} %collective-permute-done.38.other_ref), custom_call_target="tpu_custom_call" | custom-call | flops 4600000000 | bytes 1048576 | tf_op jit(solution)/shard_map/unpack/pallas_call | solution.py:524
  (272 shorter events, 47.8 us)
Async XLA Ops:
  7.2 7.9 %copy-start.11 = (bf16[2,1,512,768]{3,2,1,0:T(8,128)(2,1)S(1)}, bf16[2,1,512,768]{3,2,1,0:T(8,128)(2,1)}, u32[]{:S(2)}) copy-start(bf16[2,1,512,768]{3,2,1,0:T(8,128)(2,1)} %param.17) | copy-start | bytes 4718596
  7.2 160.8 %all-gather.2.cloned.1.call-start = ((), (), s32[]{:S(2)}) async-start(), calls=%async_computation.5 | async-start | bytes 10948608 | tf_op jit(solution)/shard_map/all_gather | solution.py:801
  8.5 6.6 %copy-start.8 = (bf16[8,24,768]{2,1,0:T(8,128)(2,1)}, bf16[8,24,768]{2,1,0:T(8,128)(2,1)S(1)}, u32[]{:S(2)}) copy-start(bf16[8,24,768]{2,1,0:T(8,128)(2,1)S(1)} %concatenate.44) | copy-start | bytes 884740
  9.6 12.8 %collective-permute-start.1 = (bf16[24,3072]{1,0:T(8,128)(2,1)S(1)}, bf16[24,3072]{1,0:T(8,128)(2,1)S(1)}, u32[]{:S(2)}, u32[]{:S(2)}) collective-permute-start(bf16[24,3072]{1,0:T(8,128)(2,1)S(1)} %fusion.11), channel_id=1, source_target_pairs={{0,1},{1,2},{2,3},{3,0},{4,5},{5,6},{6,7},{7,4},{8,9},{9,10},{10,1... | collective-permute-start | bytes 442376 | tf_op jit(solution)/shard_map/ppermute | solution.py:748
  11.7 12.8 %collective-permute-start.2 = (bf16[24,3072]{1,0:T(8,128)(2,1)S(1)}, bf16[24,3072]{1,0:T(8,128)(2,1)}, u32[]{:S(2)}, u32[]{:S(2)}) collective-permute-start(bf16[24,3072]{1,0:T(8,128)(2,1)S(1)} %fusion.11), channel_id=1, source_target_pairs={{0,2},{1,3},{2,0},{3,1},{4,6},{5,7},{6,4},{7,5},{8,10},{9,11},{10,... | collective-permute-start | bytes 442376 | tf_op jit(solution)/shard_map/ppermute | solution.py:748
  14.0 10.5 %collective-permute-start.3 = (bf16[24,3072]{1,0:T(8,128)(2,1)S(1)}, bf16[24,3072]{1,0:T(8,128)(2,1)}, u32[]{:S(2)}, u32[]{:S(2)}) collective-permute-start(bf16[24,3072]{1,0:T(8,128)(2,1)S(1)} %fusion.11), channel_id=1, source_target_pairs={{0,3},{1,0},{2,1},{3,2},{4,7},{5,4},{6,5},{7,6},{8,11},{9,8},{10,9... | collective-permute-start | bytes 442376 | tf_op jit(solution)/shard_map/ppermute | solution.py:748
  15.3 9.2 %collective-permute-start.4 = (bf16[2,256,768]{2,1,0:T(8,128)(2,1)S(1)}, bf16[2,256,768]{2,1,0:T(8,128)(2,1)S(1)}, u32[]{:S(2)}, u32[]{:S(2)}) collective-permute-start(bf16[2,256,768]{2,1,0:T(8,128)(2,1)S(1)} %get-tuple-element.231), channel_id=1, source_target_pairs={{0,4},{4,0},{8,12},{12,8},{16,20},{20,16},{24,28},{28,24},{1,5},{5... | collective-permute-start | bytes 2359304 | tf_op jit(solution)/shard_map/ppermute | solution.py:744
  17.0 5.3 %collective-permute-start = (f32[2,2189]{1,0:T(2,128)S(1)}, f32[2,2189]{1,0:T(2,128)S(1)}, u32[]{:S(2)}, u32[]{:S(2)}) collective-permute-start(f32[2,2189]{1,0:T(2,128)S(1)} %concatenate.42), channel_id=1, source_target_pairs={{0,4},{4,0},{8,12},{12,8},{16,20},{20,16},{24,28},{28,24},{1,5},{5... | collective-permute-start | bytes 52544 | tf_op jit(solution)/shard_map/ppermute | solution.py:744
  25.9 4.9 %copy-start.42 = (bf16[192]{0:T(256)(128)(2,1)S(1)}, bf16[192]{0:T(256)(128)(2,1)}, u32[]{:S(2)}) copy-start(bf16[192]{0:T(256)(128)(2,1)} %param.30) | copy-start | bytes 1156
  26.0 5.0 %copy-start.12 = (bf16[2,1,512,768]{3,2,1,0:T(8,128)(2,1)S(1)}, bf16[2,1,512,768]{3,2,1,0:T(8,128)(2,1)}, u32[]{:S(2)}) copy-start(bf16[2,1,512,768]{3,2,1,0:T(8,128)(2,1)} %param.21) | copy-start | bytes 4718596
  26.0 48.4 %all-to-all-start = ((bf16[4,256,768]{2,1,0:T(8,128)(2,1)}), bf16[4,256,768]{2,1,0:T(8,128)(2,1)S(1)}, u32[]{:S(2)}, u32[]{:S(2)}) async-start(bf16[4,256,768]{2,1,0:T(8,128)(2,1)} %bitcast.18), calls=%async_computation | async-start | bytes 3145728 | tf_op jit(solution)/shard_map/all_to_all | solution.py:763
  31.0 5.1 %copy-start.19 = (bf16[128,1152]{1,0:T(8,128)(2,1)S(1)}, bf16[128,1152]{1,0:T(8,128)(2,1)}, u32[]{:S(2)}) copy-start(bf16[128,1152]{1,0:T(8,128)(2,1)} %param.28) | copy-start | bytes 884740
  33.3 41.1 %copy-start.10 = (bf16[3,24,3072]{2,1,0:T(8,128)(2,1)}, bf16[3,24,3072]{2,1,0:T(8,128)(2,1)S(1)}, u32[]{:S(2)}) copy-start(bf16[3,24,3072]{2,1,0:T(8,128)(2,1)S(1)} %pad_maximum_fusion.3) | copy-start | bytes 1327108
  33.3 12.4 %collective-permute-start.5 = (bf16[3,24,3072]{2,1,0:T(8,128)(2,1)S(1)}, bf16[3,24,3072]{2,1,0:T(8,128)(2,1)S(1)}, u32[]{:S(2)}, u32[]{:S(2)}) collective-permute-start(bf16[3,24,3072]{2,1,0:T(8,128)(2,1)S(1)} %pad_maximum_fusion.3), channel_id=1, source_target_pairs={{0,8},{4,12},{8,0},{12,4},{16,24},{20,28},{24,16},{28,20},{1,9},{5... | collective-permute-start | bytes 1327112 | tf_op jit(solution)/shard_map/ppermute | solution.py:751
  34.6 14.9 %collective-permute-start.6 = (bf16[3,24,3072]{2,1,0:T(8,128)(2,1)S(1)}, bf16[3,24,3072]{2,1,0:T(8,128)(2,1)S(1)}, u32[]{:S(2)}, u32[]{:S(2)}) collective-permute-start(bf16[3,24,3072]{2,1,0:T(8,128)(2,1)S(1)} %pad_maximum_fusion.3), channel_id=1, source_target_pairs={{0,16},{4,20},{8,24},{12,28},{16,0},{20,4},{24,8},{28,12},{1,17},{... | collective-permute-start | bytes 1327112 | tf_op jit(solution)/shard_map/ppermute | solution.py:751
  35.8 20.3 %collective-permute-start.7 = (bf16[3,24,3072]{2,1,0:T(8,128)(2,1)S(1)}, bf16[3,24,3072]{2,1,0:T(8,128)(2,1)}, u32[]{:S(2)}, u32[]{:S(2)}) collective-permute-start(bf16[3,24,3072]{2,1,0:T(8,128)(2,1)S(1)} %pad_maximum_fusion.3), channel_id=1, source_target_pairs={{0,24},{4,28},{8,16},{12,20},{16,8},{20,12},{24,0},{28,4},{1,25},{... | collective-permute-start | bytes 1327112 | tf_op jit(solution)/shard_map/ppermute | solution.py:751
  36.1 77.6 %copy-start.33 = (f32[4,2189]{1,0:T(4,128)}, f32[4,2189]{1,0:T(4,128)S(1)}, u32[]{:S(2)}) copy-start(f32[4,2189]{1,0:T(4,128)S(1)} %select_n.210) | copy-start | bytes 105076
  45.7 28.7 %copy-start.23 = (bf16[3,24,3072]{2,1,0:T(8,128)(2,1)}, bf16[3,24,3072]{2,1,0:T(8,128)(2,1)S(1)}, u32[]{:S(2)}) copy-start(bf16[3,24,3072]{2,1,0:T(8,128)(2,1)S(1)} %collective-permute-done.5) | copy-start | bytes 1327108
  49.5 24.9 %copy-start.24 = (bf16[3,24,3072]{2,1,0:T(8,128)(2,1)}, bf16[3,24,3072]{2,1,0:T(8,128)(2,1)S(1)}, u32[]{:S(2)}) copy-start(bf16[3,24,3072]{2,1,0:T(8,128)(2,1)S(1)} %collective-permute-done.6) | copy-start | bytes 1327108
  74.4 24.5 %copy-start = (bf16[4,256,768]{2,1,0:T(8,128)(2,1)}, bf16[4,256,768]{2,1,0:T(8,128)(2,1)S(1)}, u32[]{:S(2)}) copy-start(bf16[4,256,768]{2,1,0:T(8,128)(2,1)S(1)} %all-to-all-done) | copy-start | bytes 4718596
  76.7 12.7 %copy-start.5 = (bf16[4,3,24,3072]{3,2,1,0:T(8,128)(2,1)}, bf16[4,3,24,3072]{3,2,1,0:T(8,128)(2,1)S(1)}, u32[]{:S(2)}) copy-start(bf16[4,3,24,3072]{3,2,1,0:T(8,128)(2,1)S(1)} %pad_maximum_fusion.half_ref) | copy-start | bytes 5308420
  76.7 16.2 %collective-permute-start.11 = (bf16[4,3,24,3072]{3,2,1,0:T(8,128)(2,1)S(1)}, bf16[4,3,24,3072]{3,2,1,0:T(8,128)(2,1)}, u32[]{:S(2)}, u32[]{:S(2)}) collective-permute-start(bf16[4,3,24,3072]{3,2,1,0:T(8,128)(2,1)S(1)} %pad_maximum_fusion.half_ref), channel_id=1, source_target_pairs={{0,4},{4,0},{8,12},{12,8},{16,20},{20,16},{24,28},{28,24},{1,5},{5... | collective-permute-start | bytes 5308424 | tf_op jit(solution)/shard_map/ppermute | solution.py:744
  79.5 7.5 %collective-permute-start.8 = (f32[2496]{0:T(1024)S(1)}, f32[2496]{0:T(1024)S(1)}, u32[]{:S(2)}, u32[]{:S(2)}) collective-permute-start(f32[2496]{0:T(1024)S(1)} %get-tuple-element.217), channel_id=1, source_target_pairs={{0,1},{1,2},{2,3},{3,0},{4,5},{5,6},{6,7},{7,4},{8,9},{9,10},{10,1... | collective-permute-start | bytes 29960 | tf_op jit(solution)/shard_map/ppermute | solution.py:748
  81.7 6.3 %collective-permute-start.9 = (f32[2496]{0:T(1024)S(1)}, f32[2496]{0:T(1024)S(1)}, u32[]{:S(2)}, u32[]{:S(2)}) collective-permute-start(f32[2496]{0:T(1024)S(1)} %get-tuple-element.219), channel_id=1, source_target_pairs={{0,2},{1,3},{2,0},{3,1},{4,6},{5,7},{6,4},{7,5},{8,10},{9,11},{10,... | collective-permute-start | bytes 29960 | tf_op jit(solution)/shard_map/ppermute | solution.py:748
  85.6 3.5 collective-permute-start.10
  86.2 3.3 collective-permute-start.12
  89.5 9.4 %copy-start.1 = (f32[8,768]{1,0:T(8,128)}, f32[8,768]{1,0:T(8,128)S(1)}, u32[]{:S(2)}) copy-start(f32[8,768]{1,0:T(8,128)S(1)} %stack.238.vec_ref) | copy-start | bytes 73732
  112.9 10.9 %collective-permute-start.13 = (bf16[1024,1536]{1,0:T(8,128)(2,1)}, bf16[1024,1536]{1,0:T(8,128)(2,1)}, u32[]{:S(2)}, u32[]{:S(2)}) collective-permute-start(bf16[1024,1536]{1,0:T(8,128)(2,1)} %get-tuple-element.110.kn_ref.vn_ref), channel_id=1, source_target_pairs={{0,4},{4,0},{8,12},{12,8},{16,20},{20,16},{24,28},{28,24},{1,5},{5... | collective-permute-start | bytes 9437192 | tf_op jit(solution)/shard_map/ppermute | solution.py:744
  119.3 48.6 %all-to-all-start.1 = ((bf16[4,256,768]{2,1,0:T(8,128)(2,1)}), bf16[4,256,768]{2,1,0:T(8,128)(2,1)S(1)}, u32[]{:S(2)}, u32[]{:S(2)}) async-start(bf16[4,256,768]{2,1,0:T(8,128)(2,1)} %bitcast.32), calls=%async_computation.1 | async-start | bytes 3145728 | tf_op jit(solution)/shard_map/all_to_all | solution.py:763
  122.9 186.4 %reduce-scatter.2.cloned.1.call-start = ((), (), s32[]{:S(2)}) async-start(), calls=%async_computation.6 | async-start | bytes 11943936 | tf_op jit(solution)/shard_map/reduce_scatter | solution.py:808
  226.1 79.4 %all-to-all-start.2 = ((bf16[4,256,768]{2,1,0:T(8,128)(2,1)}), bf16[4,256,768]{2,1,0:T(8,128)(2,1)S(1)}, u32[]{:S(2)}, u32[]{:S(2)}) async-start(bf16[4,256,768]{2,1,0:T(8,128)(2,1)} %bitcast.37), calls=%async_computation.3 | async-start | bytes 3145728 | tf_op jit(solution)/shard_map/all_to_all | solution.py:771
  304.6 10.6 %collective-permute-start.18 = (bf16[2,1024,768]{2,1,0:T(8,128)(2,1)}, bf16[2,1024,768]{2,1,0:T(8,128)(2,1)}, u32[]{:S(2)}, u32[]{:S(2)}) collective-permute-start(bf16[2,1024,768]{2,1,0:T(8,128)(2,1)} %get-tuple-element.123), channel_id=1, source_target_pairs={{0,4},{4,0},{8,12},{12,8},{16,20},{20,16},{24,28},{28,24},{1,5},{5... | collective-permute-start | bytes 9437192 | tf_op jit(solution)/shard_map/ppermute | solution.py:744
  309.4 27.7 %collective-permute-start.17 = (bf16[2,256,768]{2,1,0:T(8,128)(2,1)S(1)}, bf16[2,256,768]{2,1,0:T(8,128)(2,1)S(1)}, u32[]{:S(2)}, u32[]{:S(2)}) collective-permute-start(bf16[2,256,768]{2,1,0:T(8,128)(2,1)S(1)} %get-tuple-element.227), channel_id=1, source_target_pairs={{0,4},{4,0},{8,12},{12,8},{16,20},{20,16},{24,28},{28,24},{1,5},{5... | collective-permute-start | bytes 2359304 | tf_op jit(solution)/shard_map/ppermute | solution.py:744
  310.7 26.4 %collective-permute-start.14 = (bf16[24,6912]{1,0:T(8,128)(2,1)S(1)}, bf16[24,6912]{1,0:T(8,128)(2,1)S(1)}, u32[]{:S(2)}, u32[]{:S(2)}) collective-permute-start(bf16[24,6912]{1,0:T(8,128)(2,1)S(1)} %get-tuple-element.234), channel_id=1, source_target_pairs={{0,1},{1,2},{2,3},{3,0},{4,5},{5,6},{6,7},{7,4},{8,9},{9,10},{10,1... | collective-permute-start | bytes 995336 | tf_op jit(solution)/shard_map/ppermute | solution.py:748
  311.9 25.2 %collective-permute-start.15 = (bf16[24,6912]{1,0:T(8,128)(2,1)S(1)}, bf16[24,6912]{1,0:T(8,128)(2,1)S(1)}, u32[]{:S(2)}, u32[]{:S(2)}) collective-permute-start(bf16[24,6912]{1,0:T(8,128)(2,1)S(1)} %get-tuple-element.233), channel_id=1, source_target_pairs={{0,2},{1,3},{2,0},{3,1},{4,6},{5,7},{6,4},{7,5},{8,10},{9,11},{10,... | collective-permute-start | bytes 995336 | tf_op jit(solution)/shard_map/ppermute | solution.py:748
  314.1 23.0 %collective-permute-start.16 = (bf16[24,6912]{1,0:T(8,128)(2,1)S(1)}, bf16[24,6912]{1,0:T(8,128)(2,1)S(1)}, u32[]{:S(2)}, u32[]{:S(2)}) collective-permute-start(bf16[24,6912]{1,0:T(8,128)(2,1)S(1)} %get-tuple-element.232), channel_id=1, source_target_pairs={{0,3},{1,0},{2,1},{3,2},{4,7},{5,4},{6,5},{7,6},{8,11},{9,8},{10,9... | collective-permute-start | bytes 995336 | tf_op jit(solution)/shard_map/ppermute | solution.py:748
  315.2 24.3 %copy-start.34 = (f32[8,768]{1,0:T(8,128)S(1)}, f32[8,768]{1,0:T(8,128)}, u32[]{:S(2)}) copy-start(f32[8,768]{1,0:T(8,128)} %get-tuple-element.134) | copy-start | bytes 73732
  315.2 24.4 %copy-start.36 = (f32[1,3072]{1,0:T(1,128)S(1)}, f32[1,3072]{1,0:T(1,128)}, u32[]{:S(2)}) copy-start(f32[1,3072]{1,0:T(1,128)} %get-tuple-element.135) | copy-start | bytes 36868
  338.0 12.5 %collective-permute-start.19 = (bf16[4,4,24,2304]{3,2,1,0:T(8,128)(2,1)}, bf16[4,4,24,2304]{3,2,1,0:T(8,128)(2,1)}, u32[]{:S(2)}, u32[]{:S(2)}) collective-permute-start(bf16[4,4,24,2304]{3,2,1,0:T(8,128)(2,1)} %get-tuple-element.132), channel_id=1, source_target_pairs={{0,4},{4,0},{8,12},{12,8},{16,20},{20,16},{24,28},{28,24},{1,5},{5... | collective-permute-start | bytes 5308424 | tf_op jit(solution)/shard_map/ppermute | solution.py:744
  340.6 9.9 %collective-permute-start.20 = (bf16[13,768]{1,0:T(8,128)(2,1)S(1)}, bf16[13,768]{1,0:T(8,128)(2,1)S(1)}, u32[]{:S(2)}, u32[]{:S(2)}) collective-permute-start(bf16[13,768]{1,0:T(8,128)(2,1)S(1)} %concatenate.49), channel_id=1, source_target_pairs={{0,4},{4,0},{8,12},{12,8},{16,20},{20,16},{24,28},{28,24},{1,5},{5... | collective-permute-start | bytes 59912 | tf_op jit(solution)/shard_map/ppermute | solution.py:744
  340.6 44.4 %all-to-all-start.3 = ((bf16[4,256,768]{2,1,0:T(8,128)(2,1)}), bf16[4,256,768]{2,1,0:T(8,128)(2,1)S(1)}, u32[]{:S(2)}, u32[]{:S(2)}) async-start(bf16[4,256,768]{2,1,0:T(8,128)(2,1)} %bitcast.157), calls=%async_computation.4 | async-start | bytes 3145728 | tf_op jit(solution)/shard_map/all_to_all | solution.py:771
  353.8 25.0 %collective-permute-start.21 = (bf16[96,2304]{1,0:T(8,128)(2,1)}, bf16[96,2304]{1,0:T(8,128)(2,1)S(1)}, u32[]{:S(2)}, u32[]{:S(2)}) collective-permute-start(bf16[96,2304]{1,0:T(8,128)(2,1)} %bitcast.48), channel_id=1, source_target_pairs={{0,8},{4,12},{8,0},{12,4},{16,24},{20,28},{24,16},{28,20},{1,9},{5... | collective-permute-start | bytes 1327112 | tf_op jit(solution)/shard_map/ppermute | solution.py:751
  354.8 24.0 %collective-permute-start.22 = (bf16[96,2304]{1,0:T(8,128)(2,1)}, bf16[96,2304]{1,0:T(8,128)(2,1)}, u32[]{:S(2)}, u32[]{:S(2)}) collective-permute-start(bf16[96,2304]{1,0:T(8,128)(2,1)} %bitcast.49), channel_id=1, source_target_pairs={{0,16},{4,20},{8,24},{12,28},{16,0},{20,4},{24,8},{28,12},{1,17},{... | collective-permute-start | bytes 1327112 | tf_op jit(solution)/shard_map/ppermute | solution.py:751
  355.2 23.6 %collective-permute-start.23 = (bf16[96,2304]{1,0:T(8,128)(2,1)}, bf16[96,2304]{1,0:T(8,128)(2,1)}, u32[]{:S(2)}, u32[]{:S(2)}) collective-permute-start(bf16[96,2304]{1,0:T(8,128)(2,1)} %bitcast.50), channel_id=1, source_target_pairs={{0,24},{4,28},{8,16},{12,20},{16,8},{20,12},{24,0},{28,4},{1,25},{... | collective-permute-start | bytes 1327112 | tf_op jit(solution)/shard_map/ppermute | solution.py:751
  357.4 17.6 %collective-permute-start.24 = (bf16[10240]{0:T(1024)(128)(2,1)S(1)}, bf16[10240]{0:T(1024)(128)(2,1)S(1)}, u32[]{:S(2)}, u32[]{:S(2)}) collective-permute-start(bf16[10240]{0:T(1024)(128)(2,1)S(1)} %dynamic-update-slice.4), channel_id=1, source_target_pairs={{0,8},{4,12},{8,0},{12,4},{16,24},{20,28},{24,16},{28,20},{1,9},{5... | collective-permute-start | bytes 61448 | tf_op jit(solution)/shard_map/ppermute | solution.py:751
  358.5 17.6 %collective-permute-start.25 = (bf16[10240]{0:T(1024)(128)(2,1)S(1)}, bf16[10240]{0:T(1024)(128)(2,1)S(1)}, u32[]{:S(2)}, u32[]{:S(2)}) collective-permute-start(bf16[10240]{0:T(1024)(128)(2,1)S(1)} %dynamic-update-slice.4), channel_id=1, source_target_pairs={{0,16},{4,20},{8,24},{12,28},{16,0},{20,4},{24,8},{28,12},{1,17},{... | collective-permute-start | bytes 61448 | tf_op jit(solution)/shard_map/ppermute | solution.py:751
  375.0 3.8 collective-permute-start.26
  378.8 6.4 %copy-start.25 = (bf16[96,2304]{1,0:T(8,128)(2,1)}, bf16[96,2304]{1,0:T(8,128)(2,1)S(1)}, u32[]{:S(2)}) copy-start(bf16[96,2304]{1,0:T(8,128)(2,1)S(1)} %collective-permute-done.21) | copy-start | bytes 1327108
  387.1 25.2 %collective-permute-start.33 = (bf16[2,256,768]{2,1,0:T(8,128)(2,1)}, bf16[2,256,768]{2,1,0:T(8,128)(2,1)}, u32[]{:S(2)}, u32[]{:S(2)}) collective-permute-start(bf16[2,256,768]{2,1,0:T(8,128)(2,1)} %get-tuple-element.225), channel_id=1, source_target_pairs={{0,4},{4,0},{8,12},{12,8},{16,20},{20,16},{24,28},{28,24},{1,5},{5... | collective-permute-start | bytes 2359304 | tf_op jit(solution)/shard_map/ppermute | solution.py:744
  390.3 8.2 %collective-permute-start.27 = (bf16[40,2304]{1,0:T(8,128)(2,1)S(1)}, bf16[40,2304]{1,0:T(8,128)(2,1)S(1)}, u32[]{:S(2)}, u32[]{:S(2)}) collective-permute-start(bf16[40,2304]{1,0:T(8,128)(2,1)S(1)} %get-tuple-element.237), channel_id=1, source_target_pairs={{0,1},{1,2},{2,3},{3,0},{4,5},{5,6},{6,7},{7,4},{8,9},{9,10},{10,1... | collective-permute-start | bytes 552968 | tf_op jit(solution)/shard_map/ppermute | solution.py:748
  390.4 15.2 %collective-permute-start.28 = (bf16[40,2304]{1,0:T(8,128)(2,1)S(1)}, bf16[40,2304]{1,0:T(8,128)(2,1)S(1)}, u32[]{:S(2)}, u32[]{:S(2)}) collective-permute-start(bf16[40,2304]{1,0:T(8,128)(2,1)S(1)} %get-tuple-element.236), channel_id=1, source_target_pairs={{0,2},{1,3},{2,0},{3,1},{4,6},{5,7},{6,4},{7,5},{8,10},{9,11},{10,... | collective-permute-start | bytes 552968 | tf_op jit(solution)/shard_map/ppermute | solution.py:748
  391.9 20.4 %collective-permute-start.30 = (bf16[24,6912]{1,0:T(8,128)(2,1)S(1)}, bf16[24,6912]{1,0:T(8,128)(2,1)S(1)}, u32[]{:S(2)}, u32[]{:S(2)}) collective-permute-start(bf16[24,6912]{1,0:T(8,128)(2,1)S(1)} %copy-done.15), channel_id=1, source_target_pairs={{0,8},{4,12},{8,0},{12,4},{16,24},{20,28},{24,16},{28,20},{1,9},{5... | collective-permute-start | bytes 995336 | tf_op jit(solution)/shard_map/ppermute | solution.py:751
  392.9 19.3 %collective-permute-start.31 = (bf16[24,6912]{1,0:T(8,128)(2,1)S(1)}, bf16[24,6912]{1,0:T(8,128)(2,1)}, u32[]{:S(2)}, u32[]{:S(2)}) collective-permute-start(bf16[24,6912]{1,0:T(8,128)(2,1)S(1)} %copy-done.15), channel_id=1, source_target_pairs={{0,16},{4,20},{8,24},{12,28},{16,0},{20,4},{24,8},{28,12},{1,17},{... | collective-permute-start | bytes 995336 | tf_op jit(solution)/shard_map/ppermute | solution.py:751
  398.5 7.1 %copy-start.27 = (bf16[40,2304]{1,0:T(8,128)(2,1)}, bf16[40,2304]{1,0:T(8,128)(2,1)S(1)}, u32[]{:S(2)}) copy-start(bf16[40,2304]{1,0:T(8,128)(2,1)S(1)} %collective-permute-done.27) | copy-start | bytes 552964
  398.5 13.8 %collective-permute-start.32 = (bf16[24,6912]{1,0:T(8,128)(2,1)S(1)}, bf16[24,6912]{1,0:T(8,128)(2,1)}, u32[]{:S(2)}, u32[]{:S(2)}) collective-permute-start(bf16[24,6912]{1,0:T(8,128)(2,1)S(1)} %copy-done.15), channel_id=1, source_target_pairs={{0,24},{4,28},{8,16},{12,20},{16,8},{20,12},{24,0},{28,4},{1,25},{... | collective-permute-start | bytes 995336 | tf_op jit(solution)/shard_map/ppermute | solution.py:751
  406.3 5.9 %collective-permute-start.29 = (bf16[40,2304]{1,0:T(8,128)(2,1)S(1)}, bf16[40,2304]{1,0:T(8,128)(2,1)}, u32[]{:S(2)}, u32[]{:S(2)}) collective-permute-start(bf16[40,2304]{1,0:T(8,128)(2,1)S(1)} %get-tuple-element.235), channel_id=1, source_target_pairs={{0,3},{1,0},{2,1},{3,2},{4,7},{5,4},{6,5},{7,6},{8,11},{9,8},{10,9... | collective-permute-start | bytes 552968 | tf_op jit(solution)/shard_map/ppermute | solution.py:748
  414.5 6.0 %copy-start.16 = (bf16[24,6912]{1,0:T(8,128)(2,1)S(1)}, bf16[24,6912]{1,0:T(8,128)(2,1)}, u32[]{:S(2)}) copy-start(bf16[24,6912]{1,0:T(8,128)(2,1)} %fusion.5) | copy-start | bytes 995332
  416.8 9.3 %collective-permute-start.34 = (bf16[24,2304]{1,0:T(8,128)(2,1)}, bf16[24,2304]{1,0:T(8,128)(2,1)}, u32[]{:S(2)}, u32[]{:S(2)}) collective-permute-start(bf16[24,2304]{1,0:T(8,128)(2,1)} %add_convert_fusion.5), channel_id=1, source_target_pairs={{0,8},{4,12},{8,0},{12,4},{16,24},{20,28},{24,16},{28,20},{1,9},{5... | collective-permute-start | bytes 331784 | tf_op jit(solution)/shard_map/ppermute | solution.py:751
  417.8 8.2 %collective-permute-start.35 = (bf16[24,2304]{1,0:T(8,128)(2,1)}, bf16[24,2304]{1,0:T(8,128)(2,1)}, u32[]{:S(2)}, u32[]{:S(2)}) collective-permute-start(bf16[24,2304]{1,0:T(8,128)(2,1)} %add_convert_fusion.5), channel_id=1, source_target_pairs={{0,16},{4,20},{8,24},{12,28},{16,0},{20,4},{24,8},{28,12},{1,17},{... | collective-permute-start | bytes 331784 | tf_op jit(solution)/shard_map/ppermute | solution.py:751
  418.2 7.8 %collective-permute-start.36 = (bf16[24,2304]{1,0:T(8,128)(2,1)}, bf16[24,2304]{1,0:T(8,128)(2,1)}, u32[]{:S(2)}, u32[]{:S(2)}) collective-permute-start(bf16[24,2304]{1,0:T(8,128)(2,1)} %add_convert_fusion.5), channel_id=1, source_target_pairs={{0,24},{4,28},{8,16},{12,20},{16,8},{20,12},{24,0},{28,4},{1,25},{... | collective-permute-start | bytes 331784 | tf_op jit(solution)/shard_map/ppermute | solution.py:751
  420.6 7.6 %copy-start.18 = (f32[4,4,4864]{2,1,0:T(4,128)S(1)}, f32[4,4,4864]{2,1,0:T(4,128)}, u32[]{:S(2)}) copy-start(f32[4,4,4864]{2,1,0:T(4,128)} %copy-done.17) | copy-start | bytes 933892
  421.9 7.0 %copy-start.21 = (bf16[4,4,4608]{2,1,0:T(4,128)(2,1)S(1)}, bf16[4,4,4608]{2,1,0:T(4,128)(2,1)}, u32[]{:S(2)}) copy-start(bf16[4,4,4608]{2,1,0:T(4,128)(2,1)} %copy-done.20) | copy-start | bytes 442372
  421.9 23.6 %collective-permute-start.38 = (bf16[4,24,6912]{2,1,0:T(8,128)(2,1)S(1)}, bf16[4,24,6912]{2,1,0:T(8,128)(2,1)S(1)}, u32[]{:S(2)}, u32[]{:S(2)}) collective-permute-start(bf16[4,24,6912]{2,1,0:T(8,128)(2,1)S(1)} %pad_maximum_fusion.2.half_ref), channel_id=1, source_target_pairs={{0,4},{4,0},{8,12},{12,8},{16,20},{20,16},{24,28},{28,24},{1,5},{5... | collective-permute-start | bytes 3981320 | tf_op jit(solution)/shard_map/ppermute | solution.py:744
  427.2 16.5 %collective-permute-start.37 = (bf16[4,24,2304]{2,1,0:T(8,128)(2,1)S(1)}, bf16[4,24,2304]{2,1,0:T(8,128)(2,1)S(1)}, u32[]{:S(2)}, u32[]{:S(2)}) collective-permute-start(bf16[4,24,2304]{2,1,0:T(8,128)(2,1)S(1)} %pad_maximum_fusion.4.half_ref), channel_id=1, source_target_pairs={{0,4},{4,0},{8,12},{12,8},{16,20},{20,16},{24,28},{28,24},{1,5},{5... | collective-permute-start | bytes 1327112 | tf_op jit(solution)/shard_map/ppermute | solution.py:744
  (25 other events, 60.5 us)
Sparse Core Ops, SparseCore 0:
  24.6 120.5 all-gather.1
  226.2 83.0 reduce-scatter.1

commit v2 on v1

--- a/solution.py
+++ b/solution.py
@@ -242,7 +242,7 @@
         for i in range(near // BLOCK):
             rows = slice(i * BLOCK, (i + 1) * BLOCK)
             for side, acc in enumerate((dk_acc, dv_acc)):
-                near_ref[side, rows] = acc[2 * i * BLOCK : (2 * i + 1) * BLOCK]
+                near_ref[side, rows] = acc[2 * i * BLOCK : (2 * i + 1) * BLOCK].astype(BF)
                 far_ref[side, rows] = acc[(2 * i + 1) * BLOCK : (2 * i + 2) * BLOCK].astype(BF)
 
 def attn_bwd(q, kv, far, feat, hot, flags, peak, attn, dattn, lse, scale, pp):
@@ -282,7 +282,7 @@
             ]),
         out_shape=[
             jax.ShapeDtypeStruct((near, width), BF),
-            jax.ShapeDtypeStruct((2, near, width), F32),
+            jax.ShapeDtypeStruct((2, near, width), BF),
             jax.ShapeDtypeStruct((2, near, width), BF),
         ],
         compiler_params=pltpu.CompilerParams(vmem_limit_bytes=56<<20),
@@ -324,7 +324,7 @@
 
 def entry_kernel(tok_ref, vec_ref, w_ref, act_ref, q_ref, kv_ref, peak_ref):
     step = pl.program_id(0)
-    rows, pieces = BLOCK, tok_ref.shape[0] // BLOCK
+    rows, pieces = SPAN, tok_ref.shape[0] // SPAN
 
     @pl.when(step == 0)
     def _():
@@ -380,20 +380,27 @@
     )(tok, vec, qkv_w)
 
 
-def leave_kernel(spots, where, dq_ref, near_ref, far_ref, act_ref, w_ref, tok_ref, dmid_ref, vec_ref,
-                 grad_ref, mine_ref, yours_ref, sums_ref, d_all, da):
+def leave_kernel(spots, where, dq_ref, near_ref, far_ref, act_ref, w_ref, tok_in, dmid_in, vec_ref,
+                 grad_ref, mine_ref, yours_ref, sums_ref, d_all, da, tok_ref, dmid_ref, sems):
     step = pl.program_id(0)
     total = dq_ref.shape[0]
     sides, planes, places, fine = spots
 
+    late = [
+        pltpu.make_async_copy(tok_in, tok_ref, sems.at[0]),
+        pltpu.make_async_copy(dmid_in, dmid_ref, sems.at[1]),
+    ]
+
     @pl.when(step == 0)
     def _():
+        for copy in late:
+            copy.start()
         d_all[...] = dq_ref[...]
         da[...] = jnp.zeros_like(da)
 
     @pl.when(step > 0)
     def _():
-        d_all[...] = (near_ref[0] + far_ref[0].astype(F32)).astype(BF)
+        d_all[...] = (near_ref[0].astype(F32) + far_ref[0].astype(F32)).astype(BF)
 
     grad = t_mm(act_ref[...], d_all[...])
 
@@ -409,16 +416,18 @@
         pl.when(where[1] != side)(functools.partial(put, yours_ref, side))
 
     def add(r, _):
-        rows = pl.ds(pl.multiple_of(r * BLOCK, BLOCK), BLOCK)
+        rows = pl.ds(pl.multiple_of(r * SPAN, SPAN), SPAN)
         da[rows, :] += mm_t(d_all[rows, :], w_ref[...])
         return 0
 
-    lax.fori_loop(0, total // BLOCK, add, 0)
+    lax.fori_loop(0, total // SPAN, add, 0)
 
     @pl.when(step == 2)
     def _():
         gain, lift, shift = (vec_ref[i : i + 1, :] for i in range(3))
         sums_ref[...] = jnp.zeros_like(sums_ref)
+        for copy in late:
+            copy.wait()
 
         def finish(r, _):
             rows = pl.ds(pl.multiple_of(r * BLOCK, BLOCK), BLOCK)
@@ -449,14 +458,22 @@
             in_specs=[
                 whole, both, both, whole,
                 pl.BlockSpec((width, width), lambda j, w: (0, j)),
-                whole, whole, small,
+                pl.BlockSpec(memory_space=pl.ANY),
+                pl.BlockSpec(memory_space=pl.ANY),
+                small,
             ],
             out_specs=[
                 whole,
                 part, part,
                 small,
             ],
-            scratch_shapes=[pltpu.VMEM((total, width), BF), pltpu.VMEM((total, width), F32)],
+            scratch_shapes=[
+                pltpu.VMEM((total, width), BF),
+                pltpu.VMEM((total, width), F32),
+                pltpu.VMEM((total, width), BF),
+                pltpu.VMEM((total, width), F32),
+                pltpu.SemaphoreType.DMA((2,)),
+            ],
         ),
         out_shape=[
             jax.ShapeDtypeStruct((total, width), BF),
@@ -603,7 +620,7 @@
         gb1_ref[...] = jnp.zeros_like(gb1_ref)
 
         def chunk(r, _):
-            rows = rows_of(r)
+            rows = pl.ds(pl.multiple_of(r * SPAN, SPAN), SPAN)
             value, slope = gelu_parts(mm(act[rows, :], w1_ref[...]) + b1_ref[...])
             hidden = value.astype(BF)
             hid[rows, :] = hidden
@@ -614,7 +631,7 @@
             da[rows, :] += mm_t(grad, w1_ref[...])
             return 0
 
-        lax.fori_loop(0, blocks, chunk, 0)
+        lax.fori_loop(0, total // SPAN, chunk, 0)
         grad_two = t_mm(hid[...], dy[...])
         grad_one = t_mm(act[...], dpre[...])
 
@@ -1015,8 +1032,9 @@
     else:
         plane_terms = [net.plane_sum(jnp.stack(pairs)[None])[0]]
     plane_small = net.spread(per_tree)
-    plane_terms, plane_small, grads_rows, rest_line = lax.optimization_barrier(
-        (plane_terms, plane_small, grads_rows, rest_line)
+    out = net.lay_out(out_keep, out_got)
+    plane_terms, plane_small, grads_rows, rest_line, out = lax.optimization_barrier(
+        (plane_terms, plane_small, grads_rows, rest_line, out)
     )
 
     line_terms = total(plane_terms).astype(BF).reshape(shards, -1, span)
@@ -1045,7 +1063,6 @@
     everyone = everyone.reshape(shards, -1)[:, :n_line].astype(F32)
     by_tree = everyone[:, : (groups // 2) * mid_part].reshape(shards, groups // 2, mid_part)
     t_out, t_fc1, t_fc2 = unpack(net.where, rest_half, rest_other, width)
-    out = net.lay_out(out_keep, out_got)
     grads_x = net.lay_out(grads_keep, grads_got)
 
     every_dada = by_tree[:, :, : 6 * width].reshape(-1, 6 * width)

time: 467 us -> 462 us (0.989)
  Pallas kernels: 221 us -> 208 us
  waiting for transfers between devices: 82.2 us -> 90.2 us
    pallas_call x1, Pallas kernels: 73.8 us -> 67.8 us  [attn_bwd(): pl.pallas_call(functools.partial(bwd_kernel, near, pp, scale), grid_spec=...]
    reduce_scatter x1, waiting for transfers between devices: 3.82 us -> 8.84 us  [group_sum(): out = lax.psum_scatter(blocks, 'group', scatter_dimension=0, tiled=True)]
    unnamed x100 -> x96, local copies, waits for them, and re-layouts: 11.6 us -> 11.7 us
  transfers between devices with their start and end apart: 45 -> 45, of which waited for: 13 -> 15; matrix products, arithmetic and copies ran while one was open for 13% -> 13% of each run, Pallas kernels for 35% -> 32%
where the time goes in v2:
time: 462 us; the launch traced here: 453 us
  Pallas kernels  208 us (45%)
  waiting for transfers between devices  90.2 us (20%)
  starting transfers between devices  67.5 us (15%)
  local copies, waits for them, and re-layouts  35.8 us (8%)
  other arithmetic  31.7 us (7%)
  between operations  15.3 us (3%)
  matrix products  4.66 us (1%)
    pallas_call x1, Pallas kernels, attn_bwd(): pl.pallas_call(functools.partial(bwd_kernel, near, pp, scale), grid_spec=...  67.8 us
    pallas_call x1, Pallas kernels, middle(): pl.pallas_call(functools.partial(middle_kernel, shards), grid_spec=pltpu....  56.2 us
    pallas_call x1, Pallas kernels, attn_fwd(): pl.pallas_call(functools.partial(fwd_kernel, near, pp, scale), grid_spec=...  41.8 us
    ppermute x15, waiting for transfers between devices, across(): lax.ppermute(value, 'group', [(i, i ^ 2 * step) for i in range(self.group...  35.8 us
    ppermute x12, waiting for transfers between devices, turn(): return lax.ppermute(value, 'shard', [(i, (i + step) % n) for i in range(n)])  19.9 us
    all_to_all x2, waiting for transfers between devices, exchange(): return lax.all_to_all(by_tree, 'shard', 0, 0).reshape(-1, by_tree.shape[-1])  19 us
    pallas_call x1, Pallas kernels, leave(): pl.pallas_call(functools.partial(leave_kernel, spots), grid_spec=pltpu.Pr...  19 us
    ppermute x12, starting transfers between devices, turn(): return lax.ppermute(value, 'shard', [(i, (i + step) % n) for i in range(n)])  17.6 us
  transfers between devices with their start and end apart: 45, of which 15 were waited for; matrix products, arithmetic and copies ran while one was open for 13% of the time, Pallas kernels for 32%

profile of v2, /device:TPU:1, one launch (start us, length us, event | category | flops | bytes accessed | tf_op | source)
XLA Modules:
  0.0 453.1 jit_solution(10638654622116964098)
XLA Ops:
  7.3 1.3 concatenate.44
  9.6 2.2 collective-permute-start.1
  11.7 2.3 collective-permute-start.2
  15.3 1.6 collective-permute-start.4
  22.3 2.2 collective-permute-done.2
  24.5 1.4 maximum_select_fusion
  26.0 4.9 %all-to-all-start = ((bf16[4,256,768]{2,1,0:T(8,128)(2,1)}), bf16[4,256,768]{2,1,0:T(8,128)(2,1)S(1)}, u32[]{:S(2)}, u32[]{:S(2)}) async-start(bf16[4,256,768]{2,1,0:T(8,128)(2,1)} %bitcast.18), calls=%async_computation | async-start | bytes 3145728 | tf_op jit(solution)/shard_map/all_to_all | solution.py:780
  31.0 1.3 constant_dynamic-slice_fusion.11
  33.3 1.3 collective-permute-start.5
  34.6 1.2 collective-permute-start.6
  36.4 9.2 %collective-permute-done.5 = bf16[3,24,3072]{2,1,0:T(8,128)(2,1)S(1)} collective-permute-done((bf16[3,24,3072]{2,1,0:T(8,128)(2,1)S(1)}, bf16[3,24,3072]{2,1,0:T(8,128)(2,1)S(1)}, u32[]{:S(2)}, u32[]{:S(2)}) %collective-permute-start.5) | collective-permute-done | bytes 442400 | tf_op jit(solution)/shard_map/ppermute | solution.py:768
  45.7 3.8 collective-permute-done.6
  49.5 6.7 %collective-permute-done.7 = bf16[3,24,3072]{2,1,0:T(8,128)(2,1)} collective-permute-done((bf16[3,24,3072]{2,1,0:T(8,128)(2,1)S(1)}, bf16[3,24,3072]{2,1,0:T(8,128)(2,1)}, u32[]{:S(2)}, u32[]{:S(2)}) %collective-permute-start.7) | collective-permute-done | bytes 442400 | tf_op jit(solution)/shard_map/ppermute | solution.py:768
  56.1 18.2 %all-to-all-done = bf16[4,256,768]{2,1,0:T(8,128)(2,1)S(1)} async-done(((bf16[4,256,768]{2,1,0:T(8,128)(2,1)}), bf16[4,256,768]{2,1,0:T(8,128)(2,1)S(1)}, u32[]{:S(2)}, u32[]{:S(2)}) %all-to-all-start) | async-done | bytes 1572896 | tf_op jit(solution)/shard_map/all_to_all | solution.py:780
  74.4 2.2 pad_maximum_fusion.half_ref
  76.7 1.6 collective-permute-start.11
  78.3 1.1 pad_maximum_fusion.1.own_ref
  79.5 2.2 collective-permute-start.8
  81.7 3.9 collective-permute-start.9
  89.6 3.3 maximum_select_fusion.1
  92.8 5.9 %assemble.1 = bf16[32,24,3072]{2,1,0:T(8,128)(2,1)} custom-call(s32[3]{0:T(128)} %pad_add_fusion.where, bf16[8,24,3072]{2,1,0:T(8,128)(2,1)} %pad_maximum_fusion.1.own_ref, bf16[4,3,24,3072]{3,2,1,0:T(8,128)(2,1)} %copy-done.5, bf16[4,3,24,3072]{3,2,1,0:T(8,128)(2,1)} %collective-permute-done.11.other_ref), custom_call_target="tpu_custom_call" | custom-call | tf_op jit(solution)/shard_map/assemble/pallas_call | solution.py:310
  98.7 10.5 %entry.1 = (bf16[1024,768]{1,0:T(8,128)(2,1)S(1)}, bf16[1024,768]{1,0:T(8,128)(2,1)S(1)}, bf16[1024,1536]{1,0:T(8,128)(2,1)}, f32[8,768]{1,0:T(8,128)S(1)}) custom-call(bf16[1024,768]{1,0:T(8,128)(2,1)S(1)} %bitcast.140, f32[8,768]{1,0:T(8,128)S(1)} %stack.238.vec_ref, bf16[768,3072]{1,0:T(8,128)(2,1)} %bitcast.144), custom_call_target="tpu_custom_call" | custom-call | flops 10350000128 | bytes 1048576 | tf_op jit(solution)/shard_map/entry/pallas_call | solution.py:359
  109.2 1.2 copy-done.3
  110.4 1.1 copy-done.4
  118.2 3.6 all-to-all-start.1
  122.6 41.8 %attn_forward.1 = (bf16[1024,768]{1,0:T(8,128)(2,1)}, f32[6,4,1,512]{3,2,1,0:T(1,128)}) custom-call(s32[16]{0:T(128)} %reshape.333.flags, f32[1]{0:T(128)} %bitcast.30.peak_ref, bf16[1024,768]{1,0:T(8,128)(2,1)} %copy-done.4, bf16[1024,1536]{1,0:T(8,128)(2,1)} %get-tuple-element.111.kn_ref.vn_ref, bf16[1024,1536]{1,0:T(8,128)(2,1)} %get-tuple-element.111.kn_ref.vn_ref, ...), custom_call_target="tpu_custom_call" | custom-call | flops 43699998720 | bytes 1048576 | tf_op jit(solution)/shard_map/attn_forward/pallas_call | solution.py:148
  166.3 56.2 %middle.1 = (bf16[1024,768]{1,0:T(8,128)(2,1)}, bf16[1024,768]{1,0:T(8,128)(2,1)}, f32[1024,768]{1,0:T(8,128)}, bf16[8,4,24,6912]{3,2,1,0:T(8,128)(2,1)}, f32[8,768]{1,0:T(8,128)}, /*index=5*/f32[1,3072]{1,0:T(1,128)}) custom-call(s32[3]{0:T(128)} %pad_add_fusion.where, bf16[1024,768]{1,0:T(8,128)(2,1)} %get-tuple-element.112.attn_ref.o_ref, ...), custom_call_target="tpu_custom_call" | custom-call | flops 63250001920 | bytes 1048576 | tf_op jit(solution)/shard_map/middle/pallas_call | solution.py:703
  222.5 6.5 %all-to-all-start.2 = ((bf16[4,256,768]{2,1,0:T(8,128)(2,1)}), bf16[4,256,768]{2,1,0:T(8,128)(2,1)S(1)}, u32[]{:S(2)}, u32[]{:S(2)}) async-start(bf16[4,256,768]{2,1,0:T(8,128)(2,1)} %bitcast.37), calls=%async_computation.3 | async-start | bytes 3145728 | tf_op jit(solution)/shard_map/all_to_all | solution.py:788
  229.0 67.8 %attn_backward.1 = (bf16[1024,768]{1,0:T(8,128)(2,1)}, bf16[2,1024,768]{2,1,0:T(8,128)(2,1)}, bf16[2,1024,768]{2,1,0:T(8,128)(2,1)}) custom-call(s32[16]{0:T(128)} %reshape.333.flags, f32[1]{0:T(128)} %bitcast.30.peak_ref, bf16[1024,768]{1,0:T(8,128)(2,1)} %copy-done.4, bf16[1024,1536]{1,0:T(8,128)(2,1)} %get-tuple-element.111.kn_ref.vn_ref, ...), custom_call_target="tpu_custom_call" | custom-call | flops 72449998848 | bytes 1048576 | tf_op jit(solution)/shard_map/attn_backward/pallas_call | solution.py:257
  297.6 8.8 %reduce-scatter.2.cloned.1.call-done = bf16[96,6912]{1,0:T(8,128)(2,1)} async-done(((bf16[768,6912]{1,0:T(8,128)(2,1)}), bf16[96,6912]{1,0:T(8,128)(2,1)}) %reduce-scatter.2.cloned.1.call-update) | async-done | bytes 1327120 | tf_op jit(solution)/shard_map/reduce_scatter | solution.py:825
  307.9 1.2 collective-permute-start.14
  309.1 2.1 collective-permute-start.15
  311.3 1.2 collective-permute-start.16
  312.4 19.0 %leave.1 = (bf16[1024,768]{1,0:T(8,128)(2,1)}, bf16[4,4,24,2304]{3,2,1,0:T(8,128)(2,1)}, bf16[4,4,24,2304]{3,2,1,0:T(8,128)(2,1)}, f32[8,768]{1,0:T(8,128)}) custom-call(s32[3]{0:T(128)} %pad_add_fusion.where, bf16[1024,768]{1,0:T(8,128)(2,1)} %get-tuple-element.122.dq_ref, bf16[2,1024,768]{2,1,0:T(8,128)(2,1)} %get-tuple-element.123.near_ref, ...), custom_call_target="tpu_custom_call" | custom-call | flops 16099999744 | bytes 1048576 | tf_op jit(solution)/shard_map/leave/pallas_call | solution.py:453
  331.4 2.3 collective-permute-done.15
  336.4 9.5 %all-to-all-start.3 = ((bf16[4,256,768]{2,1,0:T(8,128)(2,1)}), bf16[4,256,768]{2,1,0:T(8,128)(2,1)S(1)}, u32[]{:S(2)}, u32[]{:S(2)}) async-start(bf16[4,256,768]{2,1,0:T(8,128)(2,1)} %bitcast.157), calls=%async_computation.4 | async-start | bytes 3145728 | tf_op jit(solution)/shard_map/all_to_all | solution.py:788
  345.8 1.3 fusion.5
  347.1 3.3 add_convert_fusion.1
  351.9 1.2 collective-permute-start.23
  355.6 16.1 %collective-permute-done.24 = bf16[10240]{0:T(1024)(128)(2,1)S(1)} collective-permute-done((bf16[10240]{0:T(1024)(128)(2,1)S(1)}, bf16[10240]{0:T(1024)(128)(2,1)S(1)}, u32[]{:S(2)}, u32[]{:S(2)}) %collective-permute-start.24) | collective-permute-done | bytes 20512 | tf_op jit(solution)/shard_map/ppermute | solution.py:768
  371.6 1.2 collective-permute-start.26
  372.8 2.9 maximum_select_fusion.2
  375.7 6.6 %all-to-all-done.3 = bf16[4,256,768]{2,1,0:T(8,128)(2,1)S(1)} async-done(((bf16[4,256,768]{2,1,0:T(8,128)(2,1)}), bf16[4,256,768]{2,1,0:T(8,128)(2,1)S(1)}, u32[]{:S(2)}, u32[]{:S(2)}) %all-to-all-start.3) | async-done | bytes 1572896 | tf_op jit(solution)/shard_map/all_to_all | solution.py:788
  383.1 1.3 constant_dynamic-slice_fusion.8
  384.4 1.4 collective-permute-start.33
  385.9 1.5 add_convert_fusion
  388.2 1.5 collective-permute-start.28
  391.1 5.2 %collective-permute-done.27 = bf16[40,2304]{1,0:T(8,128)(2,1)S(1)} collective-permute-done((bf16[40,2304]{1,0:T(8,128)(2,1)S(1)}, bf16[40,2304]{1,0:T(8,128)(2,1)S(1)}, u32[]{:S(2)}, u32[]{:S(2)}) %collective-permute-start.27) | collective-permute-done | bytes 184352 | tf_op jit(solution)/shard_map/ppermute | solution.py:765
  396.3 1.2 collective-permute-start.32
  397.5 5.8 %collective-permute-done.28 = bf16[40,2304]{1,0:T(8,128)(2,1)S(1)} collective-permute-done((bf16[40,2304]{1,0:T(8,128)(2,1)S(1)}, bf16[40,2304]{1,0:T(8,128)(2,1)S(1)}, u32[]{:S(2)}, u32[]{:S(2)}) %collective-permute-start.28) | collective-permute-done | bytes 184352 | tf_op jit(solution)/shard_map/ppermute | solution.py:765
  403.9 1.3 slice.253
  405.3 1.8 reshape.324
  407.2 2.5 collective-permute-done.29
  414.1 1.2 collective-permute-start.36
  416.6 2.6 collective-permute-start.38
  419.2 2.0 fusion.20
  425.4 1.4 reshape.322
  426.8 1.8 reshape.332
  428.5 1.3 dynamic_slice.164
  429.9 1.3 dynamic_slice.167
  432.5 1.5 dynamic-slice_reduce_fusion
  434.9 3.4 maximum_select_fusion.3
  439.3 1.9 settle.1
  441.1 4.9 %unpack.1 = (f32[8,24,768]{2,1,0:T(8,128)}, f32[8,24,3072]{2,1,0:T(8,128)}, f32[8,4,24,768]{3,2,1,0:T(8,128)}) custom-call(s32[3]{0:T(128)S(1)} %copy-done.2, bf16[4,24,6912]{2,1,0:T(8,128)(2,1)S(1)} %pad_maximum_fusion.2.half_ref, bf16[4,24,6912]{2,1,0:T(8,128)(2,1)S(1)} %collective-permute-done.38.other_ref), custom_call_target="tpu_custom_call" | custom-call | flops 4600000000 | bytes 1048576 | tf_op jit(solution)/shard_map/unpack/pallas_call | solution.py:541
  (268 shorter events, 48.3 us)
Async XLA Ops:
  7.2 7.9 %copy-start.11 = (bf16[2,1,512,768]{3,2,1,0:T(8,128)(2,1)S(1)}, bf16[2,1,512,768]{3,2,1,0:T(8,128)(2,1)}, u32[]{:S(2)}) copy-start(bf16[2,1,512,768]{3,2,1,0:T(8,128)(2,1)} %param.17) | copy-start | bytes 4718596
  7.2 158.0 %all-gather.2.cloned.1.call-start = ((), (), s32[]{:S(2)}) async-start(), calls=%async_computation.5 | async-start | bytes 10948608 | tf_op jit(solution)/shard_map/all_gather | solution.py:818
  8.5 6.6 %copy-start.8 = (bf16[8,24,768]{2,1,0:T(8,128)(2,1)}, bf16[8,24,768]{2,1,0:T(8,128)(2,1)S(1)}, u32[]{:S(2)}) copy-start(bf16[8,24,768]{2,1,0:T(8,128)(2,1)S(1)} %concatenate.44) | copy-start | bytes 884740
  9.6 12.8 %collective-permute-start.1 = (bf16[24,3072]{1,0:T(8,128)(2,1)S(1)}, bf16[24,3072]{1,0:T(8,128)(2,1)S(1)}, u32[]{:S(2)}, u32[]{:S(2)}) collective-permute-start(bf16[24,3072]{1,0:T(8,128)(2,1)S(1)} %fusion.11), channel_id=1, source_target_pairs={{0,1},{1,2},{2,3},{3,0},{4,5},{5,6},{6,7},{7,4},{8,9},{9,10},{10,1... | collective-permute-start | bytes 442376 | tf_op jit(solution)/shard_map/ppermute | solution.py:765
  11.7 12.8 %collective-permute-start.2 = (bf16[24,3072]{1,0:T(8,128)(2,1)S(1)}, bf16[24,3072]{1,0:T(8,128)(2,1)}, u32[]{:S(2)}, u32[]{:S(2)}) collective-permute-start(bf16[24,3072]{1,0:T(8,128)(2,1)S(1)} %fusion.11), channel_id=1, source_target_pairs={{0,2},{1,3},{2,0},{3,1},{4,6},{5,7},{6,4},{7,5},{8,10},{9,11},{10,... | collective-permute-start | bytes 442376 | tf_op jit(solution)/shard_map/ppermute | solution.py:765
  14.0 10.5 %collective-permute-start.3 = (bf16[24,3072]{1,0:T(8,128)(2,1)S(1)}, bf16[24,3072]{1,0:T(8,128)(2,1)}, u32[]{:S(2)}, u32[]{:S(2)}) collective-permute-start(bf16[24,3072]{1,0:T(8,128)(2,1)S(1)} %fusion.11), channel_id=1, source_target_pairs={{0,3},{1,0},{2,1},{3,2},{4,7},{5,4},{6,5},{7,6},{8,11},{9,8},{10,9... | collective-permute-start | bytes 442376 | tf_op jit(solution)/shard_map/ppermute | solution.py:765
  15.3 9.2 %collective-permute-start.4 = (bf16[2,256,768]{2,1,0:T(8,128)(2,1)S(1)}, bf16[2,256,768]{2,1,0:T(8,128)(2,1)S(1)}, u32[]{:S(2)}, u32[]{:S(2)}) collective-permute-start(bf16[2,256,768]{2,1,0:T(8,128)(2,1)S(1)} %get-tuple-element.233), channel_id=1, source_target_pairs={{0,4},{4,0},{8,12},{12,8},{16,20},{20,16},{24,28},{28,24},{1,5},{5... | collective-permute-start | bytes 2359304 | tf_op jit(solution)/shard_map/ppermute | solution.py:761
  17.0 5.3 %collective-permute-start = (f32[2,2189]{1,0:T(2,128)S(1)}, f32[2,2189]{1,0:T(2,128)S(1)}, u32[]{:S(2)}, u32[]{:S(2)}) collective-permute-start(f32[2,2189]{1,0:T(2,128)S(1)} %concatenate.42), channel_id=1, source_target_pairs={{0,4},{4,0},{8,12},{12,8},{16,20},{20,16},{24,28},{28,24},{1,5},{5... | collective-permute-start | bytes 52544 | tf_op jit(solution)/shard_map/ppermute | solution.py:761
  25.9 4.9 %copy-start.39 = (bf16[192]{0:T(256)(128)(2,1)S(1)}, bf16[192]{0:T(256)(128)(2,1)}, u32[]{:S(2)}) copy-start(bf16[192]{0:T(256)(128)(2,1)} %param.27) | copy-start | bytes 1156
  25.9 4.9 %copy-start.40 = (bf16[192]{0:T(256)(128)(2,1)S(1)}, bf16[192]{0:T(256)(128)(2,1)}, u32[]{:S(2)}) copy-start(bf16[192]{0:T(256)(128)(2,1)} %param.30) | copy-start | bytes 1156
  25.9 4.9 %copy-start.41 = (bf16[192]{0:T(256)(128)(2,1)S(1)}, bf16[192]{0:T(256)(128)(2,1)}, u32[]{:S(2)}) copy-start(bf16[192]{0:T(256)(128)(2,1)} %param.31) | copy-start | bytes 1156
  26.0 5.0 %copy-start.12 = (bf16[2,1,512,768]{3,2,1,0:T(8,128)(2,1)S(1)}, bf16[2,1,512,768]{3,2,1,0:T(8,128)(2,1)}, u32[]{:S(2)}) copy-start(bf16[2,1,512,768]{3,2,1,0:T(8,128)(2,1)} %param.21) | copy-start | bytes 4718596
  26.0 48.4 %all-to-all-start = ((bf16[4,256,768]{2,1,0:T(8,128)(2,1)}), bf16[4,256,768]{2,1,0:T(8,128)(2,1)S(1)}, u32[]{:S(2)}, u32[]{:S(2)}) async-start(bf16[4,256,768]{2,1,0:T(8,128)(2,1)} %bitcast.18), calls=%async_computation | async-start | bytes 3145728 | tf_op jit(solution)/shard_map/all_to_all | solution.py:780
  31.0 5.1 %copy-start.17 = (bf16[128,1152]{1,0:T(8,128)(2,1)S(1)}, bf16[128,1152]{1,0:T(8,128)(2,1)}, u32[]{:S(2)}) copy-start(bf16[128,1152]{1,0:T(8,128)(2,1)} %param.28) | copy-start | bytes 884740
  33.3 41.1 %copy-start.10 = (bf16[3,24,3072]{2,1,0:T(8,128)(2,1)}, bf16[3,24,3072]{2,1,0:T(8,128)(2,1)S(1)}, u32[]{:S(2)}) copy-start(bf16[3,24,3072]{2,1,0:T(8,128)(2,1)S(1)} %pad_maximum_fusion.3) | copy-start | bytes 1327108
  33.3 12.4 %collective-permute-start.5 = (bf16[3,24,3072]{2,1,0:T(8,128)(2,1)S(1)}, bf16[3,24,3072]{2,1,0:T(8,128)(2,1)S(1)}, u32[]{:S(2)}, u32[]{:S(2)}) collective-permute-start(bf16[3,24,3072]{2,1,0:T(8,128)(2,1)S(1)} %pad_maximum_fusion.3), channel_id=1, source_target_pairs={{0,8},{4,12},{8,0},{12,4},{16,24},{20,28},{24,16},{28,20},{1,9},{5... | collective-permute-start | bytes 1327112 | tf_op jit(solution)/shard_map/ppermute | solution.py:768
  34.6 14.9 %collective-permute-start.6 = (bf16[3,24,3072]{2,1,0:T(8,128)(2,1)S(1)}, bf16[3,24,3072]{2,1,0:T(8,128)(2,1)S(1)}, u32[]{:S(2)}, u32[]{:S(2)}) collective-permute-start(bf16[3,24,3072]{2,1,0:T(8,128)(2,1)S(1)} %pad_maximum_fusion.3), channel_id=1, source_target_pairs={{0,16},{4,20},{8,24},{12,28},{16,0},{20,4},{24,8},{28,12},{1,17},{... | collective-permute-start | bytes 1327112 | tf_op jit(solution)/shard_map/ppermute | solution.py:768
  35.8 20.3 %collective-permute-start.7 = (bf16[3,24,3072]{2,1,0:T(8,128)(2,1)S(1)}, bf16[3,24,3072]{2,1,0:T(8,128)(2,1)}, u32[]{:S(2)}, u32[]{:S(2)}) collective-permute-start(bf16[3,24,3072]{2,1,0:T(8,128)(2,1)S(1)} %pad_maximum_fusion.3), channel_id=1, source_target_pairs={{0,24},{4,28},{8,16},{12,20},{16,8},{20,12},{24,0},{28,4},{1,25},{... | collective-permute-start | bytes 1327112 | tf_op jit(solution)/shard_map/ppermute | solution.py:768
  36.1 76.4 %copy-start.31 = (f32[4,2189]{1,0:T(4,128)}, f32[4,2189]{1,0:T(4,128)S(1)}, u32[]{:S(2)}) copy-start(f32[4,2189]{1,0:T(4,128)S(1)} %select_n.209) | copy-start | bytes 105076
  45.7 28.7 %copy-start.21 = (bf16[3,24,3072]{2,1,0:T(8,128)(2,1)}, bf16[3,24,3072]{2,1,0:T(8,128)(2,1)S(1)}, u32[]{:S(2)}) copy-start(bf16[3,24,3072]{2,1,0:T(8,128)(2,1)S(1)} %collective-permute-done.5) | copy-start | bytes 1327108
  49.5 24.9 %copy-start.22 = (bf16[3,24,3072]{2,1,0:T(8,128)(2,1)}, bf16[3,24,3072]{2,1,0:T(8,128)(2,1)S(1)}, u32[]{:S(2)}) copy-start(bf16[3,24,3072]{2,1,0:T(8,128)(2,1)S(1)} %collective-permute-done.6) | copy-start | bytes 1327108
  74.4 24.3 %copy-start = (bf16[4,256,768]{2,1,0:T(8,128)(2,1)}, bf16[4,256,768]{2,1,0:T(8,128)(2,1)S(1)}, u32[]{:S(2)}) copy-start(bf16[4,256,768]{2,1,0:T(8,128)(2,1)S(1)} %all-to-all-done) | copy-start | bytes 4718596
  76.7 12.7 %copy-start.5 = (bf16[4,3,24,3072]{3,2,1,0:T(8,128)(2,1)}, bf16[4,3,24,3072]{3,2,1,0:T(8,128)(2,1)S(1)}, u32[]{:S(2)}) copy-start(bf16[4,3,24,3072]{3,2,1,0:T(8,128)(2,1)S(1)} %pad_maximum_fusion.half_ref) | copy-start | bytes 5308420
  76.7 16.2 %collective-permute-start.11 = (bf16[4,3,24,3072]{3,2,1,0:T(8,128)(2,1)S(1)}, bf16[4,3,24,3072]{3,2,1,0:T(8,128)(2,1)}, u32[]{:S(2)}, u32[]{:S(2)}) collective-permute-start(bf16[4,3,24,3072]{3,2,1,0:T(8,128)(2,1)S(1)} %pad_maximum_fusion.half_ref), channel_id=1, source_target_pairs={{0,4},{4,0},{8,12},{12,8},{16,20},{20,16},{24,28},{28,24},{1,5},{5... | collective-permute-start | bytes 5308424 | tf_op jit(solution)/shard_map/ppermute | solution.py:761
  79.5 7.5 %collective-permute-start.8 = (f32[2496]{0:T(1024)S(1)}, f32[2496]{0:T(1024)S(1)}, u32[]{:S(2)}, u32[]{:S(2)}) collective-permute-start(f32[2496]{0:T(1024)S(1)} %get-tuple-element.219), channel_id=1, source_target_pairs={{0,1},{1,2},{2,3},{3,0},{4,5},{5,6},{6,7},{7,4},{8,9},{9,10},{10,1... | collective-permute-start | bytes 29960 | tf_op jit(solution)/shard_map/ppermute | solution.py:765
  81.7 6.3 %collective-permute-start.9 = (f32[2496]{0:T(1024)S(1)}, f32[2496]{0:T(1024)S(1)}, u32[]{:S(2)}, u32[]{:S(2)}) collective-permute-start(f32[2496]{0:T(1024)S(1)} %get-tuple-element.221), channel_id=1, source_target_pairs={{0,2},{1,3},{2,0},{3,1},{4,6},{5,7},{6,4},{7,5},{8,10},{9,11},{10,... | collective-permute-start | bytes 29960 | tf_op jit(solution)/shard_map/ppermute | solution.py:765
  85.6 3.5 collective-permute-start.10
  86.2 3.3 collective-permute-start.12
  89.5 9.2 %copy-start.1 = (f32[8,768]{1,0:T(8,128)}, f32[8,768]{1,0:T(8,128)S(1)}, u32[]{:S(2)}) copy-start(f32[8,768]{1,0:T(8,128)S(1)} %stack.238.vec_ref) | copy-start | bytes 73732
  111.6 11.0 %collective-permute-start.13 = (bf16[1024,1536]{1,0:T(8,128)(2,1)}, bf16[1024,1536]{1,0:T(8,128)(2,1)}, u32[]{:S(2)}, u32[]{:S(2)}) collective-permute-start(bf16[1024,1536]{1,0:T(8,128)(2,1)} %get-tuple-element.111.kn_ref.vn_ref), channel_id=1, source_target_pairs={{0,4},{4,0},{8,12},{12,8},{16,20},{20,16},{24,28},{28,24},{1,5},{5... | collective-permute-start | bytes 9437192 | tf_op jit(solution)/shard_map/ppermute | solution.py:761
  118.2 47.0 %all-to-all-start.1 = ((bf16[4,256,768]{2,1,0:T(8,128)(2,1)}), bf16[4,256,768]{2,1,0:T(8,128)(2,1)S(1)}, u32[]{:S(2)}, u32[]{:S(2)}) async-start(bf16[4,256,768]{2,1,0:T(8,128)(2,1)} %bitcast.32), calls=%async_computation.1 | async-start | bytes 3145728 | tf_op jit(solution)/shard_map/all_to_all | solution.py:780
  121.7 184.8 %reduce-scatter.2.cloned.1.call-start = ((), (), s32[]{:S(2)}) async-start(), calls=%async_computation.6 | async-start | bytes 11943936 | tf_op jit(solution)/shard_map/reduce_scatter | solution.py:825
  222.5 75.1 %all-to-all-start.2 = ((bf16[4,256,768]{2,1,0:T(8,128)(2,1)}), bf16[4,256,768]{2,1,0:T(8,128)(2,1)S(1)}, u32[]{:S(2)}, u32[]{:S(2)}) async-start(bf16[4,256,768]{2,1,0:T(8,128)(2,1)} %bitcast.37), calls=%async_computation.3 | async-start | bytes 3145728 | tf_op jit(solution)/shard_map/all_to_all | solution.py:788
  296.8 15.6 %collective-permute-start.18 = (bf16[2,1024,768]{2,1,0:T(8,128)(2,1)}, bf16[2,1024,768]{2,1,0:T(8,128)(2,1)}, u32[]{:S(2)}, u32[]{:S(2)}) collective-permute-start(bf16[2,1024,768]{2,1,0:T(8,128)(2,1)} %get-tuple-element.124), channel_id=1, source_target_pairs={{0,4},{4,0},{8,12},{12,8},{16,20},{20,16},{24,28},{28,24},{1,5},{5... | collective-permute-start | bytes 9437192 | tf_op jit(solution)/shard_map/ppermute | solution.py:761
  306.6 27.1 %collective-permute-start.17 = (bf16[2,256,768]{2,1,0:T(8,128)(2,1)S(1)}, bf16[2,256,768]{2,1,0:T(8,128)(2,1)S(1)}, u32[]{:S(2)}, u32[]{:S(2)}) collective-permute-start(bf16[2,256,768]{2,1,0:T(8,128)(2,1)S(1)} %get-tuple-element.229), channel_id=1, source_target_pairs={{0,4},{4,0},{8,12},{12,8},{16,20},{20,16},{24,28},{28,24},{1,5},{5... | collective-permute-start | bytes 2359304 | tf_op jit(solution)/shard_map/ppermute | solution.py:761
  307.9 23.5 %collective-permute-start.14 = (bf16[24,6912]{1,0:T(8,128)(2,1)S(1)}, bf16[24,6912]{1,0:T(8,128)(2,1)S(1)}, u32[]{:S(2)}, u32[]{:S(2)}) collective-permute-start(bf16[24,6912]{1,0:T(8,128)(2,1)S(1)} %get-tuple-element.236), channel_id=1, source_target_pairs={{0,1},{1,2},{2,3},{3,0},{4,5},{5,6},{6,7},{7,4},{8,9},{9,10},{10,1... | collective-permute-start | bytes 995336 | tf_op jit(solution)/shard_map/ppermute | solution.py:765
  309.1 24.6 %collective-permute-start.15 = (bf16[24,6912]{1,0:T(8,128)(2,1)S(1)}, bf16[24,6912]{1,0:T(8,128)(2,1)S(1)}, u32[]{:S(2)}, u32[]{:S(2)}) collective-permute-start(bf16[24,6912]{1,0:T(8,128)(2,1)S(1)} %get-tuple-element.235), channel_id=1, source_target_pairs={{0,2},{1,3},{2,0},{3,1},{4,6},{5,7},{6,4},{7,5},{8,10},{9,11},{10,... | collective-permute-start | bytes 995336 | tf_op jit(solution)/shard_map/ppermute | solution.py:765
  311.3 22.5 %collective-permute-start.16 = (bf16[24,6912]{1,0:T(8,128)(2,1)S(1)}, bf16[24,6912]{1,0:T(8,128)(2,1)S(1)}, u32[]{:S(2)}, u32[]{:S(2)}) collective-permute-start(bf16[24,6912]{1,0:T(8,128)(2,1)S(1)} %get-tuple-element.234), channel_id=1, source_target_pairs={{0,3},{1,0},{2,1},{3,2},{4,7},{5,4},{6,5},{7,6},{8,11},{9,8},{10,9... | collective-permute-start | bytes 995336 | tf_op jit(solution)/shard_map/ppermute | solution.py:765
  312.4 22.8 %copy-start.32 = (f32[8,768]{1,0:T(8,128)S(1)}, f32[8,768]{1,0:T(8,128)}, u32[]{:S(2)}) copy-start(f32[8,768]{1,0:T(8,128)} %get-tuple-element.134) | copy-start | bytes 73732
  312.4 22.8 %copy-start.34 = (f32[1,3072]{1,0:T(1,128)S(1)}, f32[1,3072]{1,0:T(1,128)}, u32[]{:S(2)}) copy-start(f32[1,3072]{1,0:T(1,128)} %get-tuple-element.135) | copy-start | bytes 36868
  334.6 12.5 %collective-permute-start.19 = (bf16[4,4,24,2304]{3,2,1,0:T(8,128)(2,1)}, bf16[4,4,24,2304]{3,2,1,0:T(8,128)(2,1)}, u32[]{:S(2)}, u32[]{:S(2)}) collective-permute-start(bf16[4,4,24,2304]{3,2,1,0:T(8,128)(2,1)} %get-tuple-element.132), channel_id=1, source_target_pairs={{0,4},{4,0},{8,12},{12,8},{16,20},{20,16},{24,28},{28,24},{1,5},{5... | collective-permute-start | bytes 5308424 | tf_op jit(solution)/shard_map/ppermute | solution.py:761
  336.3 10.8 %collective-permute-start.20 = (bf16[13,768]{1,0:T(8,128)(2,1)S(1)}, bf16[13,768]{1,0:T(8,128)(2,1)S(1)}, u32[]{:S(2)}, u32[]{:S(2)}) collective-permute-start(bf16[13,768]{1,0:T(8,128)(2,1)S(1)} %concatenate.49), channel_id=1, source_target_pairs={{0,4},{4,0},{8,12},{12,8},{16,20},{20,16},{24,28},{28,24},{1,5},{5... | collective-permute-start | bytes 59912 | tf_op jit(solution)/shard_map/ppermute | solution.py:761
  336.4 46.0 %all-to-all-start.3 = ((bf16[4,256,768]{2,1,0:T(8,128)(2,1)}), bf16[4,256,768]{2,1,0:T(8,128)(2,1)S(1)}, u32[]{:S(2)}, u32[]{:S(2)}) async-start(bf16[4,256,768]{2,1,0:T(8,128)(2,1)} %bitcast.157), calls=%async_computation.4 | async-start | bytes 3145728 | tf_op jit(solution)/shard_map/all_to_all | solution.py:788
  350.4 25.3 %collective-permute-start.21 = (bf16[96,2304]{1,0:T(8,128)(2,1)}, bf16[96,2304]{1,0:T(8,128)(2,1)}, u32[]{:S(2)}, u32[]{:S(2)}) collective-permute-start(bf16[96,2304]{1,0:T(8,128)(2,1)} %bitcast.46), channel_id=1, source_target_pairs={{0,8},{4,12},{8,0},{12,4},{16,24},{20,28},{24,16},{28,20},{1,9},{5... | collective-permute-start | bytes 1327112 | tf_op jit(solution)/shard_map/ppermute | solution.py:768
  351.4 24.3 %collective-permute-start.22 = (bf16[96,2304]{1,0:T(8,128)(2,1)}, bf16[96,2304]{1,0:T(8,128)(2,1)}, u32[]{:S(2)}, u32[]{:S(2)}) collective-permute-start(bf16[96,2304]{1,0:T(8,128)(2,1)} %bitcast.47), channel_id=1, source_target_pairs={{0,16},{4,20},{8,24},{12,28},{16,0},{20,4},{24,8},{28,12},{1,17},{... | collective-permute-start | bytes 1327112 | tf_op jit(solution)/shard_map/ppermute | solution.py:768
  351.9 23.9 %collective-permute-start.23 = (bf16[96,2304]{1,0:T(8,128)(2,1)}, bf16[96,2304]{1,0:T(8,128)(2,1)}, u32[]{:S(2)}, u32[]{:S(2)}) collective-permute-start(bf16[96,2304]{1,0:T(8,128)(2,1)} %bitcast.48), channel_id=1, source_target_pairs={{0,24},{4,28},{8,16},{12,20},{16,8},{20,12},{24,0},{28,4},{1,25},{... | collective-permute-start | bytes 1327112 | tf_op jit(solution)/shard_map/ppermute | solution.py:768
  354.0 17.6 %collective-permute-start.24 = (bf16[10240]{0:T(1024)(128)(2,1)S(1)}, bf16[10240]{0:T(1024)(128)(2,1)S(1)}, u32[]{:S(2)}, u32[]{:S(2)}) collective-permute-start(bf16[10240]{0:T(1024)(128)(2,1)S(1)} %dynamic-update-slice.4), channel_id=1, source_target_pairs={{0,8},{4,12},{8,0},{12,4},{16,24},{20,28},{24,16},{28,20},{1,9},{5... | collective-permute-start | bytes 61448 | tf_op jit(solution)/shard_map/ppermute | solution.py:768
  355.1 20.5 %collective-permute-start.25 = (bf16[10240]{0:T(1024)(128)(2,1)S(1)}, bf16[10240]{0:T(1024)(128)(2,1)S(1)}, u32[]{:S(2)}, u32[]{:S(2)}) collective-permute-start(bf16[10240]{0:T(1024)(128)(2,1)S(1)} %dynamic-update-slice.4), channel_id=1, source_target_pairs={{0,16},{4,20},{8,24},{12,28},{16,0},{20,4},{24,8},{28,12},{1,17},{... | collective-permute-start | bytes 61448 | tf_op jit(solution)/shard_map/ppermute | solution.py:768
  371.6 4.1 collective-permute-start.26
  384.4 25.3 %collective-permute-start.33 = (bf16[2,256,768]{2,1,0:T(8,128)(2,1)}, bf16[2,256,768]{2,1,0:T(8,128)(2,1)}, u32[]{:S(2)}, u32[]{:S(2)}) collective-permute-start(bf16[2,256,768]{2,1,0:T(8,128)(2,1)} %get-tuple-element.227), channel_id=1, source_target_pairs={{0,4},{4,0},{8,12},{12,8},{16,20},{20,16},{24,28},{28,24},{1,5},{5... | collective-permute-start | bytes 2359304 | tf_op jit(solution)/shard_map/ppermute | solution.py:761
  388.2 8.1 %collective-permute-start.27 = (bf16[40,2304]{1,0:T(8,128)(2,1)S(1)}, bf16[40,2304]{1,0:T(8,128)(2,1)S(1)}, u32[]{:S(2)}, u32[]{:S(2)}) collective-permute-start(bf16[40,2304]{1,0:T(8,128)(2,1)S(1)} %get-tuple-element.239), channel_id=1, source_target_pairs={{0,1},{1,2},{2,3},{3,0},{4,5},{5,6},{6,7},{7,4},{8,9},{9,10},{10,1... | collective-permute-start | bytes 552968 | tf_op jit(solution)/shard_map/ppermute | solution.py:765
  388.2 15.1 %collective-permute-start.28 = (bf16[40,2304]{1,0:T(8,128)(2,1)S(1)}, bf16[40,2304]{1,0:T(8,128)(2,1)S(1)}, u32[]{:S(2)}, u32[]{:S(2)}) collective-permute-start(bf16[40,2304]{1,0:T(8,128)(2,1)S(1)} %get-tuple-element.238), channel_id=1, source_target_pairs={{0,2},{1,3},{2,0},{3,1},{4,6},{5,7},{6,4},{7,5},{8,10},{9,11},{10,... | collective-permute-start | bytes 552968 | tf_op jit(solution)/shard_map/ppermute | solution.py:765
  389.7 20.0 %collective-permute-start.30 = (bf16[24,6912]{1,0:T(8,128)(2,1)S(1)}, bf16[24,6912]{1,0:T(8,128)(2,1)S(1)}, u32[]{:S(2)}, u32[]{:S(2)}) collective-permute-start(bf16[24,6912]{1,0:T(8,128)(2,1)S(1)} %fusion.5), channel_id=1, source_target_pairs={{0,8},{4,12},{8,0},{12,4},{16,24},{20,28},{24,16},{28,20},{1,9},{5... | collective-permute-start | bytes 995336 | tf_op jit(solution)/shard_map/ppermute | solution.py:768
  390.7 18.9 %collective-permute-start.31 = (bf16[24,6912]{1,0:T(8,128)(2,1)S(1)}, bf16[24,6912]{1,0:T(8,128)(2,1)S(1)}, u32[]{:S(2)}, u32[]{:S(2)}) collective-permute-start(bf16[24,6912]{1,0:T(8,128)(2,1)S(1)} %fusion.5), channel_id=1, source_target_pairs={{0,16},{4,20},{8,24},{12,28},{16,0},{20,4},{24,8},{28,12},{1,17},{... | collective-permute-start | bytes 995336 | tf_op jit(solution)/shard_map/ppermute | solution.py:768
  396.3 13.4 %copy-start.25 = (bf16[40,2304]{1,0:T(8,128)(2,1)}, bf16[40,2304]{1,0:T(8,128)(2,1)S(1)}, u32[]{:S(2)}) copy-start(bf16[40,2304]{1,0:T(8,128)(2,1)S(1)} %collective-permute-done.27) | copy-start | bytes 552964
  396.3 13.3 %collective-permute-start.32 = (bf16[24,6912]{1,0:T(8,128)(2,1)S(1)}, bf16[24,6912]{1,0:T(8,128)(2,1)S(1)}, u32[]{:S(2)}, u32[]{:S(2)}) collective-permute-start(bf16[24,6912]{1,0:T(8,128)(2,1)S(1)} %fusion.5), channel_id=1, source_target_pairs={{0,24},{4,28},{8,16},{12,20},{16,8},{20,12},{24,0},{28,4},{1,25},{... | collective-permute-start | bytes 995336 | tf_op jit(solution)/shard_map/ppermute | solution.py:768
  403.9 5.7 %collective-permute-start.29 = (bf16[40,2304]{1,0:T(8,128)(2,1)}, bf16[40,2304]{1,0:T(8,128)(2,1)}, u32[]{:S(2)}, u32[]{:S(2)}) collective-permute-start(bf16[40,2304]{1,0:T(8,128)(2,1)} %get-tuple-element.237), channel_id=1, source_target_pairs={{0,3},{1,0},{2,1},{3,2},{4,7},{5,4},{6,5},{7,6},{8,11},{9,8},{10,9... | collective-permute-start | bytes 552968 | tf_op jit(solution)/shard_map/ppermute | solution.py:765
  412.6 8.7 %collective-permute-start.34 = (bf16[24,2304]{1,0:T(8,128)(2,1)S(1)}, bf16[24,2304]{1,0:T(8,128)(2,1)S(1)}, u32[]{:S(2)}, u32[]{:S(2)}) collective-permute-start(bf16[24,2304]{1,0:T(8,128)(2,1)S(1)} %add_convert_fusion.5), channel_id=1, source_target_pairs={{0,8},{4,12},{8,0},{12,4},{16,24},{20,28},{24,16},{28,20},{1,9},{5... | collective-permute-start | bytes 331784 | tf_op jit(solution)/shard_map/ppermute | solution.py:768
  413.7 7.6 %collective-permute-start.35 = (bf16[24,2304]{1,0:T(8,128)(2,1)S(1)}, bf16[24,2304]{1,0:T(8,128)(2,1)}, u32[]{:S(2)}, u32[]{:S(2)}) collective-permute-start(bf16[24,2304]{1,0:T(8,128)(2,1)S(1)} %add_convert_fusion.5), channel_id=1, source_target_pairs={{0,16},{4,20},{8,24},{12,28},{16,0},{20,4},{24,8},{28,12},{1,17},{... | collective-permute-start | bytes 331784 | tf_op jit(solution)/shard_map/ppermute | solution.py:768
  414.1 7.2 %collective-permute-start.36 = (bf16[24,2304]{1,0:T(8,128)(2,1)S(1)}, bf16[24,2304]{1,0:T(8,128)(2,1)}, u32[]{:S(2)}, u32[]{:S(2)}) collective-permute-start(bf16[24,2304]{1,0:T(8,128)(2,1)S(1)} %add_convert_fusion.5), channel_id=1, source_target_pairs={{0,24},{4,28},{8,16},{12,20},{16,8},{20,12},{24,0},{28,4},{1,25},{... | collective-permute-start | bytes 331784 | tf_op jit(solution)/shard_map/ppermute | solution.py:768
  416.4 7.4 %copy-start.16 = (f32[4,4,4864]{2,1,0:T(4,128)S(1)}, f32[4,4,4864]{2,1,0:T(4,128)}, u32[]{:S(2)}) copy-start(f32[4,4,4864]{2,1,0:T(4,128)} %copy-done.15) | copy-start | bytes 933892
  416.6 7.9 %copy-start.19 = (bf16[4,4,4608]{2,1,0:T(4,128)(2,1)S(1)}, bf16[4,4,4608]{2,1,0:T(4,128)(2,1)}, u32[]{:S(2)}) copy-start(bf16[4,4,4608]{2,1,0:T(4,128)(2,1)} %copy-done.18) | copy-start | bytes 442372
  416.6 24.5 %collective-permute-start.38 = (bf16[4,24,6912]{2,1,0:T(8,128)(2,1)S(1)}, bf16[4,24,6912]{2,1,0:T(8,128)(2,1)S(1)}, u32[]{:S(2)}, u32[]{:S(2)}) collective-permute-start(bf16[4,24,6912]{2,1,0:T(8,128)(2,1)S(1)} %pad_maximum_fusion.2.half_ref), channel_id=1, source_target_pairs={{0,4},{4,0},{8,12},{12,8},{16,20},{20,16},{24,28},{28,24},{1,5},{5... | collective-permute-start | bytes 3981320 | tf_op jit(solution)/shard_map/ppermute | solution.py:761
  422.3 17.0 %collective-permute-start.37 = (bf16[4,24,2304]{2,1,0:T(8,128)(2,1)S(1)}, bf16[4,24,2304]{2,1,0:T(8,128)(2,1)S(1)}, u32[]{:S(2)}, u32[]{:S(2)}) collective-permute-start(bf16[4,24,2304]{2,1,0:T(8,128)(2,1)S(1)} %pad_maximum_fusion.4.half_ref), channel_id=1, source_target_pairs={{0,4},{4,0},{8,12},{12,8},{16,20},{20,16},{24,28},{28,24},{1,5},{5... | collective-permute-start | bytes 1327112 | tf_op jit(solution)/shard_map/ppermute | solution.py:761
  (23 other events, 50.1 us)
Sparse Core Ops, SparseCore 0:
  24.6 121.1 all-gather.1
  222.6 83.8 reduce-scatter.1

commit v3 on v2

--- a/solution.py
+++ b/solution.py
@@ -430,7 +430,7 @@
             copy.wait()
 
         def finish(r, _):
-            rows = pl.ds(pl.multiple_of(r * BLOCK, BLOCK), BLOCK)
+            rows = pl.ds(pl.multiple_of(r * SPAN, SPAN), SPAN)
             normed, inv = layer_norm(tok_ref[rows, :].astype(F32))
             part = da[rows, :]
             grad_h = part * lift
@@ -440,7 +440,7 @@
                 sums_ref[i : i + 1, :] += jnp.sum(term, axis=0, keepdims=True)
             return 0
 
-        lax.fori_loop(0, total // BLOCK, finish, 0)
+        lax.fori_loop(0, total // SPAN, finish, 0)
 
 
 def leave(where, q_grads, near, far, act, qkv_w, tok, dmid, vec, spots):
@@ -587,11 +587,11 @@
 
     step = pl.program_id(0)
     total = attn_ref.shape[0]
-    blocks = total // BLOCK
+    blocks = total // SPAN
     gate_one, gain, lift, shift, gate_two, fc2_b = (vec_ref[i : i + 1, :] for i in range(6))
 
     def rows_of(r):
-        return pl.ds(pl.multiple_of(r * BLOCK, BLOCK), BLOCK)
+        return pl.ds(pl.multiple_of(r * SPAN, SPAN), SPAN)
 
     @pl.when(step == 0)
     def _():
@@ -606,8 +606,8 @@
             mid[rows, :] = middle
             act[rows, :] = (normed * gain * lift + shift).astype(BF)
             dy[rows, :] = (cot_ref[rows, :].astype(F32) * gate_two).astype(BF)
-            two[rows, :] = jnp.zeros((BLOCK, two.shape[1]), F32)
-            da[rows, :] = jnp.zeros((BLOCK, da.shape[1]), F32)
+            two[rows, :] = jnp.zeros((SPAN, two.shape[1]), F32)
+            da[rows, :] = jnp.zeros((SPAN, da.shape[1]), F32)
             return 0
 
         lax.fori_loop(0, blocks, start, 0)
@@ -620,7 +620,7 @@
         gb1_ref[...] = jnp.zeros_like(gb1_ref)
 
         def chunk(r, _):
-            rows = pl.ds(pl.multiple_of(r * SPAN, SPAN), SPAN)
+            rows = rows_of(r)
             value, slope = gelu_parts(mm(act[rows, :], w1_ref[...]) + b1_ref[...])
             hidden = value.astype(BF)
             hid[rows, :] = hidden
@@ -631,7 +631,7 @@
             da[rows, :] += mm_t(grad, w1_ref[...])
             return 0
 
-        lax.fori_loop(0, total // SPAN, chunk, 0)
+        lax.fori_loop(0, blocks, chunk, 0)
         grad_two = t_mm(hid[...], dy[...])
         grad_one = t_mm(act[...], dpre[...])
 

time: 462 us -> 462 us (level)
  Pallas kernels: 208 us -> 215 us
    pallas_call x1, Pallas kernels: 67.8 us -> 72.5 us  [attn_bwd(): pl.pallas_call(functools.partial(bwd_kernel, near, pp, scale), grid_spec=...]
  transfers between devices with their start and end apart: 45 -> 45, of which waited for: 15 -> 14; matrix products, arithmetic and copies ran while one was open for 13% -> 13% of each run, Pallas kernels for 32% -> 34%
where the time goes in v3:
time: 462 us; the launch traced here: 454 us
  Pallas kernels  215 us (47%)
  waiting for transfers between devices  85.9 us (19%)
  starting transfers between devices  65.8 us (14%)
  local copies, waits for them, and re-layouts  35.9 us (8%)
  other arithmetic  31.7 us (7%)
  between operations  15.6 us (3%)
  matrix products  4.66 us (1%)
    pallas_call x1, Pallas kernels, attn_bwd(): pl.pallas_call(functools.partial(bwd_kernel, near, pp, scale), grid_spec=...  72.5 us
    pallas_call x1, Pallas kernels, middle(): pl.pallas_call(functools.partial(middle_kernel, shards), grid_spec=pltpu....  55.7 us
    pallas_call x1, Pallas kernels, attn_fwd(): pl.pallas_call(functools.partial(fwd_kernel, near, pp, scale), grid_spec=...  44.2 us
    ppermute x15, waiting for transfers between devices, across(): lax.ppermute(value, 'group', [(i, i ^ 2 * step) for i in range(self.group...  35.8 us
    ppermute x12, waiting for transfers between devices, turn(): return lax.ppermute(value, 'shard', [(i, (i + step) % n) for i in range(n)])  19.9 us
    pallas_call x1, Pallas kernels, leave(): pl.pallas_call(functools.partial(leave_kernel, spots), grid_spec=pltpu.Pr...  18.9 us
    all_to_all x2, waiting for transfers between devices, exchange(): return lax.all_to_all(by_tree, 'shard', 0, 0).reshape(-1, by_tree.shape[-1])  18.3 us
    ppermute x12, starting transfers between devices, turn(): return lax.ppermute(value, 'shard', [(i, (i + step) % n) for i in range(n)])  17.6 us
  transfers between devices with their start and end apart: 45, of which 14 were waited for; matrix products, arithmetic and copies ran while one was open for 13% of the time, Pallas kernels for 34%

profile of v3, /device:TPU:1, one launch (start us, length us, event | category | flops | bytes accessed | tf_op | source)
XLA Modules:
  0.0 454.2 jit_solution(10084714111706510959)
XLA Ops:
  7.3 1.3 concatenate.44
  9.6 2.2 collective-permute-start.1
  11.7 2.3 collective-permute-start.2
  15.3 1.6 collective-permute-start.4
  22.3 2.2 collective-permute-done.2
  24.5 1.4 maximum_select_fusion
  26.0 4.9 %all-to-all-start = ((bf16[4,256,768]{2,1,0:T(8,128)(2,1)}), bf16[4,256,768]{2,1,0:T(8,128)(2,1)S(1)}, u32[]{:S(2)}, u32[]{:S(2)}) async-start(bf16[4,256,768]{2,1,0:T(8,128)(2,1)} %bitcast.18), calls=%async_computation | async-start | bytes 3145728 | tf_op jit(solution)/shard_map/all_to_all | solution.py:780
  31.0 1.3 constant_dynamic-slice_fusion.11
  33.3 1.3 collective-permute-start.5
  34.6 1.2 collective-permute-start.6
  36.4 9.2 %collective-permute-done.5 = bf16[3,24,3072]{2,1,0:T(8,128)(2,1)S(1)} collective-permute-done((bf16[3,24,3072]{2,1,0:T(8,128)(2,1)S(1)}, bf16[3,24,3072]{2,1,0:T(8,128)(2,1)S(1)}, u32[]{:S(2)}, u32[]{:S(2)}) %collective-permute-start.5) | collective-permute-done | bytes 442400 | tf_op jit(solution)/shard_map/ppermute | solution.py:768
  45.7 3.8 collective-permute-done.6
  49.5 6.7 %collective-permute-done.7 = bf16[3,24,3072]{2,1,0:T(8,128)(2,1)} collective-permute-done((bf16[3,24,3072]{2,1,0:T(8,128)(2,1)S(1)}, bf16[3,24,3072]{2,1,0:T(8,128)(2,1)}, u32[]{:S(2)}, u32[]{:S(2)}) %collective-permute-start.7) | collective-permute-done | bytes 442400 | tf_op jit(solution)/shard_map/ppermute | solution.py:768
  56.1 18.2 %all-to-all-done = bf16[4,256,768]{2,1,0:T(8,128)(2,1)S(1)} async-done(((bf16[4,256,768]{2,1,0:T(8,128)(2,1)}), bf16[4,256,768]{2,1,0:T(8,128)(2,1)S(1)}, u32[]{:S(2)}, u32[]{:S(2)}) %all-to-all-start) | async-done | bytes 1572896 | tf_op jit(solution)/shard_map/all_to_all | solution.py:780
  74.4 2.2 pad_maximum_fusion.half_ref
  76.7 1.6 collective-permute-start.11
  78.3 1.1 pad_maximum_fusion.1.own_ref
  79.5 2.2 collective-permute-start.8
  81.7 3.9 collective-permute-start.9
  89.6 3.3 maximum_select_fusion.1
  92.8 5.9 %assemble.1 = bf16[32,24,3072]{2,1,0:T(8,128)(2,1)} custom-call(s32[3]{0:T(128)} %pad_add_fusion.where, bf16[8,24,3072]{2,1,0:T(8,128)(2,1)} %pad_maximum_fusion.1.own_ref, bf16[4,3,24,3072]{3,2,1,0:T(8,128)(2,1)} %copy-done.5, bf16[4,3,24,3072]{3,2,1,0:T(8,128)(2,1)} %collective-permute-done.11.other_ref), custom_call_target="tpu_custom_call" | custom-call | tf_op jit(solution)/shard_map/assemble/pallas_call | solution.py:310
  98.7 10.5 %entry.1 = (bf16[1024,768]{1,0:T(8,128)(2,1)S(1)}, bf16[1024,768]{1,0:T(8,128)(2,1)S(1)}, bf16[1024,1536]{1,0:T(8,128)(2,1)}, f32[8,768]{1,0:T(8,128)S(1)}) custom-call(bf16[1024,768]{1,0:T(8,128)(2,1)S(1)} %bitcast.140, f32[8,768]{1,0:T(8,128)S(1)} %stack.238.vec_ref, bf16[768,3072]{1,0:T(8,128)(2,1)} %bitcast.144), custom_call_target="tpu_custom_call" | custom-call | flops 10350000128 | bytes 1048576 | tf_op jit(solution)/shard_map/entry/pallas_call | solution.py:359
  109.3 1.2 copy-done.3
  118.2 3.6 all-to-all-start.1
  122.9 44.2 %attn_forward.1 = (bf16[1024,768]{1,0:T(8,128)(2,1)}, f32[6,4,1,512]{3,2,1,0:T(1,128)}) custom-call(s32[16]{0:T(128)} %reshape.333.flags, f32[1]{0:T(128)} %bitcast.30.peak_ref, bf16[1024,768]{1,0:T(8,128)(2,1)} %copy-done.4, bf16[1024,1536]{1,0:T(8,128)(2,1)} %get-tuple-element.111.kn_ref.vn_ref, bf16[1024,1536]{1,0:T(8,128)(2,1)} %get-tuple-element.111.kn_ref.vn_ref, ...), custom_call_target="tpu_custom_call" | custom-call | flops 43699998720 | bytes 1048576 | tf_op jit(solution)/shard_map/attn_forward/pallas_call | solution.py:148
  168.3 55.7 %middle.1 = (bf16[1024,768]{1,0:T(8,128)(2,1)}, bf16[1024,768]{1,0:T(8,128)(2,1)}, f32[1024,768]{1,0:T(8,128)}, bf16[8,4,24,6912]{3,2,1,0:T(8,128)(2,1)}, f32[8,768]{1,0:T(8,128)}, /*index=5*/f32[1,3072]{1,0:T(1,128)}) custom-call(s32[3]{0:T(128)} %pad_add_fusion.where, bf16[1024,768]{1,0:T(8,128)(2,1)} %get-tuple-element.112.attn_ref.o_ref, ...), custom_call_target="tpu_custom_call" | custom-call | flops 63250001920 | bytes 1048576 | tf_op jit(solution)/shard_map/middle/pallas_call | solution.py:703
  224.0 4.7 %all-to-all-start.2 = ((bf16[4,256,768]{2,1,0:T(8,128)(2,1)}), bf16[4,256,768]{2,1,0:T(8,128)(2,1)S(1)}, u32[]{:S(2)}, u32[]{:S(2)}) async-start(bf16[4,256,768]{2,1,0:T(8,128)(2,1)} %bitcast.37), calls=%async_computation.3 | async-start | bytes 3145728 | tf_op jit(solution)/shard_map/all_to_all | solution.py:788
  228.7 72.5 %attn_backward.1 = (bf16[1024,768]{1,0:T(8,128)(2,1)}, bf16[2,1024,768]{2,1,0:T(8,128)(2,1)}, bf16[2,1024,768]{2,1,0:T(8,128)(2,1)}) custom-call(s32[16]{0:T(128)} %reshape.333.flags, f32[1]{0:T(128)} %bitcast.30.peak_ref, bf16[1024,768]{1,0:T(8,128)(2,1)} %copy-done.4, bf16[1024,1536]{1,0:T(8,128)(2,1)} %get-tuple-element.111.kn_ref.vn_ref, ...), custom_call_target="tpu_custom_call" | custom-call | flops 72449998848 | bytes 1048576 | tf_op jit(solution)/shard_map/attn_backward/pallas_call | solution.py:257
  302.0 5.3 %reduce-scatter.2.cloned.1.call-done = bf16[96,6912]{1,0:T(8,128)(2,1)} async-done(((bf16[768,6912]{1,0:T(8,128)(2,1)}), bf16[96,6912]{1,0:T(8,128)(2,1)}) %reduce-scatter.2.cloned.1.call-update) | async-done | bytes 1327120 | tf_op jit(solution)/shard_map/reduce_scatter | solution.py:825
  308.7 1.2 collective-permute-start.14
  309.9 2.1 collective-permute-start.15
  312.0 1.2 collective-permute-start.16
  313.2 18.9 %leave.1 = (bf16[1024,768]{1,0:T(8,128)(2,1)}, bf16[4,4,24,2304]{3,2,1,0:T(8,128)(2,1)}, bf16[4,4,24,2304]{3,2,1,0:T(8,128)(2,1)}, f32[8,768]{1,0:T(8,128)}) custom-call(s32[3]{0:T(128)} %pad_add_fusion.where, bf16[1024,768]{1,0:T(8,128)(2,1)} %get-tuple-element.122.dq_ref, bf16[2,1024,768]{2,1,0:T(8,128)(2,1)} %get-tuple-element.123.near_ref, ...), custom_call_target="tpu_custom_call" | custom-call | flops 16099999744 | bytes 1048576 | tf_op jit(solution)/shard_map/leave/pallas_call | solution.py:453
  332.2 2.4 collective-permute-done.15
  337.1 9.5 %all-to-all-start.3 = ((bf16[4,256,768]{2,1,0:T(8,128)(2,1)}), bf16[4,256,768]{2,1,0:T(8,128)(2,1)S(1)}, u32[]{:S(2)}, u32[]{:S(2)}) async-start(bf16[4,256,768]{2,1,0:T(8,128)(2,1)} %bitcast.157), calls=%async_computation.4 | async-start | bytes 3145728 | tf_op jit(solution)/shard_map/all_to_all | solution.py:788
  346.6 1.3 fusion.5
  347.9 3.3 add_convert_fusion.1
  352.6 1.2 collective-permute-start.23
  356.3 16.1 %collective-permute-done.24 = bf16[10240]{0:T(1024)(128)(2,1)S(1)} collective-permute-done((bf16[10240]{0:T(1024)(128)(2,1)S(1)}, bf16[10240]{0:T(1024)(128)(2,1)S(1)}, u32[]{:S(2)}, u32[]{:S(2)}) %collective-permute-start.24) | collective-permute-done | bytes 20512 | tf_op jit(solution)/shard_map/ppermute | solution.py:768
  372.4 1.2 collective-permute-start.26
  373.6 2.9 maximum_select_fusion.2
  376.5 6.6 %all-to-all-done.3 = bf16[4,256,768]{2,1,0:T(8,128)(2,1)S(1)} async-done(((bf16[4,256,768]{2,1,0:T(8,128)(2,1)}), bf16[4,256,768]{2,1,0:T(8,128)(2,1)S(1)}, u32[]{:S(2)}, u32[]{:S(2)}) %all-to-all-start.3) | async-done | bytes 1572896 | tf_op jit(solution)/shard_map/all_to_all | solution.py:788
  383.9 1.3 constant_dynamic-slice_fusion.8
  385.1 1.4 collective-permute-start.33
  386.7 1.5 add_convert_fusion
  389.0 1.5 collective-permute-start.28
  390.4 1.3 collective-permute-start.30
  391.9 5.2 %collective-permute-done.27 = bf16[40,2304]{1,0:T(8,128)(2,1)S(1)} collective-permute-done((bf16[40,2304]{1,0:T(8,128)(2,1)S(1)}, bf16[40,2304]{1,0:T(8,128)(2,1)S(1)}, u32[]{:S(2)}, u32[]{:S(2)}) %collective-permute-start.27) | collective-permute-done | bytes 184352 | tf_op jit(solution)/shard_map/ppermute | solution.py:765
  397.1 1.2 collective-permute-start.32
  398.2 5.8 %collective-permute-done.28 = bf16[40,2304]{1,0:T(8,128)(2,1)S(1)} collective-permute-done((bf16[40,2304]{1,0:T(8,128)(2,1)S(1)}, bf16[40,2304]{1,0:T(8,128)(2,1)S(1)}, u32[]{:S(2)}, u32[]{:S(2)}) %collective-permute-start.28) | collective-permute-done | bytes 184352 | tf_op jit(solution)/shard_map/ppermute | solution.py:765
  404.7 1.3 slice.253
  406.1 1.8 reshape.324
  408.0 2.4 collective-permute-done.29
  414.9 1.2 collective-permute-start.36
  417.4 2.6 collective-permute-start.38
  420.0 2.0 fusion.20
  426.1 1.4 reshape.322
  427.5 1.8 reshape.332
  429.3 1.3 dynamic_slice.164
  430.6 1.3 dynamic_slice.167
  433.2 1.5 dynamic-slice_reduce_fusion
  435.7 3.4 maximum_select_fusion.3
  440.0 1.9 settle.1
  441.9 4.9 %unpack.1 = (f32[8,24,768]{2,1,0:T(8,128)}, f32[8,24,3072]{2,1,0:T(8,128)}, f32[8,4,24,768]{3,2,1,0:T(8,128)}) custom-call(s32[3]{0:T(128)S(1)} %copy-done.2, bf16[4,24,6912]{2,1,0:T(8,128)(2,1)S(1)} %pad_maximum_fusion.2.half_ref, bf16[4,24,6912]{2,1,0:T(8,128)(2,1)S(1)} %collective-permute-done.38.other_ref), custom_call_target="tpu_custom_call" | custom-call | flops 4600000000 | bytes 1048576 | tf_op jit(solution)/shard_map/unpack/pallas_call | solution.py:541
  (268 shorter events, 47.7 us)
Async XLA Ops:
  7.2 7.9 %copy-start.11 = (bf16[2,1,512,768]{3,2,1,0:T(8,128)(2,1)S(1)}, bf16[2,1,512,768]{3,2,1,0:T(8,128)(2,1)}, u32[]{:S(2)}) copy-start(bf16[2,1,512,768]{3,2,1,0:T(8,128)(2,1)} %param.17) | copy-start | bytes 4718596
  7.2 160.0 %all-gather.2.cloned.1.call-start = ((), (), s32[]{:S(2)}) async-start(), calls=%async_computation.5 | async-start | bytes 10948608 | tf_op jit(solution)/shard_map/all_gather | solution.py:818
  8.5 6.6 %copy-start.8 = (bf16[8,24,768]{2,1,0:T(8,128)(2,1)}, bf16[8,24,768]{2,1,0:T(8,128)(2,1)S(1)}, u32[]{:S(2)}) copy-start(bf16[8,24,768]{2,1,0:T(8,128)(2,1)S(1)} %concatenate.44) | copy-start | bytes 884740
  9.6 12.8 %collective-permute-start.1 = (bf16[24,3072]{1,0:T(8,128)(2,1)S(1)}, bf16[24,3072]{1,0:T(8,128)(2,1)S(1)}, u32[]{:S(2)}, u32[]{:S(2)}) collective-permute-start(bf16[24,3072]{1,0:T(8,128)(2,1)S(1)} %fusion.11), channel_id=1, source_target_pairs={{0,1},{1,2},{2,3},{3,0},{4,5},{5,6},{6,7},{7,4},{8,9},{9,10},{10,1... | collective-permute-start | bytes 442376 | tf_op jit(solution)/shard_map/ppermute | solution.py:765
  11.7 12.8 %collective-permute-start.2 = (bf16[24,3072]{1,0:T(8,128)(2,1)S(1)}, bf16[24,3072]{1,0:T(8,128)(2,1)}, u32[]{:S(2)}, u32[]{:S(2)}) collective-permute-start(bf16[24,3072]{1,0:T(8,128)(2,1)S(1)} %fusion.11), channel_id=1, source_target_pairs={{0,2},{1,3},{2,0},{3,1},{4,6},{5,7},{6,4},{7,5},{8,10},{9,11},{10,... | collective-permute-start | bytes 442376 | tf_op jit(solution)/shard_map/ppermute | solution.py:765
  14.0 10.5 %collective-permute-start.3 = (bf16[24,3072]{1,0:T(8,128)(2,1)S(1)}, bf16[24,3072]{1,0:T(8,128)(2,1)}, u32[]{:S(2)}, u32[]{:S(2)}) collective-permute-start(bf16[24,3072]{1,0:T(8,128)(2,1)S(1)} %fusion.11), channel_id=1, source_target_pairs={{0,3},{1,0},{2,1},{3,2},{4,7},{5,4},{6,5},{7,6},{8,11},{9,8},{10,9... | collective-permute-start | bytes 442376 | tf_op jit(solution)/shard_map/ppermute | solution.py:765
  15.3 9.2 %collective-permute-start.4 = (bf16[2,256,768]{2,1,0:T(8,128)(2,1)S(1)}, bf16[2,256,768]{2,1,0:T(8,128)(2,1)S(1)}, u32[]{:S(2)}, u32[]{:S(2)}) collective-permute-start(bf16[2,256,768]{2,1,0:T(8,128)(2,1)S(1)} %get-tuple-element.233), channel_id=1, source_target_pairs={{0,4},{4,0},{8,12},{12,8},{16,20},{20,16},{24,28},{28,24},{1,5},{5... | collective-permute-start | bytes 2359304 | tf_op jit(solution)/shard_map/ppermute | solution.py:761
  17.0 5.3 %collective-permute-start = (f32[2,2189]{1,0:T(2,128)S(1)}, f32[2,2189]{1,0:T(2,128)S(1)}, u32[]{:S(2)}, u32[]{:S(2)}) collective-permute-start(f32[2,2189]{1,0:T(2,128)S(1)} %concatenate.42), channel_id=1, source_target_pairs={{0,4},{4,0},{8,12},{12,8},{16,20},{20,16},{24,28},{28,24},{1,5},{5... | collective-permute-start | bytes 52544 | tf_op jit(solution)/shard_map/ppermute | solution.py:761
  25.9 4.9 %copy-start.39 = (bf16[192]{0:T(256)(128)(2,1)S(1)}, bf16[192]{0:T(256)(128)(2,1)}, u32[]{:S(2)}) copy-start(bf16[192]{0:T(256)(128)(2,1)} %param.27) | copy-start | bytes 1156
  25.9 4.9 %copy-start.40 = (bf16[192]{0:T(256)(128)(2,1)S(1)}, bf16[192]{0:T(256)(128)(2,1)}, u32[]{:S(2)}) copy-start(bf16[192]{0:T(256)(128)(2,1)} %param.30) | copy-start | bytes 1156
  25.9 4.9 %copy-start.41 = (bf16[192]{0:T(256)(128)(2,1)S(1)}, bf16[192]{0:T(256)(128)(2,1)}, u32[]{:S(2)}) copy-start(bf16[192]{0:T(256)(128)(2,1)} %param.31) | copy-start | bytes 1156
  26.0 5.0 %copy-start.12 = (bf16[2,1,512,768]{3,2,1,0:T(8,128)(2,1)S(1)}, bf16[2,1,512,768]{3,2,1,0:T(8,128)(2,1)}, u32[]{:S(2)}) copy-start(bf16[2,1,512,768]{3,2,1,0:T(8,128)(2,1)} %param.21) | copy-start | bytes 4718596
  26.0 48.4 %all-to-all-start = ((bf16[4,256,768]{2,1,0:T(8,128)(2,1)}), bf16[4,256,768]{2,1,0:T(8,128)(2,1)S(1)}, u32[]{:S(2)}, u32[]{:S(2)}) async-start(bf16[4,256,768]{2,1,0:T(8,128)(2,1)} %bitcast.18), calls=%async_computation | async-start | bytes 3145728 | tf_op jit(solution)/shard_map/all_to_all | solution.py:780
  31.0 5.1 %copy-start.17 = (bf16[128,1152]{1,0:T(8,128)(2,1)S(1)}, bf16[128,1152]{1,0:T(8,128)(2,1)}, u32[]{:S(2)}) copy-start(bf16[128,1152]{1,0:T(8,128)(2,1)} %param.28) | copy-start | bytes 884740
  33.3 41.1 %copy-start.10 = (bf16[3,24,3072]{2,1,0:T(8,128)(2,1)}, bf16[3,24,3072]{2,1,0:T(8,128)(2,1)S(1)}, u32[]{:S(2)}) copy-start(bf16[3,24,3072]{2,1,0:T(8,128)(2,1)S(1)} %pad_maximum_fusion.3) | copy-start | bytes 1327108
  33.3 12.4 %collective-permute-start.5 = (bf16[3,24,3072]{2,1,0:T(8,128)(2,1)S(1)}, bf16[3,24,3072]{2,1,0:T(8,128)(2,1)S(1)}, u32[]{:S(2)}, u32[]{:S(2)}) collective-permute-start(bf16[3,24,3072]{2,1,0:T(8,128)(2,1)S(1)} %pad_maximum_fusion.3), channel_id=1, source_target_pairs={{0,8},{4,12},{8,0},{12,4},{16,24},{20,28},{24,16},{28,20},{1,9},{5... | collective-permute-start | bytes 1327112 | tf_op jit(solution)/shard_map/ppermute | solution.py:768
  34.6 14.9 %collective-permute-start.6 = (bf16[3,24,3072]{2,1,0:T(8,128)(2,1)S(1)}, bf16[3,24,3072]{2,1,0:T(8,128)(2,1)S(1)}, u32[]{:S(2)}, u32[]{:S(2)}) collective-permute-start(bf16[3,24,3072]{2,1,0:T(8,128)(2,1)S(1)} %pad_maximum_fusion.3), channel_id=1, source_target_pairs={{0,16},{4,20},{8,24},{12,28},{16,0},{20,4},{24,8},{28,12},{1,17},{... | collective-permute-start | bytes 1327112 | tf_op jit(solution)/shard_map/ppermute | solution.py:768
  35.8 20.3 %collective-permute-start.7 = (bf16[3,24,3072]{2,1,0:T(8,128)(2,1)S(1)}, bf16[3,24,3072]{2,1,0:T(8,128)(2,1)}, u32[]{:S(2)}, u32[]{:S(2)}) collective-permute-start(bf16[3,24,3072]{2,1,0:T(8,128)(2,1)S(1)} %pad_maximum_fusion.3), channel_id=1, source_target_pairs={{0,24},{4,28},{8,16},{12,20},{16,8},{20,12},{24,0},{28,4},{1,25},{... | collective-permute-start | bytes 1327112 | tf_op jit(solution)/shard_map/ppermute | solution.py:768
  36.1 76.4 %copy-start.31 = (f32[4,2189]{1,0:T(4,128)}, f32[4,2189]{1,0:T(4,128)S(1)}, u32[]{:S(2)}) copy-start(f32[4,2189]{1,0:T(4,128)S(1)} %select_n.209) | copy-start | bytes 105076
  45.7 28.7 %copy-start.21 = (bf16[3,24,3072]{2,1,0:T(8,128)(2,1)}, bf16[3,24,3072]{2,1,0:T(8,128)(2,1)S(1)}, u32[]{:S(2)}) copy-start(bf16[3,24,3072]{2,1,0:T(8,128)(2,1)S(1)} %collective-permute-done.5) | copy-start | bytes 1327108
  49.5 24.9 %copy-start.22 = (bf16[3,24,3072]{2,1,0:T(8,128)(2,1)}, bf16[3,24,3072]{2,1,0:T(8,128)(2,1)S(1)}, u32[]{:S(2)}) copy-start(bf16[3,24,3072]{2,1,0:T(8,128)(2,1)S(1)} %collective-permute-done.6) | copy-start | bytes 1327108
  74.4 24.3 %copy-start = (bf16[4,256,768]{2,1,0:T(8,128)(2,1)}, bf16[4,256,768]{2,1,0:T(8,128)(2,1)S(1)}, u32[]{:S(2)}) copy-start(bf16[4,256,768]{2,1,0:T(8,128)(2,1)S(1)} %all-to-all-done) | copy-start | bytes 4718596
  76.7 12.7 %copy-start.5 = (bf16[4,3,24,3072]{3,2,1,0:T(8,128)(2,1)}, bf16[4,3,24,3072]{3,2,1,0:T(8,128)(2,1)S(1)}, u32[]{:S(2)}) copy-start(bf16[4,3,24,3072]{3,2,1,0:T(8,128)(2,1)S(1)} %pad_maximum_fusion.half_ref) | copy-start | bytes 5308420
  76.7 16.2 %collective-permute-start.11 = (bf16[4,3,24,3072]{3,2,1,0:T(8,128)(2,1)S(1)}, bf16[4,3,24,3072]{3,2,1,0:T(8,128)(2,1)}, u32[]{:S(2)}, u32[]{:S(2)}) collective-permute-start(bf16[4,3,24,3072]{3,2,1,0:T(8,128)(2,1)S(1)} %pad_maximum_fusion.half_ref), channel_id=1, source_target_pairs={{0,4},{4,0},{8,12},{12,8},{16,20},{20,16},{24,28},{28,24},{1,5},{5... | collective-permute-start | bytes 5308424 | tf_op jit(solution)/shard_map/ppermute | solution.py:761
  79.5 7.5 %collective-permute-start.8 = (f32[2496]{0:T(1024)S(1)}, f32[2496]{0:T(1024)S(1)}, u32[]{:S(2)}, u32[]{:S(2)}) collective-permute-start(f32[2496]{0:T(1024)S(1)} %get-tuple-element.219), channel_id=1, source_target_pairs={{0,1},{1,2},{2,3},{3,0},{4,5},{5,6},{6,7},{7,4},{8,9},{9,10},{10,1... | collective-permute-start | bytes 29960 | tf_op jit(solution)/shard_map/ppermute | solution.py:765
  81.7 6.3 %collective-permute-start.9 = (f32[2496]{0:T(1024)S(1)}, f32[2496]{0:T(1024)S(1)}, u32[]{:S(2)}, u32[]{:S(2)}) collective-permute-start(f32[2496]{0:T(1024)S(1)} %get-tuple-element.221), channel_id=1, source_target_pairs={{0,2},{1,3},{2,0},{3,1},{4,6},{5,7},{6,4},{7,5},{8,10},{9,11},{10,... | collective-permute-start | bytes 29960 | tf_op jit(solution)/shard_map/ppermute | solution.py:765
  85.6 3.5 collective-permute-start.10
  86.2 3.3 collective-permute-start.12
  89.5 9.2 %copy-start.1 = (f32[8,768]{1,0:T(8,128)}, f32[8,768]{1,0:T(8,128)S(1)}, u32[]{:S(2)}) copy-start(f32[8,768]{1,0:T(8,128)S(1)} %stack.238.vec_ref) | copy-start | bytes 73732
  111.6 11.4 %collective-permute-start.13 = (bf16[1024,1536]{1,0:T(8,128)(2,1)}, bf16[1024,1536]{1,0:T(8,128)(2,1)}, u32[]{:S(2)}, u32[]{:S(2)}) collective-permute-start(bf16[1024,1536]{1,0:T(8,128)(2,1)} %get-tuple-element.111.kn_ref.vn_ref), channel_id=1, source_target_pairs={{0,4},{4,0},{8,12},{12,8},{16,20},{20,16},{24,28},{28,24},{1,5},{5... | collective-permute-start | bytes 9437192 | tf_op jit(solution)/shard_map/ppermute | solution.py:761
  118.2 49.0 %all-to-all-start.1 = ((bf16[4,256,768]{2,1,0:T(8,128)(2,1)}), bf16[4,256,768]{2,1,0:T(8,128)(2,1)S(1)}, u32[]{:S(2)}, u32[]{:S(2)}) async-start(bf16[4,256,768]{2,1,0:T(8,128)(2,1)} %bitcast.32), calls=%async_computation.1 | async-start | bytes 3145728 | tf_op jit(solution)/shard_map/all_to_all | solution.py:780
  121.7 185.5 %reduce-scatter.2.cloned.1.call-start = ((), (), s32[]{:S(2)}) async-start(), calls=%async_computation.6 | async-start | bytes 11943936 | tf_op jit(solution)/shard_map/reduce_scatter | solution.py:825
  224.0 78.0 %all-to-all-start.2 = ((bf16[4,256,768]{2,1,0:T(8,128)(2,1)}), bf16[4,256,768]{2,1,0:T(8,128)(2,1)S(1)}, u32[]{:S(2)}, u32[]{:S(2)}) async-start(bf16[4,256,768]{2,1,0:T(8,128)(2,1)} %bitcast.37), calls=%async_computation.3 | async-start | bytes 3145728 | tf_op jit(solution)/shard_map/all_to_all | solution.py:788
  301.2 12.0 %collective-permute-start.18 = (bf16[2,1024,768]{2,1,0:T(8,128)(2,1)}, bf16[2,1024,768]{2,1,0:T(8,128)(2,1)}, u32[]{:S(2)}, u32[]{:S(2)}) collective-permute-start(bf16[2,1024,768]{2,1,0:T(8,128)(2,1)} %get-tuple-element.124), channel_id=1, source_target_pairs={{0,4},{4,0},{8,12},{12,8},{16,20},{20,16},{24,28},{28,24},{1,5},{5... | collective-permute-start | bytes 9437192 | tf_op jit(solution)/shard_map/ppermute | solution.py:761
  307.4 27.1 %collective-permute-start.17 = (bf16[2,256,768]{2,1,0:T(8,128)(2,1)S(1)}, bf16[2,256,768]{2,1,0:T(8,128)(2,1)S(1)}, u32[]{:S(2)}, u32[]{:S(2)}) collective-permute-start(bf16[2,256,768]{2,1,0:T(8,128)(2,1)S(1)} %get-tuple-element.229), channel_id=1, source_target_pairs={{0,4},{4,0},{8,12},{12,8},{16,20},{20,16},{24,28},{28,24},{1,5},{5... | collective-permute-start | bytes 2359304 | tf_op jit(solution)/shard_map/ppermute | solution.py:761
  308.7 23.5 %collective-permute-start.14 = (bf16[24,6912]{1,0:T(8,128)(2,1)S(1)}, bf16[24,6912]{1,0:T(8,128)(2,1)S(1)}, u32[]{:S(2)}, u32[]{:S(2)}) collective-permute-start(bf16[24,6912]{1,0:T(8,128)(2,1)S(1)} %get-tuple-element.236), channel_id=1, source_target_pairs={{0,1},{1,2},{2,3},{3,0},{4,5},{5,6},{6,7},{7,4},{8,9},{9,10},{10,1... | collective-permute-start | bytes 995336 | tf_op jit(solution)/shard_map/ppermute | solution.py:765
  309.9 24.6 %collective-permute-start.15 = (bf16[24,6912]{1,0:T(8,128)(2,1)S(1)}, bf16[24,6912]{1,0:T(8,128)(2,1)S(1)}, u32[]{:S(2)}, u32[]{:S(2)}) collective-permute-start(bf16[24,6912]{1,0:T(8,128)(2,1)S(1)} %get-tuple-element.235), channel_id=1, source_target_pairs={{0,2},{1,3},{2,0},{3,1},{4,6},{5,7},{6,4},{7,5},{8,10},{9,11},{10,... | collective-permute-start | bytes 995336 | tf_op jit(solution)/shard_map/ppermute | solution.py:765
  312.0 22.5 %collective-permute-start.16 = (bf16[24,6912]{1,0:T(8,128)(2,1)S(1)}, bf16[24,6912]{1,0:T(8,128)(2,1)S(1)}, u32[]{:S(2)}, u32[]{:S(2)}) collective-permute-start(bf16[24,6912]{1,0:T(8,128)(2,1)S(1)} %get-tuple-element.234), channel_id=1, source_target_pairs={{0,3},{1,0},{2,1},{3,2},{4,7},{5,4},{6,5},{7,6},{8,11},{9,8},{10,9... | collective-permute-start | bytes 995336 | tf_op jit(solution)/shard_map/ppermute | solution.py:765
  313.2 22.8 %copy-start.32 = (f32[8,768]{1,0:T(8,128)S(1)}, f32[8,768]{1,0:T(8,128)}, u32[]{:S(2)}) copy-start(f32[8,768]{1,0:T(8,128)} %get-tuple-element.134) | copy-start | bytes 73732
  313.2 22.9 %copy-start.34 = (f32[1,3072]{1,0:T(1,128)S(1)}, f32[1,3072]{1,0:T(1,128)}, u32[]{:S(2)}) copy-start(f32[1,3072]{1,0:T(1,128)} %get-tuple-element.135) | copy-start | bytes 36868
  335.4 12.5 %collective-permute-start.19 = (bf16[4,4,24,2304]{3,2,1,0:T(8,128)(2,1)}, bf16[4,4,24,2304]{3,2,1,0:T(8,128)(2,1)}, u32[]{:S(2)}, u32[]{:S(2)}) collective-permute-start(bf16[4,4,24,2304]{3,2,1,0:T(8,128)(2,1)} %get-tuple-element.132), channel_id=1, source_target_pairs={{0,4},{4,0},{8,12},{12,8},{16,20},{20,16},{24,28},{28,24},{1,5},{5... | collective-permute-start | bytes 5308424 | tf_op jit(solution)/shard_map/ppermute | solution.py:761
  337.1 10.8 %collective-permute-start.20 = (bf16[13,768]{1,0:T(8,128)(2,1)S(1)}, bf16[13,768]{1,0:T(8,128)(2,1)S(1)}, u32[]{:S(2)}, u32[]{:S(2)}) collective-permute-start(bf16[13,768]{1,0:T(8,128)(2,1)S(1)} %concatenate.49), channel_id=1, source_target_pairs={{0,4},{4,0},{8,12},{12,8},{16,20},{20,16},{24,28},{28,24},{1,5},{5... | collective-permute-start | bytes 59912 | tf_op jit(solution)/shard_map/ppermute | solution.py:761
  337.1 46.0 %all-to-all-start.3 = ((bf16[4,256,768]{2,1,0:T(8,128)(2,1)}), bf16[4,256,768]{2,1,0:T(8,128)(2,1)S(1)}, u32[]{:S(2)}, u32[]{:S(2)}) async-start(bf16[4,256,768]{2,1,0:T(8,128)(2,1)} %bitcast.157), calls=%async_computation.4 | async-start | bytes 3145728 | tf_op jit(solution)/shard_map/all_to_all | solution.py:788
  351.2 25.3 %collective-permute-start.21 = (bf16[96,2304]{1,0:T(8,128)(2,1)}, bf16[96,2304]{1,0:T(8,128)(2,1)}, u32[]{:S(2)}, u32[]{:S(2)}) collective-permute-start(bf16[96,2304]{1,0:T(8,128)(2,1)} %bitcast.46), channel_id=1, source_target_pairs={{0,8},{4,12},{8,0},{12,4},{16,24},{20,28},{24,16},{28,20},{1,9},{5... | collective-permute-start | bytes 1327112 | tf_op jit(solution)/shard_map/ppermute | solution.py:768
  352.2 24.2 %collective-permute-start.22 = (bf16[96,2304]{1,0:T(8,128)(2,1)}, bf16[96,2304]{1,0:T(8,128)(2,1)}, u32[]{:S(2)}, u32[]{:S(2)}) collective-permute-start(bf16[96,2304]{1,0:T(8,128)(2,1)} %bitcast.47), channel_id=1, source_target_pairs={{0,16},{4,20},{8,24},{12,28},{16,0},{20,4},{24,8},{28,12},{1,17},{... | collective-permute-start | bytes 1327112 | tf_op jit(solution)/shard_map/ppermute | solution.py:768
  352.6 23.9 %collective-permute-start.23 = (bf16[96,2304]{1,0:T(8,128)(2,1)}, bf16[96,2304]{1,0:T(8,128)(2,1)}, u32[]{:S(2)}, u32[]{:S(2)}) collective-permute-start(bf16[96,2304]{1,0:T(8,128)(2,1)} %bitcast.48), channel_id=1, source_target_pairs={{0,24},{4,28},{8,16},{12,20},{16,8},{20,12},{24,0},{28,4},{1,25},{... | collective-permute-start | bytes 1327112 | tf_op jit(solution)/shard_map/ppermute | solution.py:768
  354.8 17.6 %collective-permute-start.24 = (bf16[10240]{0:T(1024)(128)(2,1)S(1)}, bf16[10240]{0:T(1024)(128)(2,1)S(1)}, u32[]{:S(2)}, u32[]{:S(2)}) collective-permute-start(bf16[10240]{0:T(1024)(128)(2,1)S(1)} %dynamic-update-slice.4), channel_id=1, source_target_pairs={{0,8},{4,12},{8,0},{12,4},{16,24},{20,28},{24,16},{28,20},{1,9},{5... | collective-permute-start | bytes 61448 | tf_op jit(solution)/shard_map/ppermute | solution.py:768
  355.9 20.5 %collective-permute-start.25 = (bf16[10240]{0:T(1024)(128)(2,1)S(1)}, bf16[10240]{0:T(1024)(128)(2,1)S(1)}, u32[]{:S(2)}, u32[]{:S(2)}) collective-permute-start(bf16[10240]{0:T(1024)(128)(2,1)S(1)} %dynamic-update-slice.4), channel_id=1, source_target_pairs={{0,16},{4,20},{8,24},{12,28},{16,0},{20,4},{24,8},{28,12},{1,17},{... | collective-permute-start | bytes 61448 | tf_op jit(solution)/shard_map/ppermute | solution.py:768
  372.4 4.1 collective-permute-start.26
  385.1 25.3 %collective-permute-start.33 = (bf16[2,256,768]{2,1,0:T(8,128)(2,1)}, bf16[2,256,768]{2,1,0:T(8,128)(2,1)}, u32[]{:S(2)}, u32[]{:S(2)}) collective-permute-start(bf16[2,256,768]{2,1,0:T(8,128)(2,1)} %get-tuple-element.227), channel_id=1, source_target_pairs={{0,4},{4,0},{8,12},{12,8},{16,20},{20,16},{24,28},{28,24},{1,5},{5... | collective-permute-start | bytes 2359304 | tf_op jit(solution)/shard_map/ppermute | solution.py:761
  389.0 8.1 %collective-permute-start.27 = (bf16[40,2304]{1,0:T(8,128)(2,1)S(1)}, bf16[40,2304]{1,0:T(8,128)(2,1)S(1)}, u32[]{:S(2)}, u32[]{:S(2)}) collective-permute-start(bf16[40,2304]{1,0:T(8,128)(2,1)S(1)} %get-tuple-element.239), channel_id=1, source_target_pairs={{0,1},{1,2},{2,3},{3,0},{4,5},{5,6},{6,7},{7,4},{8,9},{9,10},{10,1... | collective-permute-start | bytes 552968 | tf_op jit(solution)/shard_map/ppermute | solution.py:765
  389.0 15.1 %collective-permute-start.28 = (bf16[40,2304]{1,0:T(8,128)(2,1)S(1)}, bf16[40,2304]{1,0:T(8,128)(2,1)S(1)}, u32[]{:S(2)}, u32[]{:S(2)}) collective-permute-start(bf16[40,2304]{1,0:T(8,128)(2,1)S(1)} %get-tuple-element.238), channel_id=1, source_target_pairs={{0,2},{1,3},{2,0},{3,1},{4,6},{5,7},{6,4},{7,5},{8,10},{9,11},{10,... | collective-permute-start | bytes 552968 | tf_op jit(solution)/shard_map/ppermute | solution.py:765
  390.4 20.0 %collective-permute-start.30 = (bf16[24,6912]{1,0:T(8,128)(2,1)S(1)}, bf16[24,6912]{1,0:T(8,128)(2,1)S(1)}, u32[]{:S(2)}, u32[]{:S(2)}) collective-permute-start(bf16[24,6912]{1,0:T(8,128)(2,1)S(1)} %fusion.5), channel_id=1, source_target_pairs={{0,8},{4,12},{8,0},{12,4},{16,24},{20,28},{24,16},{28,20},{1,9},{5... | collective-permute-start | bytes 995336 | tf_op jit(solution)/shard_map/ppermute | solution.py:768
  391.7 18.7 %collective-permute-start.31 = (bf16[24,6912]{1,0:T(8,128)(2,1)S(1)}, bf16[24,6912]{1,0:T(8,128)(2,1)S(1)}, u32[]{:S(2)}, u32[]{:S(2)}) collective-permute-start(bf16[24,6912]{1,0:T(8,128)(2,1)S(1)} %fusion.5), channel_id=1, source_target_pairs={{0,16},{4,20},{8,24},{12,28},{16,0},{20,4},{24,8},{28,12},{1,17},{... | collective-permute-start | bytes 995336 | tf_op jit(solution)/shard_map/ppermute | solution.py:768
  397.1 13.4 %copy-start.25 = (bf16[40,2304]{1,0:T(8,128)(2,1)}, bf16[40,2304]{1,0:T(8,128)(2,1)S(1)}, u32[]{:S(2)}) copy-start(bf16[40,2304]{1,0:T(8,128)(2,1)S(1)} %collective-permute-done.27) | copy-start | bytes 552964
  397.1 13.3 %collective-permute-start.32 = (bf16[24,6912]{1,0:T(8,128)(2,1)S(1)}, bf16[24,6912]{1,0:T(8,128)(2,1)S(1)}, u32[]{:S(2)}, u32[]{:S(2)}) collective-permute-start(bf16[24,6912]{1,0:T(8,128)(2,1)S(1)} %fusion.5), channel_id=1, source_target_pairs={{0,24},{4,28},{8,16},{12,20},{16,8},{20,12},{24,0},{28,4},{1,25},{... | collective-permute-start | bytes 995336 | tf_op jit(solution)/shard_map/ppermute | solution.py:768
  404.7 5.7 %collective-permute-start.29 = (bf16[40,2304]{1,0:T(8,128)(2,1)}, bf16[40,2304]{1,0:T(8,128)(2,1)}, u32[]{:S(2)}, u32[]{:S(2)}) collective-permute-start(bf16[40,2304]{1,0:T(8,128)(2,1)} %get-tuple-element.237), channel_id=1, source_target_pairs={{0,3},{1,0},{2,1},{3,2},{4,7},{5,4},{6,5},{7,6},{8,11},{9,8},{10,9... | collective-permute-start | bytes 552968 | tf_op jit(solution)/shard_map/ppermute | solution.py:765
  413.4 8.7 %collective-permute-start.34 = (bf16[24,2304]{1,0:T(8,128)(2,1)S(1)}, bf16[24,2304]{1,0:T(8,128)(2,1)S(1)}, u32[]{:S(2)}, u32[]{:S(2)}) collective-permute-start(bf16[24,2304]{1,0:T(8,128)(2,1)S(1)} %add_convert_fusion.5), channel_id=1, source_target_pairs={{0,8},{4,12},{8,0},{12,4},{16,24},{20,28},{24,16},{28,20},{1,9},{5... | collective-permute-start | bytes 331784 | tf_op jit(solution)/shard_map/ppermute | solution.py:768
  414.5 7.6 %collective-permute-start.35 = (bf16[24,2304]{1,0:T(8,128)(2,1)S(1)}, bf16[24,2304]{1,0:T(8,128)(2,1)}, u32[]{:S(2)}, u32[]{:S(2)}) collective-permute-start(bf16[24,2304]{1,0:T(8,128)(2,1)S(1)} %add_convert_fusion.5), channel_id=1, source_target_pairs={{0,16},{4,20},{8,24},{12,28},{16,0},{20,4},{24,8},{28,12},{1,17},{... | collective-permute-start | bytes 331784 | tf_op jit(solution)/shard_map/ppermute | solution.py:768
  414.9 7.2 %collective-permute-start.36 = (bf16[24,2304]{1,0:T(8,128)(2,1)S(1)}, bf16[24,2304]{1,0:T(8,128)(2,1)}, u32[]{:S(2)}, u32[]{:S(2)}) collective-permute-start(bf16[24,2304]{1,0:T(8,128)(2,1)S(1)} %add_convert_fusion.5), channel_id=1, source_target_pairs={{0,24},{4,28},{8,16},{12,20},{16,8},{20,12},{24,0},{28,4},{1,25},{... | collective-permute-start | bytes 331784 | tf_op jit(solution)/shard_map/ppermute | solution.py:768
  417.2 7.3 %copy-start.16 = (f32[4,4,4864]{2,1,0:T(4,128)S(1)}, f32[4,4,4864]{2,1,0:T(4,128)}, u32[]{:S(2)}) copy-start(f32[4,4,4864]{2,1,0:T(4,128)} %copy-done.15) | copy-start | bytes 933892
  417.4 7.9 %copy-start.19 = (bf16[4,4,4608]{2,1,0:T(4,128)(2,1)S(1)}, bf16[4,4,4608]{2,1,0:T(4,128)(2,1)}, u32[]{:S(2)}) copy-start(bf16[4,4,4608]{2,1,0:T(4,128)(2,1)} %copy-done.18) | copy-start | bytes 442372
  417.4 24.5 %collective-permute-start.38 = (bf16[4,24,6912]{2,1,0:T(8,128)(2,1)S(1)}, bf16[4,24,6912]{2,1,0:T(8,128)(2,1)S(1)}, u32[]{:S(2)}, u32[]{:S(2)}) collective-permute-start(bf16[4,24,6912]{2,1,0:T(8,128)(2,1)S(1)} %pad_maximum_fusion.2.half_ref), channel_id=1, source_target_pairs={{0,4},{4,0},{8,12},{12,8},{16,20},{20,16},{24,28},{28,24},{1,5},{5... | collective-permute-start | bytes 3981320 | tf_op jit(solution)/shard_map/ppermute | solution.py:761
  423.1 16.9 %collective-permute-start.37 = (bf16[4,24,2304]{2,1,0:T(8,128)(2,1)S(1)}, bf16[4,24,2304]{2,1,0:T(8,128)(2,1)S(1)}, u32[]{:S(2)}, u32[]{:S(2)}) collective-permute-start(bf16[4,24,2304]{2,1,0:T(8,128)(2,1)S(1)} %pad_maximum_fusion.4.half_ref), channel_id=1, source_target_pairs={{0,4},{4,0},{8,12},{12,8},{16,20},{20,16},{24,28},{28,24},{1,5},{5... | collective-permute-start | bytes 1327112 | tf_op jit(solution)/shard_map/ppermute | solution.py:761
  (23 other events, 50.1 us)
Sparse Core Ops, SparseCore 0:
  24.6 121.1 all-gather.1
  224.1 83.0 reduce-scatter.1
